TPU v7x, 32 devices: a whole 2x2x4 slice. The times are simulated.
32 devices in a mesh: dom: 8 (over z, x), cls: 4 (over y, core).
Axes of the slice: x: 2, y: 2, z: 4, core: 2. Of those that a mesh axis runs over, the one named last changes fastest.
Arguments:
- spectra: bfloat16 [512, 128, 512], P(('dom', 'cls')), may hold values from -6 to 6
- ctf: bfloat16 [512, 128], P(('dom', 'cls')), may hold values from -1 to 1
- noise_power: float32 [128], replicated, may hold values from 0.5 to 8
- references: bfloat16 [48, 32, 512], P('cls'), may hold values from -3 to 3
- owner: int32 [512, 1], P(('dom', 'cls')), may hold values from 0 to 3; in each aligned block of 16 rows (0 to 15, 16 to 31, ...) at most 8 rows name the same one
- sub_class: int32 [512], P(('dom', 'cls')), may hold values from 0 to 11
- rotation: int32 [512], P(('dom', 'cls')), may hold values from 0 to 511
Outputs:
- new_refs: float32 [48, 128, 512], P('cls', 'dom')
- log_evidence: float32 [512], P(('dom', 'cls'))
Inputs may be any that keep to these rules, and one draw needn't show every extreme that they name: Among the 16 particles of one device, at most 8 have the same owner, a bound that some block reaches of them.
All inputs are finite; a program needn't handle non-finite values.
Results may differ from a plain program's by a relative error of at most 0.00067.
Values may be sent and summed in bfloat16 or wider, within the bound.
No kernel may reach another device: no remote copies, remote signals or barrier semaphores. Data moves between devices by JAX's collectives and lax.ppermute only.
A program may use at most 128 MiB of HBM per device.

v0:
```python
import functools
import math

import jax
import jax.numpy as jnp
from jax import lax
from jax.experimental import pallas as pl
from jax.experimental.pallas import tpu as pltpu
from jax.sharding import PartitionSpec as P


CHUNKS = 2
GROUP = 4
FAR_CALLS = 1
LANES = 128
PAD = 16
STEPS = 64.0
UNIT = math.log(2.0) / STEPS


def table_kernel(out_ref):
    width, turns_all = out_ref.shape
    half = width // 2
    step = 64
    for at in range(0, half, step):
        turns = (iota((step, turns_all), 0) + at) * iota((step, turns_all), 1) & (turns_all - 1)
        angle = turns.astype(jnp.float32) * (2.0 * math.pi / turns_all)
        out_ref[at : at + step, :] = jnp.cos(angle).astype(jnp.bfloat16)
        out_ref[half + at : half + at + step, :] = (-jnp.sin(angle)).astype(jnp.bfloat16)


def rotation_table(width):
    return pl.pallas_call(
        table_kernel,
        out_shape=pltpu.VMEM((width, width), jnp.bfloat16),
        out_specs=HERE,
        cost_estimate=cost(2),
        compiler_params=room(((width, width), 4)),
        name="table",
    )()


def held_near(*values):
    return [pltpu.with_memory_space_constraint(v, pltpu.VMEM) for v in values]


def held_far(*values):
    return [pltpu.with_memory_space_constraint(v, pltpu.HBM) for v in values]


def swap(value, axis, mask):
    size = lax.axis_size(axis)
    return lax.ppermute(value, axis, [(i, i ^ mask) for i in range(size)])


def iota(shape, axis):
    return lax.broadcasted_iota(jnp.int32, shape, axis)


HERE = pl.BlockSpec(memory_space=pltpu.VMEM)
SCALARS = pl.BlockSpec(memory_space=pltpu.SMEM)
THERE = pl.BlockSpec(memory_space=pltpu.HBM)


def room(*arrays):
    size = sum(math.prod(shape) * bits for shape, bits in arrays)
    return pltpu.CompilerParams(vmem_limit_bytes=size + (8 << 20))


def cost(us):
    return pl.CostEstimate(flops=0, transcendentals=0, bytes_accessed=int(us * 3.6e6))


def score_kernel(
    image_ref, ctf_ref, noise_ref, first_ref, second_ref, table_ref, *refs, merge, start
):
    before = refs[:2] if merge else None
    row_ref = refs[2] if merge else None
    outs = refs[3:4] if merge else refs[:2]
    low_ref, image, image_sum, staged, classes, cross, sem = refs[4 if merge else 2 :]
    count, cycles, width = low_ref.shape
    fetch = pltpu.make_async_copy(image_ref.at[pl.ds(start, count), :cycles, :], low_ref, sem)
    fetch.start()
    tiles = width // LANES
    pairs = tiles // 2
    kinds = cross.shape[0] // count
    part = first_ref.shape[0]
    ctf = ctf_ref[start : start + count, :].astype(jnp.float32)
    weight = ctf / noise_ref[...]
    power = ctf * weight
    eye = iota((cycles, LANES), 0) == iota((cycles, LANES), 1)
    fetch.wait()
    for n in range(count):
        row = jnp.broadcast_to(weight[n : n + 1, :], (cycles, LANES))
        column = jnp.sum(jnp.where(eye, row, 0.0), axis=1, keepdims=True)
        low = low_ref[n].astype(jnp.float32)
        weighted = (column * low).astype(jnp.bfloat16).astype(jnp.float32)
        for f in range(tiles):
            image[f, n * cycles : (n + 1) * cycles, :] = weighted[:, f * LANES : (f + 1) * LANES]
        for f in range(pairs):
            re = weighted[:, f * LANES : (f + 1) * LANES]
            im = weighted[:, (f + pairs) * LANES : (f + pairs + 1) * LANES]
            image_sum[f, n * cycles : (n + 1) * cycles, :] = re + im
    for at, ref in ((0, first_ref), (part, second_ref)):
        for f in range(tiles):
            staged[f, at : at + part, :] = ref[:, f * LANES : (f + 1) * LANES].astype(jnp.float32)
    blocks = kinds // 8
    zero = jnp.zeros((8, LANES), jnp.float32)
    norms = []
    for b in range(blocks):
        square = jnp.zeros((cycles, 8, LANES), jnp.float32)
        for f in range(pairs):
            rows = pl.ds(b * 8 * cycles, 8 * cycles)
            re = jnp.swapaxes(staged[f, rows, :].reshape(8, cycles, LANES), 0, 1)
            im = jnp.swapaxes(staged[f + pairs, rows, :].reshape(8, cycles, LANES), 0, 1)
            classes[3 * f, :, b * 8 : b * 8 + 8, :] = re
            classes[3 * f + 1, :, b * 8 : b * 8 + 8, :] = re - im
            classes[3 * f + 2, :, b * 8 : b * 8 + 8, :] = re + im
            square = square + (re * re + im * im)
        norm = zero
        for r in range(cycles):
            total = jnp.sum(square[r], axis=1, keepdims=True)
            norm = jnp.where(iota((8, LANES), 1) == r, total, norm)
        norms.append(norm)
    group = 2
    for f in range(pairs):

        def particles(g, _):
            def cycle(r, sums):
                new = list(sums)
                for i in range(group):
                    row = pl.ds((g * group + i) * cycles + r, 8, stride=0)
                    a_sum, a_im, a_re = image_sum[f, row, :], image[f + pairs, row, :], image[f, row, :]
                    for b in range(blocks):
                        at = slice(b * 8, b * 8 + 8)
                        j = 3 * (i * blocks + b)
                        new[j] = new[j] + classes[3 * f, r, at, :] * a_sum
                        new[j + 1] = new[j + 1] + classes[3 * f + 1, r, at, :] * a_im
                        new[j + 2] = new[j + 2] + classes[3 * f + 2, r, at, :] * a_re
                return tuple(new)

            sums = lax.fori_loop(0, cycles, cycle, (zero,) * (3 * group * blocks), unroll=4)
            for i in range(group):
                for b in range(blocks):
                    s1, s2, s3 = sums[3 * (i * blocks + b) : 3 * (i * blocks + b) + 3]
                    at = pl.ds(pl.multiple_of((g * group + i) * kinds + b * 8, 8), 8)
                    cross[at, f * LANES : (f + 1) * LANES] = s1 - s2
                    cross[at, (f + pairs) * LANES : (f + pairs + 1) * LANES] = s1 - s3
            return 0

        lax.fori_loop(0, count // group, particles, 0)
    scores = jnp.dot(
        cross[...].astype(jnp.bfloat16), table_ref[...], preferred_element_type=jnp.float32
    )
    cross[...] = scores
    inner = iota((8, LANES), 1) < cycles
    row = row_ref[...] if merge else None
    for n in range(count):
            mine = []
            for b in range(blocks):
                powers = jnp.where(inner, jnp.broadcast_to(power[n : n + 1, :], (8, LANES)), 0.0)
                energy = jnp.sum(powers * norms[b], axis=1, keepdims=True)
                at = n * kinds + b * 8
                mine.append(cross[at : at + 8, :] - 0.5 * energy)
            mine = jnp.concatenate(mine, axis=0)
            top = jnp.max(mine, axis=(0, 1), keepdims=True)
            if merge:
                top_before, total_before = before[0][start + n : start + n + 1, :], before[1][start + n : start + n + 1, :]
                top = jnp.maximum(top, jnp.max(top_before, axis=1, keepdims=True))
            total = jnp.sum(jnp.exp(mine - top), axis=(0, 1), keepdims=True)
            if merge:
                total = total + (total_before * jnp.exp(top_before - top))[:, :1]
                here = iota(row.shape, 1) == start + n
                row = jnp.where(here, jnp.broadcast_to(top + jnp.log(total), row.shape), row)
            else:
                outs[0][n : n + 1, :] = jnp.broadcast_to(top, (1, LANES))
                outs[1][n : n + 1, :] = jnp.broadcast_to(total, (1, LANES))
    if merge:
        outs[0][...] = row


def score(spectra, ctf, noise, first, second, table, before, start, count):
    width = spectra.shape[2]
    cycles = first.shape[1]
    kinds = 2 * first.shape[0]
    merge = before is not None
    each = pltpu.VMEM((count, LANES), jnp.float32)
    row = jax.ShapeDtypeStruct((1, ctf.shape[0]), jnp.float32)
    part = (kinds // 2 * cycles, width)
    outs = pl.pallas_call(
        functools.partial(score_kernel, merge=merge, start=start),
        out_shape=row if merge else (each, each),
        in_specs=[THERE] + [HERE] * (8 if merge else 5),
        out_specs=HERE if merge else (HERE, HERE),
        scratch_shapes=[
            pltpu.VMEM((count, cycles, width), spectra.dtype),
            pltpu.VMEM((width // LANES, count * cycles, LANES), jnp.float32),
            pltpu.VMEM((width // LANES // 2, count * cycles, LANES), jnp.float32),
            pltpu.VMEM((width // LANES, kinds * cycles, LANES), jnp.float32),
            pltpu.VMEM((width // LANES // 2 * 3, cycles, kinds, LANES), jnp.float32),
            pltpu.VMEM((count * kinds, width), jnp.float32),
            pltpu.SemaphoreType.DMA,
        ],
        cost_estimate=cost(8),
        compiler_params=room(
            ((count * cycles, width), 10),
            ((kinds * cycles, width), 12),
            ((count * kinds, width), 8),
            (table.shape, 2),
        ),
    )(
        *held_far(spectra), ctf, noise, *held_near(first.reshape(part), second.reshape(part), table),
        *(before or ()),
    )
    return outs


def part_of(view_ref, top, near):
    if view_ref.shape[0] == 2:
        return view_ref.at[top, near]
    return view_ref.at[:, top, near]


def column(row):
    size = row.shape[1]
    eye = iota((size, size), 0) == iota((size, size), 1)
    return jnp.sum(jnp.where(eye, jnp.broadcast_to(row, (size, size)), 0.0), axis=1, keepdims=True)


def pieces_kernel(near_ref, top_ref, view_ref, *refs, chunk):
    outs, sems = refs[-GROUP:-1], refs[-1]
    if chunk == 0:
        ctf_ref, owner_ref, sub_ref, turn_ref, meta_ref = refs[:5]
        outs = refs[5 : 5 + GROUP - 1]
        ctf_here, owner_here, sub_here, turn_here, small, sems = refs[5 + GROUP - 1 :]
        fetches = [
            pltpu.make_async_copy(there, here, small.at[i])
            for i, (there, here) in enumerate(
                ((ctf_ref, ctf_here), (owner_ref, owner_here), (sub_ref, sub_here), (turn_ref, turn_here))
            )
        ]
        for fetch in fetches:
            fetch.start()
    count = view_ref.shape[2] if view_ref.shape[0] == 2 else view_ref.shape[0]
    copies = [
        pltpu.make_async_copy(
            part_of(view_ref, top_ref[0] ^ (1 - chunk), near_ref[0] ^ (i + 1)),
            out.at[pl.ds(0, count)],
            sems.at[i],
        )
        for i, out in enumerate(outs)
    ]
    for copy in copies:
        copy.start()
    if chunk == 0:
        for fetch in fetches:
            fetch.wait()
        cycles = ctf_ref.shape[1]
        turn = turn_here[...]
        shape = (count, meta_ref.shape[1] - cycles)
        at = iota(shape, 1)
        rest = jnp.where(at == 0, column((turn >> 4).astype(jnp.float32)), 0.0)
        rest = jnp.where(at == 1, column((turn & 15).astype(jnp.float32)), rest)
        rest = jnp.where(at == 2, column(owner_here[...].astype(jnp.float32)), rest)
        rest = jnp.where(at == 3, column(sub_here[...].astype(jnp.float32)), rest)
        meta_ref[:, :cycles] = ctf_here[...]
        meta_ref[:, cycles:] = rest.astype(jnp.bfloat16)
        for out in outs:
            out[count, :, :] = jnp.zeros(out.shape[1:], out.dtype)
            out[count, :, : meta_ref.shape[1]] = meta_ref[...]
    for copy in copies:
        copy.wait()


def pieces(near, top, view, chunk, others):
    count, width = view.shape[2] if view.shape[0] == 2 else view.shape[0], view.shape[-1]
    out = pltpu.VMEM((count + (chunk == 0), PAD, width), view.dtype)
    shapes = [out] * (GROUP - 1)
    scratch = [pltpu.SemaphoreType.DMA((GROUP - 1,))]
    if chunk == 0:
        ctf = others[0]
        shapes = [pltpu.VMEM((count, 2 * ctf.shape[1]), view.dtype)] + shapes
        scratch = [
            pltpu.VMEM(ctf.shape, ctf.dtype),
            pltpu.VMEM((1, count), jnp.int32),
            pltpu.VMEM((1, count), jnp.int32),
            pltpu.VMEM((1, count), jnp.int32),
            pltpu.SemaphoreType.DMA((4,)),
        ] + scratch
    return pl.pallas_call(
        functools.partial(pieces_kernel, chunk=chunk),
        out_shape=shapes,
        in_specs=[SCALARS] * 2 + [THERE] * (1 + len(others)),
        out_specs=[HERE] * len(shapes),
        scratch_shapes=scratch,
        cost_estimate=cost(1.5),
        compiler_params=room(((count * PAD, width), 2 * GROUP)),
    )(near, top, *held_far(view, *others))


def sums_kernel(
    near_ref, top_ref, cls_ref, *refs, slice_cycles, far, chunk, shards,
):
    if chunk == 0:
        meta_ref, refs = refs[0], refs[1:]
    noise_ref, view_ref, refs = refs[0], refs[1], refs[2:]
    given, refs = refs[: GROUP - 1], refs[GROUP - 1 :]
    if chunk == 0:
        keep_ref, give_ref = refs[:2]
        shared, refs = refs[2:6], refs[6:]
        total, powers, own, plan, metas, cos_ref, sin_ref, place_ref, sems = refs
    else:
        shared, refs = refs[:4], refs[4:]
        keep_ref, give_ref, total, own, metas, cos_ref, sin_ref, place_ref, sems = refs
    cycles, half = PAD, cos_ref.shape[1]
    side = top_ref[0] ^ (1 - chunk)
    fetch = pltpu.make_async_copy(part_of(view_ref, side, near_ref[0]), own, sems.at[0])
    fetch.start()
    particles = cos_ref.shape[0]
    count = particles // GROUP
    width = 2 * half
    size = keep_ref.shape[0] // (shards // 2)
    if chunk == 0:
        metas[:count] = meta_ref[...]
        for g, piece in enumerate(given):
            metas[(g + 1) * count : (g + 2) * count] = piece[count, :, : metas.shape[1]]
        ints = metas[:, LANES : LANES + LANES].astype(jnp.float32).astype(jnp.int32)
        turn = ints[:, 0:1] * 16 + ints[:, 1:2]
        shard, inside = ints[:, 2:3], ints[:, 3:4]
        block = ((shard ^ cls_ref[0]) & 1) * (shards // 2) + (shard >> 1)
        lane_at = iota((particles, LANES), 1)
        places = jnp.where(lane_at == 0, block * size + inside * cycles, block * PAD + inside)
        plan[...] = jnp.where(lane_at == 2, block * (size - PAD) + inside * cycles, places)
        schedule = pltpu.make_async_copy(plan, place_ref, sems.at[1])
        schedule.start()
        total[...] = jnp.zeros_like(total)
        powers[...] = jnp.zeros_like(powers)
        turns = iota((particles, half), 1) * turn & (width - 1)
        angle = turns.astype(jnp.float32) * (2.0 * math.pi / width)
        cos_ref[...] = jnp.cos(angle)
        sin_ref[...] = jnp.sin(angle)
        saves = [
            pltpu.make_async_copy(here, there, sems.at[2 + i])
            for i, (here, there) in enumerate(zip((plan, metas, cos_ref, sin_ref), shared))
        ]
        for save in saves:
            save.start()
    else:
        loads = [
            pltpu.make_async_copy(there, here, sems.at[1 + i])
            for i, (here, there) in enumerate(zip((place_ref, metas, cos_ref, sin_ref), shared))
        ]
        for load in loads:
            load.start()
        total[...] = jnp.zeros_like(total)
    r = iota((cycles, LANES), 0)
    domain = (side * (far // 2) + r // slice_cycles) * GROUP + near_ref[0]
    pick = iota((cycles, LANES), 1) == domain * slice_cycles + r % slice_cycles
    batch = 2
    fetch.wait()
    if chunk == 0:
        schedule.wait()
    else:
        for load in loads:
            load.wait()
    place_at = 0 if chunk == 0 else 2

    def one(n, source):
        ctf = metas[n : n + 1, :LANES].astype(jnp.float32)
        weight_row = ctf / noise_ref[...]
        weight = jnp.sum(
            jnp.where(pick, jnp.broadcast_to(weight_row, pick.shape), 0.0), axis=1, keepdims=True
        )
        x = source[n % count].astype(jnp.float32)
        x_re, x_im = x[:, :half], x[:, half:]
        cosv, sinv = cos_ref[n : n + 1, :], sin_ref[n : n + 1, :]
        re = weight * (x_re * cosv - x_im * sinv)
        im = weight * (x_re * sinv + x_im * cosv)
        return re, im, ctf * weight_row

    for g in range(GROUP):
        source = own if g == 0 else given[g - 1]
        for start in range(g * count, (g + 1) * count, batch):
            done = [one(n, source) for n in range(start, start + batch)]
            for n, (re, im, power) in zip(range(start, start + batch), done):
                at = pl.ds(pl.multiple_of(place_ref[n, place_at], PAD), cycles)
                total[at, :half] += re
                total[at, half:] += im
                if chunk == 0:
                    powers[pl.ds(place_ref[n, 1], 1), :] += power
    if chunk == 0:
        blocks = powers.shape[0] // PAD
        for b in range(blocks):
            at = slice((b + 1) * size - PAD, (b + 1) * size)
            total[at, :LANES] = powers[b * PAD : (b + 1) * PAD]
    rows = keep_ref.shape[0]
    keep_ref[...] = total[:rows]
    give_ref[...] = total[rows:]
    if chunk == 0:
        for save in saves:
            save.wait()


def class_sums(scalars, view, chunk, given, meta, noise, shared, slice_cycles, far, rows, shards):
    width = view.shape[-1]
    first = chunk == 0
    count = view.shape[2] if view.shape[0] == 2 else view.shape[0]
    particles = count * GROUP
    out = pltpu.VMEM((rows, width), jnp.float32)
    kinds = [
        ((particles, LANES), jnp.int32),
        ((particles, 2 * LANES), view.dtype),
        ((particles, width // 2), jnp.float32),
        ((particles, width // 2), jnp.float32),
    ]
    held = [pltpu.VMEM(shape, dtype) for shape, dtype in kinds]
    shapes = [out, out] + ([pltpu.HBM(shape, dtype) for shape, dtype in kinds] if first else [])
    own = pltpu.VMEM((count, PAD, width), view.dtype)
    scratch = [pltpu.VMEM((2 * rows, width), jnp.float32)]
    if first:
        scratch += [pltpu.VMEM((shards * PAD, LANES), jnp.float32), own, *held]
    else:
        scratch += [own, *held[1:]]
    ins = [meta] if first else []
    return pl.pallas_call(
        functools.partial(
            sums_kernel, slice_cycles=slice_cycles, far=far, chunk=chunk, shards=shards
        ),
        out_shape=shapes,
        in_specs=[SCALARS] * 3 + [HERE] * len(ins) + [HERE, THERE] + [HERE] * (GROUP - 1)
        + [THERE] * len(shared),
        out_specs=[HERE, HERE] + [THERE] * (len(shapes) - 2),
        scratch_shapes=scratch
        + [pltpu.SMEM((particles, LANES), jnp.int32), pltpu.SemaphoreType.DMA((6,))],
        cost_estimate=cost(2.5),
        compiler_params=room(((2 * rows, width), 8), ((particles * PAD, width), 4)),
    )(
        *scalars, *held_near(*ins), noise, *held_far(view), *held_near(*given), *held_far(*shared)
    )


def spans(rows):
    return [(at, min(LANES, rows - at)) for at in range(0, rows, LANES)]


def encode(value, out, at):
    rows = value.shape[0]
    codes = jnp.zeros((PAD, LANES), jnp.float32)
    for i, (start, size) in enumerate(spans(rows)):
        x = value[start : start + size]
        top = jnp.maximum(jnp.max(jnp.abs(x), axis=1, keepdims=True), 1e-30)
        code = jnp.floor(jnp.log(top) / UNIT) + 1.0
        scaled = x * (jnp.exp(-code * UNIT) * 32767.0)
        scaled = jnp.clip(jnp.round(scaled), -32767.0, 32767.0)
        out[at + start : at + start + size, :] = scaled.astype(jnp.int32).astype(jnp.int16)
        eye = iota((size, LANES), 0) == iota((size, LANES), 1)
        row = jnp.sum(jnp.where(eye, code, 0.0), axis=0, keepdims=True)
        codes = jnp.where(iota((PAD, LANES), 0) == i, row, codes)
    for f in range(out.shape[1] // LANES):
        out[at + rows : at + rows + PAD, f * LANES : (f + 1) * LANES] = codes.astype(
            jnp.int32
        ).astype(jnp.int16)


def decode(ref, at, rows):
    codes = ref[at + rows : at + rows + PAD, :LANES].astype(jnp.int32).astype(jnp.float32)
    parts = []
    for i, (start, size) in enumerate(spans(rows)):
        eye = iota((size, LANES), 0) == iota((size, LANES), 1)
        row = jnp.broadcast_to(codes[i : i + 1], (size, LANES))
        code = jnp.sum(jnp.where(eye, row, 0.0), axis=1, keepdims=True)
        x = ref[at + start : at + start + size, :].astype(jnp.int32).astype(jnp.float32)
        parts.append(x * (jnp.exp(code * UNIT) * (1.0 / 32767.0)))
    return jnp.concatenate(parts, axis=0)


def shard_kernel(bit_ref, keep_ref, get_ref, own_ref, code_ref, *, coded):
    parts, rows, _ = own_ref.shape
    if coded:
        for p in range(2 * parts):
            keep_ref[p] = keep_ref[p] + decode(get_ref.at[p], 0, rows)
    bit = bit_ref[0]
    for p in range(parts):
        mine, other = bit * parts + p, (1 - bit) * parts + p
        if coded:
            encode(keep_ref[other], code_ref.at[p], 0)
            own_ref[p] = keep_ref[mine]
        else:
            encode(keep_ref[other] + get_ref[other], code_ref.at[p], 0)
            own_ref[p] = keep_ref[mine] + get_ref[mine]


def split_shards(bit, keep, get):
    parts, rows, width = keep.shape
    parts = parts // 2
    own = pltpu.VMEM((parts, rows, width), jnp.float32)
    code = pltpu.VMEM((parts, rows + PAD, width), jnp.int16)
    return pl.pallas_call(
        functools.partial(shard_kernel, coded=get.dtype == jnp.int16),
        out_shape=(own, code),
        in_specs=[SCALARS, HERE, HERE],
        out_specs=(HERE, HERE),
        cost_estimate=cost(1.5),
        compiler_params=room((keep.shape, 16)),
    )(bit, *held_near(keep, get))


def ahead_kernel(keep_ref, get_ref, power_ref, code_ref):
    rows = keep_ref.shape[0]
    total = keep_ref[...] + decode(get_ref, 0, rows)
    power_ref[...] = total[rows - PAD :, :LANES]
    encode(total, code_ref, 0)


def ahead(keep, get):
    rows, width = keep.shape
    return pl.pallas_call(
        ahead_kernel,
        out_shape=(
            pltpu.VMEM((PAD, LANES), jnp.float32),
            pltpu.VMEM((rows + PAD, width), jnp.int16),
        ),
        in_specs=[HERE, HERE],
        out_specs=(HERE, HERE),
        cost_estimate=cost(1),
        compiler_params=room((keep.shape, 16)),
        name="ahead",
    )(*held_near(keep, get))


def final_kernel(dom_ref, keep_ref, get_ref, power_ref, came_ref, out):
    classes, cycles, _ = out.shape
    rows = classes * cycles
    came = decode(came_ref, 0, rows + PAD)
    sums = keep_ref[...] + decode(get_ref, 0, rows) + came[:rows]
    powers = power_ref[...] + came[rows:, :LANES]
    r = iota((cycles, LANES), 0)
    pick = iota((cycles, LANES), 1) == dom_ref[0] * cycles + r
    for k in range(classes):
        row = jnp.broadcast_to(powers[k : k + 1], pick.shape)
        denom = jnp.sum(jnp.where(pick, row, 0.0), axis=1, keepdims=True) + 1.0
        out[k] = sums[k * cycles : (k + 1) * cycles, :] / denom


def finish(dom, keep, get, power, came, classes, cycles, width):
    out = (classes, cycles, width)
    return pl.pallas_call(
        final_kernel,
        out_shape=jax.ShapeDtypeStruct(out, jnp.float32),
        in_specs=[SCALARS] + [HERE] * 4,
        out_specs=HERE,
        cost_estimate=cost(1),
        compiler_params=room((out, 16)),
        name="finish",
    )(dom, *held_near(keep, get, power, came))


def decoded(keep, get):
    rows = keep.shape[0]
    code = get[rows:, :LANES].astype(jnp.float32).reshape(-1)[:rows]
    scale = jnp.exp(code * UNIT) * (1.0 / 32767.0)
    return keep + get[:rows].astype(jnp.float32) * scale[:, None]


def per_device(spectra, ctf, noise_power, references, owner, sub_class, rotation):
    count, cycles, width = spectra.shape
    k_local = references.shape[0]
    turns_all = width
    domains, shards = lax.axis_size("dom"), lax.axis_size("cls")
    dom, cls = lax.axis_index("dom"), lax.axis_index("cls")
    far = domains // GROUP
    slice_cycles = cycles // domains
    near = (dom & (GROUP - 1)).reshape(1)
    top = (dom // (domains // 2)).reshape(1)
    noise = noise_power.reshape(1, cycles)

    if slice_cycles == PAD:
        view = spectra.reshape(count, 2, GROUP, PAD, width)
    else:
        view = spectra.reshape(count, 2, far // 2, GROUP, slice_cycles, width)
        view = view.transpose(1, 3, 0, 2, 4, 5).reshape(2, GROUP, count, PAD, width)
    rows_of = [v.reshape(1, count) for v in (owner, sub_class, rotation)]
    meta, *sent_0 = pieces(near, top, view, 0, (ctf, *rows_of))
    sent = (sent_0, pieces(near, top, view, 1, ()))
    got = [[swap(sent[c][m - 1], "dom", m) for m in range(1, GROUP)] for c in range(CHUNKS)]

    held, mask = references, 2
    own_side, other_side = references, None
    while mask < shards:
        new = swap(held, "cls", mask)
        other_side = new if other_side is None else jnp.concatenate([other_side, new], axis=0)
        held = jnp.concatenate([held, new], axis=0) if 2 * mask < shards else held
        mask *= 2
    table = rotation_table(turns_all)
    near_refs = swap(own_side, "cls", 1)
    before = score(spectra, ctf, noise, own_side, near_refs, table, None, 0, count)
    far_refs = swap(other_side, "cls", 1)
    size = count // FAR_CALLS
    row = jnp.zeros((1, count), jnp.float32)
    for i in range(FAR_CALLS):
        row = score(
            spectra, ctf, noise, other_side, far_refs, table, (*before, row), i * size, size,
        )
    log_evidence = row.reshape(count)

    scalars = (near, top, cls.reshape(1))
    ends, shared = [], []
    for chunk in range(CHUNKS):
        size = k_local * PAD + (PAD if chunk == 0 else 0)
        keep, give, *more = class_sums(
            scalars, view, chunk, got[chunk], meta, noise, shared, slice_cycles, far,
            shards // 2 * size, shards,
        )
        shared = more
        get = swap(give, "cls", 1)
        shape = (shards // 2, size, width)
        keep, get = keep.reshape(shape), get.reshape(shape)
        mask = shards // 2
        while mask >= 2:
            bit = ((cls // mask) & 1).reshape(1)
            keep, code = split_shards(bit, keep, get)
            get = swap(code, "cls", mask)
            mask //= 2
        ends.append((keep[0], get[0]))
    power, code = ahead(*ends[0])
    came = swap(code, "dom", domains // 2)
    if far == 2:
        new_refs = finish(dom.reshape(1), *ends[1], power, came, k_local, slice_cycles, width)
        return (new_refs, log_evidence)

    came = decoded(jnp.zeros((came.shape[0] - PAD, width), jnp.float32), came)
    numer = decoded(*ends[1]) + came[: k_local * PAD]
    numer = numer.reshape(k_local, PAD, width)
    power = power + came[k_local * PAD :, :LANES]
    left, mask = PAD, domains // 4
    while mask >= GROUP:
        bit = (dom // mask) & 1
        left = left // 2
        own = lax.dynamic_slice_in_dim(numer, bit * left, left, 1)
        other = lax.dynamic_slice_in_dim(numer, (1 - bit) * left, left, 1)
        numer = own + swap(other, "dom", mask)
        power = power + swap(power, "dom", mask)
        mask //= 2
    denom = lax.dynamic_slice_in_dim(power[:k_local], dom * left, left, 1)
    return (numer / (denom + 1.0)[:, :, None], log_evidence)


def solution(mesh):
    return jax.shard_map(
        per_device,
        mesh=mesh,
        in_specs=(
            P(("dom", "cls"), None, None),
            P(("dom", "cls"), None),
            P(),
            P("cls", None, None),
            P(("dom", "cls"), None),
            P(("dom", "cls")),
            P(("dom", "cls")),
        ),
        out_specs=(P("cls", "dom", None), P(("dom", "cls"))),
        check_vma=False,
    )
```

profile of v0, /device:TPU:0, one launch (start us, length us, event | category | flops | bytes accessed | tf_op | source)
XLA Modules:
  0.0 85.1 jit_solution(15398334162171143030)
XLA Ops:
  0.7 1.2 %shard_map.87 = (bf16[16,256]{1,0:T(8,128)(2,1)S(1)}, bf16[17,16,512]{2,1,0:T(8,128)(2,1)S(1)}, bf16[17,16,512]{2,1,0:T(8,128)(2,1)S(1)}, bf16[17,16,512]{2,1,0:T(8,128)(2,1)S(1)}) custom-call(s32[1]{0:T(128)} %bitcast.2.near_ref, s32[1]{0:T(128)} %bitcast.3.top_ref, bf16[16,2,4,16,512]{4,3,2,1,0:T(8,128)(2,1)} %bitcast.37, bf16[16,128]{1,0:T(8,128)(2,1)} %ctf_ref.3, ...), custom_call_target="tpu_custom_call" | custom-call | bytes 5400000 | tf_op jit(solution)/shard_map/pallas_call | solution.py:290
  1.9 3.0 %collective-permute-start.3 = (bf16[17,16,512]{2,1,0:T(8,128)(2,1)S(1)}, bf16[17,16,512]{2,1,0:T(8,128)(2,1)S(1)}, u32[]{:S(2)}, u32[]{:S(2)}) collective-permute-start(bf16[17,16,512]{2,1,0:T(8,128)(2,1)S(1)} %get-tuple-element.29), channel_id=1, source_target_pairs={{0,4},{4,0},{8,12},{12,8},{16,20},{20,16},{24,28},{28,24},{1,5},{5... | collective-permute-start | bytes 835592 | tf_op jit(solution)/shard_map/ppermute | solution.py:53
  4.9 1.6 %collective-permute-start.4 = (bf16[17,16,512]{2,1,0:T(8,128)(2,1)S(1)}, bf16[17,16,512]{2,1,0:T(8,128)(2,1)S(1)}, u32[]{:S(2)}, u32[]{:S(2)}) collective-permute-start(bf16[17,16,512]{2,1,0:T(8,128)(2,1)S(1)} %get-tuple-element.30), channel_id=1, source_target_pairs={{0,8},{4,12},{8,0},{12,4},{16,24},{20,28},{24,16},{28,20},{1,9},{5... | collective-permute-start | bytes 835592 | tf_op jit(solution)/shard_map/ppermute | solution.py:53
  6.5 5.1 %collective-permute-done.3.refs_3_ = bf16[17,16,512]{2,1,0:T(8,128)(2,1)S(1)} collective-permute-done((bf16[17,16,512]{2,1,0:T(8,128)(2,1)S(1)}, bf16[17,16,512]{2,1,0:T(8,128)(2,1)S(1)}, u32[]{:S(2)}, u32[]{:S(2)}) %collective-permute-start.3) | collective-permute-done | bytes 278560 | tf_op jit(solution)/shard_map/ppermute | solution.py:53
  11.6 2.9 %collective-permute-done.4.refs_4_ = bf16[17,16,512]{2,1,0:T(8,128)(2,1)S(1)} collective-permute-done((bf16[17,16,512]{2,1,0:T(8,128)(2,1)S(1)}, bf16[17,16,512]{2,1,0:T(8,128)(2,1)S(1)}, u32[]{:S(2)}, u32[]{:S(2)}) %collective-permute-start.4) | collective-permute-done | bytes 278560 | tf_op jit(solution)/shard_map/ppermute | solution.py:53
  14.5 4.4 %collective-permute-done.5.refs_5_ = bf16[17,16,512]{2,1,0:T(8,128)(2,1)S(1)} collective-permute-done((bf16[17,16,512]{2,1,0:T(8,128)(2,1)S(1)}, bf16[17,16,512]{2,1,0:T(8,128)(2,1)S(1)}, u32[]{:S(2)}, u32[]{:S(2)}) %collective-permute-start.5) | collective-permute-done | bytes 278560 | tf_op jit(solution)/shard_map/ppermute | solution.py:53
  18.8 3.2 %shard_map.88 = (f32[416,512]{1,0:T(8,128)S(1)}, f32[416,512]{1,0:T(8,128)}, s32[64,128]{1,0:T(8,128)}, bf16[64,256]{1,0:T(8,128)(2,1)}, f32[64,256]{1,0:T(8,128)}, /*index=5*/f32[64,256]{1,0:T(8,128)}) custom-call(s32[1]{0:T(128)} %bitcast.2.near_ref, s32[1]{0:T(128)} %bitcast.3.top_ref, s32[1]{0:T(128)} %bitcast.4.cls_ref, ...), custom_call_target="tpu_custom_call" | custom-call | bytes 9000000 | tf_op jit(solution)/shard_map/pallas_call | solution.py:425
  22.1 1.1 %shard_map.86 = (bf16[16,16,512]{2,1,0:T(8,128)(2,1)S(1)}, bf16[16,16,512]{2,1,0:T(8,128)(2,1)S(1)}, bf16[16,16,512]{2,1,0:T(8,128)(2,1)S(1)}) custom-call(s32[1]{0:T(128)} %bitcast.2.near_ref, s32[1]{0:T(128)} %bitcast.3.top_ref, bf16[16,2,4,16,512]{4,3,2,1,0:T(8,128)(2,1)} %bitcast.39), custom_call_target="tpu_custom_call" | custom-call | bytes 5400000 | tf_op jit(solution)/shard_map/pallas_call | solution.py:290
  23.2 1.7 %collective-permute-start = (bf16[16,16,512]{2,1,0:T(8,128)(2,1)S(1)}, bf16[16,16,512]{2,1,0:T(8,128)(2,1)S(1)}, u32[]{:S(2)}, u32[]{:S(2)}) collective-permute-start(bf16[16,16,512]{2,1,0:T(8,128)(2,1)S(1)} %get-tuple-element.25), channel_id=1, source_target_pairs={{0,4},{4,0},{8,12},{12,8},{16,20},{20,16},{24,28},{28,24},{1,5},{5... | collective-permute-start | bytes 786440 | tf_op jit(solution)/shard_map/ppermute | solution.py:53
  25.0 1.6 %collective-permute-start.1 = (bf16[16,16,512]{2,1,0:T(8,128)(2,1)S(1)}, bf16[16,16,512]{2,1,0:T(8,128)(2,1)S(1)}, u32[]{:S(2)}, u32[]{:S(2)}) collective-permute-start(bf16[16,16,512]{2,1,0:T(8,128)(2,1)S(1)} %get-tuple-element.26), channel_id=1, source_target_pairs={{0,8},{4,12},{8,0},{12,4},{16,24},{20,28},{24,16},{28,20},{1,9},{5... | collective-permute-start | bytes 786440 | tf_op jit(solution)/shard_map/ppermute | solution.py:53
  26.8 5.2 %collective-permute-done.refs_2_ = bf16[16,16,512]{2,1,0:T(8,128)(2,1)S(1)} collective-permute-done((bf16[16,16,512]{2,1,0:T(8,128)(2,1)S(1)}, bf16[16,16,512]{2,1,0:T(8,128)(2,1)S(1)}, u32[]{:S(2)}, u32[]{:S(2)}) %collective-permute-start) | collective-permute-done | bytes 262176 | tf_op jit(solution)/shard_map/ppermute | solution.py:53
  32.0 2.1 %collective-permute-done.1.refs_3_ = bf16[16,16,512]{2,1,0:T(8,128)(2,1)S(1)} collective-permute-done((bf16[16,16,512]{2,1,0:T(8,128)(2,1)S(1)}, bf16[16,16,512]{2,1,0:T(8,128)(2,1)S(1)}, u32[]{:S(2)}, u32[]{:S(2)}) %collective-permute-start.1) | collective-permute-done | bytes 262176 | tf_op jit(solution)/shard_map/ppermute | solution.py:53
  34.2 4.7 %collective-permute-done.2.refs_4_ = bf16[16,16,512]{2,1,0:T(8,128)(2,1)S(1)} collective-permute-done((bf16[16,16,512]{2,1,0:T(8,128)(2,1)S(1)}, bf16[16,16,512]{2,1,0:T(8,128)(2,1)S(1)}, u32[]{:S(2)}, u32[]{:S(2)}) %collective-permute-start.2) | collective-permute-done | bytes 262176 | tf_op jit(solution)/shard_map/ppermute | solution.py:53
  38.8 2.9 %shard_map.89 = (f32[384,512]{1,0:T(8,128)S(1)}, f32[384,512]{1,0:T(8,128)}) custom-call(s32[1]{0:T(128)} %bitcast.2.near_ref, s32[1]{0:T(128)} %bitcast.3.top_ref, s32[1]{0:T(128)} %bitcast.4.cls_ref, f32[1,128]{1,0:T(1,128)S(1)} %bitcast.34, bf16[16,2,4,16,512]{4,3,2,1,0:T(8,128)(2,1)} %bitcast.40, bf16[16,16,512]{2,1,0:T(8,128)(2,1)S(1)} %collective-permute-done.refs_2_, ...), custom_call_target="tpu_custom_call" | custom-call | bytes 9000000 | tf_op jit(solution)/shard_map/pallas_call | solution.py:425
  41.8 1.8 %collective-permute-start.11 = (bf16[12,32,512]{2,1,0:T(8,128)(2,1)}, bf16[12,32,512]{2,1,0:T(8,128)(2,1)}, u32[]{:S(2)}, u32[]{:S(2)}) collective-permute-start(bf16[12,32,512]{2,1,0:T(8,128)(2,1)} %param.10), channel_id=1, source_target_pairs={{0,2},{1,3},{2,0},{3,1},{4,6},{5,7},{6,4},{7,5},{8,10},{9,11},{10,... | collective-permute-start | bytes 1179656 | tf_op jit(solution)/shard_map/ppermute | solution.py:53
  43.8 0.4 collective-permute-start.9
  44.2 10.0 %collective-permute-done.11 = bf16[12,32,512]{2,1,0:T(8,128)(2,1)} collective-permute-done((bf16[12,32,512]{2,1,0:T(8,128)(2,1)}, bf16[12,32,512]{2,1,0:T(8,128)(2,1)}, u32[]{:S(2)}, u32[]{:S(2)}) %collective-permute-start.11) | collective-permute-done | bytes 393248 | tf_op jit(solution)/shard_map/ppermute | solution.py:53
  54.2 4.3 %collective-permute-done.9 = s16[1,224,512]{2,1,0:T(8,128)(2,1)S(1)} collective-permute-done((s16[1,224,512]{2,1,0:T(8,128)(2,1)S(1)}, s16[1,224,512]{2,1,0:T(8,128)(2,1)S(1)}, u32[]{:S(2)}, u32[]{:S(2)}) %collective-permute-start.9) | collective-permute-done | bytes 229408 | tf_op jit(solution)/shard_map/ppermute | solution.py:53
  58.8 2.8 %collective-permute-start.10 = (s16[224,512]{1,0:T(8,128)(2,1)S(1)}, s16[224,512]{1,0:T(8,128)(2,1)S(1)}, u32[]{:S(2)}, u32[]{:S(2)}) collective-permute-start(s16[224,512]{1,0:T(8,128)(2,1)S(1)} %get-tuple-element.45), channel_id=1, source_target_pairs={{0,16},{4,20},{8,24},{12,28},{16,0},{20,4},{24,8},{28,12},{1,17},{... | collective-permute-start | bytes 688136 | tf_op jit(solution)/shard_map/ppermute | solution.py:53
  61.8 1.6 %collective-permute-start.7 = (s16[1,208,512]{2,1,0:T(8,128)(2,1)S(1)}, s16[1,208,512]{2,1,0:T(8,128)(2,1)S(1)}, u32[]{:S(2)}, u32[]{:S(2)}) collective-permute-start(s16[1,208,512]{2,1,0:T(8,128)(2,1)S(1)} %get-tuple-element.39), channel_id=1, source_target_pairs={{0,2},{1,3},{2,0},{3,1},{4,6},{5,7},{6,4},{7,5},{8,10},{9,11},{10,... | collective-permute-start | bytes 638984 | tf_op jit(solution)/shard_map/ppermute | solution.py:53
  63.4 2.0 %table.1.table_ref = bf16[512,512]{1,0:T(8,128)(2,1)S(1)} custom-call(), custom_call_target="tpu_custom_call" | custom-call | bytes 7200000 | tf_op jit(solution)/shard_map/table/pallas_call | solution.py:33
  65.5 9.0 %shard_map.92 = (f32[16,128]{1,0:T(8,128)S(1)}, f32[16,128]{1,0:T(8,128)S(1)}) custom-call(bf16[16,128,512]{2,1,0:T(8,128)(2,1)} %image_ref.3, bf16[16,128]{1,0:T(8,128)(2,1)S(1)} %copy-done, f32[1,128]{1,0:T(1,128)S(1)} %bitcast.35, bf16[384,512]{1,0:T(8,128)(2,1)} %bitcast.20.first_ref, bf16[384,512]{1,0:T(8,128)(2,1)S(1)} %bitcast.30, ...), custom_call_target="tpu_custom_call" | custom-call | bytes 28800000 | tf_op jit(solution)/shard_map/pallas_call | solution.py:190
  74.5 9.6 %shard_map.93 = f32[1,16]{1,0:T(1,128)} custom-call(bf16[16,128,512]{2,1,0:T(8,128)(2,1)} %image_ref.3, bf16[16,128]{1,0:T(8,128)(2,1)S(1)} %copy-done, f32[1,128]{1,0:T(1,128)S(1)} %bitcast.36, bf16[384,512]{1,0:T(8,128)(2,1)} %bitcast.18.first_ref, bf16[384,512]{1,0:T(8,128)(2,1)S(1)} %bitcast.29, bf16[512,512]{1,0:T(8,128)(2,1)S(1)} %table.1.table_ref, ...), custom_call_target="tpu_custom_call" | custom-call | bytes 28800000 | tf_op jit(solution)/shard_map/pallas_call | solution.py:190
  84.1 1.0 %finish.1 = f32[12,16,512]{2,1,0:T(8,128)} custom-call(s32[1]{0:T(128)} %bitcast.dom_ref, f32[192,512]{1,0:T(8,128)S(1)} %bitcast.28, s16[208,512]{1,0:T(8,128)(2,1)S(1)} %bitcast.32, f32[16,128]{1,0:T(8,128)S(1)} %get-tuple-element.44.power_ref, s16[224,512]{1,0:T(8,128)(2,1)S(1)} %collective-permute-done.10.came_ref), custom_call_target="tpu_custom_call" | custom-call | bytes 3600000 | tf_op jit(solution)/shard_map/finish/pallas_call | solution.py:547
  (20 shorter events, 1.2 us)
Async XLA Ops:
  0.6 18.2 %copy-start.1 = (f32[128]{0:T(128)S(1)}, f32[128]{0:T(128)}, u32[]{:S(2)}) copy-start(f32[128]{0:T(128)} %param.9) | copy-start | bytes 1540
  1.9 9.7 %collective-permute-start.3 = (bf16[17,16,512]{2,1,0:T(8,128)(2,1)S(1)}, bf16[17,16,512]{2,1,0:T(8,128)(2,1)S(1)}, u32[]{:S(2)}, u32[]{:S(2)}) collective-permute-start(bf16[17,16,512]{2,1,0:T(8,128)(2,1)S(1)} %get-tuple-element.29), channel_id=1, source_target_pairs={{0,4},{4,0},{8,12},{12,8},{16,20},{20,16},{24,28},{28,24},{1,5},{5... | collective-permute-start | bytes 835592 | tf_op jit(solution)/shard_map/ppermute | solution.py:53
  4.9 9.5 %collective-permute-start.4 = (bf16[17,16,512]{2,1,0:T(8,128)(2,1)S(1)}, bf16[17,16,512]{2,1,0:T(8,128)(2,1)S(1)}, u32[]{:S(2)}, u32[]{:S(2)}) collective-permute-start(bf16[17,16,512]{2,1,0:T(8,128)(2,1)S(1)} %get-tuple-element.30), channel_id=1, source_target_pairs={{0,8},{4,12},{8,0},{12,4},{16,24},{20,28},{24,16},{28,20},{1,9},{5... | collective-permute-start | bytes 835592 | tf_op jit(solution)/shard_map/ppermute | solution.py:53
  6.5 12.3 %collective-permute-start.5 = (bf16[17,16,512]{2,1,0:T(8,128)(2,1)S(1)}, bf16[17,16,512]{2,1,0:T(8,128)(2,1)S(1)}, u32[]{:S(2)}, u32[]{:S(2)}) collective-permute-start(bf16[17,16,512]{2,1,0:T(8,128)(2,1)S(1)} %get-tuple-element.31), channel_id=1, source_target_pairs={{0,12},{4,8},{8,4},{12,0},{16,28},{20,24},{24,20},{28,16},{1,13},{... | collective-permute-start | bytes 835592 | tf_op jit(solution)/shard_map/ppermute | solution.py:53
  22.0 21.6 %collective-permute-start.8 = (f32[416,512]{1,0:T(8,128)}, f32[416,512]{1,0:T(8,128)S(1)}, u32[]{:S(2)}, u32[]{:S(2)}) collective-permute-start(f32[416,512]{1,0:T(8,128)} %get-tuple-element.41), channel_id=1, source_target_pairs={{0,1},{1,0},{2,3},{3,2},{4,5},{5,4},{6,7},{7,6},{8,9},{9,8},{10,11... | collective-permute-start | bytes 2555912 | tf_op jit(solution)/shard_map/ppermute | solution.py:53
  23.2 8.8 %collective-permute-start = (bf16[16,16,512]{2,1,0:T(8,128)(2,1)S(1)}, bf16[16,16,512]{2,1,0:T(8,128)(2,1)S(1)}, u32[]{:S(2)}, u32[]{:S(2)}) collective-permute-start(bf16[16,16,512]{2,1,0:T(8,128)(2,1)S(1)} %get-tuple-element.25), channel_id=1, source_target_pairs={{0,4},{4,0},{8,12},{12,8},{16,20},{20,16},{24,28},{28,24},{1,5},{5... | collective-permute-start | bytes 786440 | tf_op jit(solution)/shard_map/ppermute | solution.py:53
  25.0 9.2 %collective-permute-start.1 = (bf16[16,16,512]{2,1,0:T(8,128)(2,1)S(1)}, bf16[16,16,512]{2,1,0:T(8,128)(2,1)S(1)}, u32[]{:S(2)}, u32[]{:S(2)}) collective-permute-start(bf16[16,16,512]{2,1,0:T(8,128)(2,1)S(1)} %get-tuple-element.26), channel_id=1, source_target_pairs={{0,8},{4,12},{8,0},{12,4},{16,24},{20,28},{24,16},{28,20},{1,9},{5... | collective-permute-start | bytes 786440 | tf_op jit(solution)/shard_map/ppermute | solution.py:53
  26.6 12.3 %collective-permute-start.2 = (bf16[16,16,512]{2,1,0:T(8,128)(2,1)S(1)}, bf16[16,16,512]{2,1,0:T(8,128)(2,1)S(1)}, u32[]{:S(2)}, u32[]{:S(2)}) collective-permute-start(bf16[16,16,512]{2,1,0:T(8,128)(2,1)S(1)} %get-tuple-element.27), channel_id=1, source_target_pairs={{0,12},{4,8},{8,4},{12,0},{16,28},{20,24},{24,20},{28,16},{1,13},{... | collective-permute-start | bytes 786440 | tf_op jit(solution)/shard_map/ppermute | solution.py:53
  41.8 19.8 %collective-permute-start.6 = (f32[384,512]{1,0:T(8,128)}, f32[384,512]{1,0:T(8,128)S(1)}, u32[]{:S(2)}, u32[]{:S(2)}) collective-permute-start(f32[384,512]{1,0:T(8,128)} %get-tuple-element.37), channel_id=1, source_target_pairs={{0,1},{1,0},{2,3},{3,2},{4,5},{5,4},{6,7},{7,6},{8,9},{9,8},{10,11... | collective-permute-start | bytes 2359304 | tf_op jit(solution)/shard_map/ppermute | solution.py:53
  41.8 12.4 %collective-permute-start.11 = (bf16[12,32,512]{2,1,0:T(8,128)(2,1)}, bf16[12,32,512]{2,1,0:T(8,128)(2,1)}, u32[]{:S(2)}, u32[]{:S(2)}) collective-permute-start(bf16[12,32,512]{2,1,0:T(8,128)(2,1)} %param.10), channel_id=1, source_target_pairs={{0,2},{1,3},{2,0},{3,1},{4,6},{5,7},{6,4},{7,5},{8,10},{9,11},{10,... | collective-permute-start | bytes 1179656 | tf_op jit(solution)/shard_map/ppermute | solution.py:53
  43.6 21.9 %copy-start = (bf16[16,128]{1,0:T(8,128)(2,1)S(1)}, bf16[16,128]{1,0:T(8,128)(2,1)}, u32[]{:S(2)}) copy-start(bf16[16,128]{1,0:T(8,128)(2,1)} %ctf_ref.3) | copy-start | bytes 12292
  43.8 14.6 %collective-permute-start.9 = (s16[1,224,512]{2,1,0:T(8,128)(2,1)S(1)}, s16[1,224,512]{2,1,0:T(8,128)(2,1)S(1)}, u32[]{:S(2)}, u32[]{:S(2)}) collective-permute-start(s16[1,224,512]{2,1,0:T(8,128)(2,1)S(1)} %get-tuple-element.43), channel_id=1, source_target_pairs={{0,2},{1,3},{2,0},{3,1},{4,6},{5,7},{6,4},{7,5},{8,10},{9,11},{10,... | collective-permute-start | bytes 688136 | tf_op jit(solution)/shard_map/ppermute | solution.py:53
  44.2 21.2 %collective-permute-start.13 = (bf16[12,32,512]{2,1,0:T(8,128)(2,1)}, bf16[12,32,512]{2,1,0:T(8,128)(2,1)S(1)}, u32[]{:S(2)}, u32[]{:S(2)}) collective-permute-start(bf16[12,32,512]{2,1,0:T(8,128)(2,1)} %param.10), channel_id=1, source_target_pairs={{0,1},{1,0},{2,3},{3,2},{4,5},{5,4},{6,7},{7,6},{8,9},{9,8},{10,11... | collective-permute-start | bytes 1179656 | tf_op jit(solution)/shard_map/ppermute | solution.py:53
  54.2 20.3 %collective-permute-start.12 = (bf16[12,32,512]{2,1,0:T(8,128)(2,1)}, bf16[12,32,512]{2,1,0:T(8,128)(2,1)S(1)}, u32[]{:S(2)}, u32[]{:S(2)}) collective-permute-start(bf16[12,32,512]{2,1,0:T(8,128)(2,1)} %collective-permute-done.11), channel_id=1, source_target_pairs={{0,1},{1,0},{2,3},{3,2},{4,5},{5,4},{6,7},{7,6},{8,9},{9,8},{10,11... | collective-permute-start | bytes 1179656 | tf_op jit(solution)/shard_map/ppermute | solution.py:53
  58.8 25.3 %collective-permute-start.10 = (s16[224,512]{1,0:T(8,128)(2,1)S(1)}, s16[224,512]{1,0:T(8,128)(2,1)S(1)}, u32[]{:S(2)}, u32[]{:S(2)}) collective-permute-start(s16[224,512]{1,0:T(8,128)(2,1)S(1)} %get-tuple-element.45), channel_id=1, source_target_pairs={{0,16},{4,20},{8,24},{12,28},{16,0},{20,4},{24,8},{28,12},{1,17},{... | collective-permute-start | bytes 688136 | tf_op jit(solution)/shard_map/ppermute | solution.py:53
  61.8 22.3 %collective-permute-start.7 = (s16[1,208,512]{2,1,0:T(8,128)(2,1)S(1)}, s16[1,208,512]{2,1,0:T(8,128)(2,1)S(1)}, u32[]{:S(2)}, u32[]{:S(2)}) collective-permute-start(s16[1,208,512]{2,1,0:T(8,128)(2,1)S(1)} %get-tuple-element.39), channel_id=1, source_target_pairs={{0,2},{1,3},{2,0},{3,1},{4,6},{5,7},{6,4},{7,5},{8,10},{9,11},{10,... | collective-permute-start | bytes 638984 | tf_op jit(solution)/shard_map/ppermute | solution.py:53
where the time goes:
time: 85.5 us; the launch traced here: 85.1 us
  waiting for transfers between devices  38.6 us (45%)
  Pallas kernels  30.8 us (36%)
  starting transfers between devices  14.9 us (17%)
    ppermute x14, waiting for transfers between devices, swap(): return lax.ppermute(value, axis, [(i, i ^ mask) for i in range(size)])  38.6 us
    pallas_call x2, Pallas kernels, score(): pl.pallas_call(functools.partial(score_kernel, merge=merge, start=start),...  18.6 us
    ppermute x14, starting transfers between devices, swap(): return lax.ppermute(value, axis, [(i, i ^ mask) for i in range(size)])  14.9 us
    pallas_call x2, Pallas kernels, class_sums(): pl.pallas_call(functools.partial(sums_kernel, slice_cycles=slice_cycles,...  6.12 us
    pallas_call x2, Pallas kernels, pieces(): pl.pallas_call(functools.partial(pieces_kernel, chunk=chunk), out_shape=s...  2.38 us
    pallas_call x1, Pallas kernels, rotation_table(): pl.pallas_call(table_kernel, out_shape=pltpu.VMEM((width, width), jnp.bfl...  2.04 us
  transfers between devices with their start and end apart: 14, of which 8 were waited for; matrix products, arithmetic and copies ran while one was open for 0% of the time, Pallas kernels for 30%

commit v1 on v0

--- a/solution.py
+++ b/solution.py
@@ -12,6 +12,7 @@
 CHUNKS = 2
 GROUP = 4
 FAR_CALLS = 1
+SPLITS = 4
 LANES = 128
 PAD = 16
 STEPS = 64.0
@@ -21,12 +22,21 @@
 def table_kernel(out_ref):
     width, turns_all = out_ref.shape
     half = width // 2
-    step = 64
-    for at in range(0, half, step):
-        turns = (iota((step, turns_all), 0) + at) * iota((step, turns_all), 1) & (turns_all - 1)
+    quarter = half // 2
+    step = 32
+    for at in range(0, quarter, step):
+        shape = (step, turns_all)
+        turns = (iota(shape, 0) + at) * iota(shape, 1) & (turns_all - 1)
         angle = turns.astype(jnp.float32) * (2.0 * math.pi / turns_all)
-        out_ref[at : at + step, :] = jnp.cos(angle).astype(jnp.bfloat16)
-        out_ref[half + at : half + at + step, :] = (-jnp.sin(angle)).astype(jnp.bfloat16)
+        cosv, sinv = jnp.cos(angle), jnp.sin(angle)
+        odd, back = (iota(shape, 1) & 1) == 1, (iota(shape, 1) & 2) == 2
+        cos_on, sin_on = jnp.where(odd, -sinv, cosv), jnp.where(odd, cosv, sinv)
+        cos_on, sin_on = jnp.where(back, -cos_on, cos_on), jnp.where(back, -sin_on, sin_on)
+        out_ref[at : at + step, :] = cosv.astype(jnp.bfloat16)
+        out_ref[quarter + at : quarter + at + step, :] = cos_on.astype(jnp.bfloat16)
+        out_ref[half + at : half + at + step, :] = (-sinv).astype(jnp.bfloat16)
+        at = half + quarter + at
+        out_ref[at : at + step, :] = (-sin_on).astype(jnp.bfloat16)
 
 
 def rotation_table(width):
@@ -89,18 +99,6 @@
     weight = ctf / noise_ref[...]
     power = ctf * weight
     eye = iota((cycles, LANES), 0) == iota((cycles, LANES), 1)
-    fetch.wait()
-    for n in range(count):
-        row = jnp.broadcast_to(weight[n : n + 1, :], (cycles, LANES))
-        column = jnp.sum(jnp.where(eye, row, 0.0), axis=1, keepdims=True)
-        low = low_ref[n].astype(jnp.float32)
-        weighted = (column * low).astype(jnp.bfloat16).astype(jnp.float32)
-        for f in range(tiles):
-            image[f, n * cycles : (n + 1) * cycles, :] = weighted[:, f * LANES : (f + 1) * LANES]
-        for f in range(pairs):
-            re = weighted[:, f * LANES : (f + 1) * LANES]
-            im = weighted[:, (f + pairs) * LANES : (f + pairs + 1) * LANES]
-            image_sum[f, n * cycles : (n + 1) * cycles, :] = re + im
     for at, ref in ((0, first_ref), (part, second_ref)):
         for f in range(tiles):
             staged[f, at : at + part, :] = ref[:, f * LANES : (f + 1) * LANES].astype(jnp.float32)
@@ -122,6 +120,18 @@
             total = jnp.sum(square[r], axis=1, keepdims=True)
             norm = jnp.where(iota((8, LANES), 1) == r, total, norm)
         norms.append(norm)
+    fetch.wait()
+    for n in range(count):
+        row = jnp.broadcast_to(weight[n : n + 1, :], (cycles, LANES))
+        column = jnp.sum(jnp.where(eye, row, 0.0), axis=1, keepdims=True)
+        low = low_ref[n].astype(jnp.float32)
+        weighted = (column * low).astype(jnp.bfloat16).astype(jnp.float32)
+        for f in range(tiles):
+            image[f, n * cycles : (n + 1) * cycles, :] = weighted[:, f * LANES : (f + 1) * LANES]
+        for f in range(pairs):
+            re = weighted[:, f * LANES : (f + 1) * LANES]
+            im = weighted[:, (f + pairs) * LANES : (f + pairs + 1) * LANES]
+            image_sum[f, n * cycles : (n + 1) * cycles, :] = re + im
     group = 2
     for f in range(pairs):
 
@@ -242,13 +252,17 @@
         for fetch in fetches:
             fetch.start()
     count = view_ref.shape[2] if view_ref.shape[0] == 2 else view_ref.shape[0]
+    part = count // SPLITS
     copies = [
         pltpu.make_async_copy(
-            part_of(view_ref, top_ref[0] ^ (1 - chunk), near_ref[0] ^ (i + 1)),
-            out.at[pl.ds(0, count)],
-            sems.at[i],
+            part_of(view_ref, top_ref[0] ^ (1 - chunk), near_ref[0] ^ (i + 1)).at[
+                pl.ds(j * part, part)
+            ],
+            out.at[pl.ds(j * part, part)],
+            sems.at[i * SPLITS + j],
         )
         for i, out in enumerate(outs)
+        for j in range(SPLITS)
     ]
     for copy in copies:
         copy.start()
@@ -276,7 +290,7 @@
     count, width = view.shape[2] if view.shape[0] == 2 else view.shape[0], view.shape[-1]
     out = pltpu.VMEM((count + (chunk == 0), PAD, width), view.dtype)
     shapes = [out] * (GROUP - 1)
-    scratch = [pltpu.SemaphoreType.DMA((GROUP - 1,))]
+    scratch = [pltpu.SemaphoreType.DMA(((GROUP - 1) * SPLITS,))]
     if chunk == 0:
         ctf = others[0]
         shapes = [pltpu.VMEM((count, 2 * ctf.shape[1]), view.dtype)] + shapes
@@ -308,18 +322,19 @@
     if chunk == 0:
         keep_ref, give_ref = refs[:2]
         shared, refs = refs[2:6], refs[6:]
-        total, powers, own, plan, metas, cos_ref, sin_ref, place_ref, sems = refs
+        total, own, powers, plan, metas, cos_ref, sin_ref, place_ref, sems = refs
     else:
-        shared, refs = refs[:4], refs[4:]
-        keep_ref, give_ref, total, own, metas, cos_ref, sin_ref, place_ref, sems = refs
+        plan, metas, cos_ref, sin_ref = refs[:4]
+        keep_ref, give_ref, total, own, place_ref, sems = refs[4:]
     cycles, half = PAD, cos_ref.shape[1]
     side = top_ref[0] ^ (1 - chunk)
-    fetch = pltpu.make_async_copy(part_of(view_ref, side, near_ref[0]), own, sems.at[0])
-    fetch.start()
     particles = cos_ref.shape[0]
     count = particles // GROUP
     width = 2 * half
     size = keep_ref.shape[0] // (shards // 2)
+    fetch = pltpu.make_async_copy(part_of(view_ref, side, near_ref[0]), own, sems.at[5])
+    fetch.start()
+    schedule = pltpu.make_async_copy(plan, place_ref, sems.at[0])
     if chunk == 0:
         metas[:count] = meta_ref[...]
         for g, piece in enumerate(given):
@@ -328,10 +343,19 @@
         turn = ints[:, 0:1] * 16 + ints[:, 1:2]
         shard, inside = ints[:, 2:3], ints[:, 3:4]
         block = ((shard ^ cls_ref[0]) & 1) * (shards // 2) + (shard >> 1)
-        lane_at = iota((particles, LANES), 1)
-        places = jnp.where(lane_at == 0, block * size + inside * cycles, block * PAD + inside)
-        plan[...] = jnp.where(lane_at == 2, block * (size - PAD) + inside * cycles, places)
-        schedule = pltpu.make_async_copy(plan, place_ref, sems.at[1])
+        here = iota((particles, LANES), 0) == iota((particles, LANES), 1)
+
+        def in_row(values):
+            return jnp.sum(jnp.where(here, values.astype(jnp.float32), 0.0), axis=0, keepdims=True)
+
+        rows = (
+            in_row(block * size + inside * cycles),
+            in_row(block * PAD + inside),
+            in_row(block * (size - PAD) + inside * cycles),
+        )
+        at = iota(plan.shape, 0)
+        places = jnp.where(at == 0, rows[0], jnp.where(at == 1, rows[1], rows[2]))
+        plan[...] = places.astype(jnp.int32)
         schedule.start()
         total[...] = jnp.zeros_like(total)
         powers[...] = jnp.zeros_like(powers)
@@ -340,29 +364,19 @@
         cos_ref[...] = jnp.cos(angle)
         sin_ref[...] = jnp.sin(angle)
         saves = [
-            pltpu.make_async_copy(here, there, sems.at[2 + i])
+            pltpu.make_async_copy(here, there, sems.at[1 + i])
             for i, (here, there) in enumerate(zip((plan, metas, cos_ref, sin_ref), shared))
         ]
         for save in saves:
             save.start()
     else:
-        loads = [
-            pltpu.make_async_copy(there, here, sems.at[1 + i])
-            for i, (here, there) in enumerate(zip((place_ref, metas, cos_ref, sin_ref), shared))
-        ]
-        for load in loads:
-            load.start()
+        schedule.start()
         total[...] = jnp.zeros_like(total)
     r = iota((cycles, LANES), 0)
     domain = (side * (far // 2) + r // slice_cycles) * GROUP + near_ref[0]
     pick = iota((cycles, LANES), 1) == domain * slice_cycles + r % slice_cycles
     batch = 2
-    fetch.wait()
-    if chunk == 0:
-        schedule.wait()
-    else:
-        for load in loads:
-            load.wait()
+    schedule.wait()
     place_at = 0 if chunk == 0 else 2
 
     def one(n, source):
@@ -378,16 +392,18 @@
         im = weight * (x_re * sinv + x_im * cosv)
         return re, im, ctf * weight_row
 
-    for g in range(GROUP):
-        source = own if g == 0 else given[g - 1]
+    for g in (*range(1, GROUP), 0):
+        source = given[g - 1] if g else own
+        if g == 0:
+            fetch.wait()
         for start in range(g * count, (g + 1) * count, batch):
             done = [one(n, source) for n in range(start, start + batch)]
             for n, (re, im, power) in zip(range(start, start + batch), done):
-                at = pl.ds(pl.multiple_of(place_ref[n, place_at], PAD), cycles)
+                at = pl.ds(pl.multiple_of(place_ref[place_at, n], PAD), cycles)
                 total[at, :half] += re
                 total[at, half:] += im
                 if chunk == 0:
-                    powers[pl.ds(place_ref[n, 1], 1), :] += power
+                    powers[pl.ds(place_ref[1, n], 1), :] += power
     if chunk == 0:
         blocks = powers.shape[0] // PAD
         for b in range(blocks):
@@ -403,40 +419,38 @@
 
 def class_sums(scalars, view, chunk, given, meta, noise, shared, slice_cycles, far, rows, shards):
     width = view.shape[-1]
+    count = view.shape[2] if view.shape[0] == 2 else view.shape[0]
     first = chunk == 0
-    count = view.shape[2] if view.shape[0] == 2 else view.shape[0]
     particles = count * GROUP
     out = pltpu.VMEM((rows, width), jnp.float32)
     kinds = [
-        ((particles, LANES), jnp.int32),
-        ((particles, 2 * LANES), view.dtype),
+        ((8, LANES), jnp.int32),
+        ((particles, 2 * LANES), given[0].dtype),
         ((particles, width // 2), jnp.float32),
         ((particles, width // 2), jnp.float32),
     ]
-    held = [pltpu.VMEM(shape, dtype) for shape, dtype in kinds]
     shapes = [out, out] + ([pltpu.HBM(shape, dtype) for shape, dtype in kinds] if first else [])
-    own = pltpu.VMEM((count, PAD, width), view.dtype)
-    scratch = [pltpu.VMEM((2 * rows, width), jnp.float32)]
+    scratch = [
+        pltpu.VMEM((2 * rows, width), jnp.float32),
+        pltpu.VMEM((count, PAD, width), view.dtype),
+    ]
     if first:
-        scratch += [pltpu.VMEM((shards * PAD, LANES), jnp.float32), own, *held]
-    else:
-        scratch += [own, *held[1:]]
+        scratch += [pltpu.VMEM((shards * PAD, LANES), jnp.float32)]
+        scratch += [pltpu.VMEM(shape, dtype) for shape, dtype in kinds]
     ins = [meta] if first else []
     return pl.pallas_call(
         functools.partial(
             sums_kernel, slice_cycles=slice_cycles, far=far, chunk=chunk, shards=shards
         ),
         out_shape=shapes,
-        in_specs=[SCALARS] * 3 + [HERE] * len(ins) + [HERE, THERE] + [HERE] * (GROUP - 1)
-        + [THERE] * len(shared),
+        in_specs=[SCALARS] * 3 + [HERE] * (len(ins) + 1) + [THERE]
+        + [HERE] * (GROUP - 1 + len(shared)),
         out_specs=[HERE, HERE] + [THERE] * (len(shapes) - 2),
         scratch_shapes=scratch
-        + [pltpu.SMEM((particles, LANES), jnp.int32), pltpu.SemaphoreType.DMA((6,))],
+        + [pltpu.SMEM((8, LANES), jnp.int32), pltpu.SemaphoreType.DMA((6,))],
         cost_estimate=cost(2.5),
         compiler_params=room(((2 * rows, width), 8), ((particles * PAD, width), 4)),
-    )(
-        *scalars, *held_near(*ins), noise, *held_far(view), *held_near(*given), *held_far(*shared)
-    )
+    )(*scalars, *held_near(*ins), noise, *held_far(view), *held_near(*given, *shared))
 
 
 def spans(rows):

time: 85.5 us -> 83.7 us (0.979)
  Pallas kernels: 30.8 us -> 28.9 us
    pallas_call x2, Pallas kernels: 6.12 us -> 5.12 us  [class_sums(): pl.pallas_call(functools.partial(sums_kernel, slice_cycles=slice_cycles,...]
    pallas_call x1, Pallas kernels: 2.04 us -> 1.08 us  [rotation_table(): pl.pallas_call(table_kernel, out_shape=pltpu.VMEM((width, width), jnp.bfl...]
  transfers between devices with their start and end apart: 14 -> 14, of which waited for: 8 -> 8; matrix products, arithmetic and copies ran while one was open for 0% -> 0% of each run, Pallas kernels for 30% -> 29%
where the time goes in v1:
time: 83.7 us; the launch traced here: 83.2 us
  waiting for transfers between devices  38.6 us (46%)
  Pallas kernels  28.9 us (35%)
  starting transfers between devices  14.9 us (18%)
  between operations  0.85 us (1%)
    ppermute x14, waiting for transfers between devices, swap(): return lax.ppermute(value, axis, [(i, i ^ mask) for i in range(size)])  38.6 us
    pallas_call x2, Pallas kernels, score(): pl.pallas_call(functools.partial(score_kernel, merge=merge, start=start),...  18.4 us
    ppermute x14, starting transfers between devices, swap(): return lax.ppermute(value, axis, [(i, i ^ mask) for i in range(size)])  14.9 us
    pallas_call x2, Pallas kernels, class_sums(): pl.pallas_call(functools.partial(sums_kernel, slice_cycles=slice_cycles,...  5.12 us
    pallas_call x2, Pallas kernels, pieces(): pl.pallas_call(functools.partial(pieces_kernel, chunk=chunk), out_shape=s...  2.6 us
  transfers between devices with their start and end apart: 14, of which 8 were waited for; matrix products, arithmetic and copies ran while one was open for 0% of the time, Pallas kernels for 29%

profile of v1, /device:TPU:0, one launch (start us, length us, event | category | flops | bytes accessed | tf_op | source)
XLA Modules:
  0.0 83.2 jit_solution(16013237317730631233)
XLA Ops:
  0.7 1.3 %shard_map.87 = (bf16[16,256]{1,0:T(8,128)(2,1)S(1)}, bf16[17,16,512]{2,1,0:T(8,128)(2,1)S(1)}, bf16[17,16,512]{2,1,0:T(8,128)(2,1)S(1)}, bf16[17,16,512]{2,1,0:T(8,128)(2,1)S(1)}) custom-call(s32[1]{0:T(128)} %bitcast.2.near_ref, s32[1]{0:T(128)} %bitcast.3.top_ref, bf16[16,2,4,16,512]{4,3,2,1,0:T(8,128)(2,1)} %bitcast.37, bf16[16,128]{1,0:T(8,128)(2,1)} %ctf_ref.3, ...), custom_call_target="tpu_custom_call" | custom-call | bytes 5400000 | tf_op jit(solution)/shard_map/pallas_call | solution.py:304
  2.0 3.0 %collective-permute-start.3 = (bf16[17,16,512]{2,1,0:T(8,128)(2,1)S(1)}, bf16[17,16,512]{2,1,0:T(8,128)(2,1)S(1)}, u32[]{:S(2)}, u32[]{:S(2)}) collective-permute-start(bf16[17,16,512]{2,1,0:T(8,128)(2,1)S(1)} %get-tuple-element.29), channel_id=1, source_target_pairs={{0,4},{4,0},{8,12},{12,8},{16,20},{20,16},{24,28},{28,24},{1,5},{5... | collective-permute-start | bytes 835592 | tf_op jit(solution)/shard_map/ppermute | solution.py:63
  5.0 1.6 %collective-permute-start.4 = (bf16[17,16,512]{2,1,0:T(8,128)(2,1)S(1)}, bf16[17,16,512]{2,1,0:T(8,128)(2,1)S(1)}, u32[]{:S(2)}, u32[]{:S(2)}) collective-permute-start(bf16[17,16,512]{2,1,0:T(8,128)(2,1)S(1)} %get-tuple-element.30), channel_id=1, source_target_pairs={{0,8},{4,12},{8,0},{12,4},{16,24},{20,28},{24,16},{28,20},{1,9},{5... | collective-permute-start | bytes 835592 | tf_op jit(solution)/shard_map/ppermute | solution.py:63
  6.6 5.1 %collective-permute-done.3.refs_3_ = bf16[17,16,512]{2,1,0:T(8,128)(2,1)S(1)} collective-permute-done((bf16[17,16,512]{2,1,0:T(8,128)(2,1)S(1)}, bf16[17,16,512]{2,1,0:T(8,128)(2,1)S(1)}, u32[]{:S(2)}, u32[]{:S(2)}) %collective-permute-start.3) | collective-permute-done | bytes 278560 | tf_op jit(solution)/shard_map/ppermute | solution.py:63
  11.7 2.9 %collective-permute-done.4.refs_4_ = bf16[17,16,512]{2,1,0:T(8,128)(2,1)S(1)} collective-permute-done((bf16[17,16,512]{2,1,0:T(8,128)(2,1)S(1)}, bf16[17,16,512]{2,1,0:T(8,128)(2,1)S(1)}, u32[]{:S(2)}, u32[]{:S(2)}) %collective-permute-start.4) | collective-permute-done | bytes 278560 | tf_op jit(solution)/shard_map/ppermute | solution.py:63
  14.6 4.4 %collective-permute-done.5.refs_5_ = bf16[17,16,512]{2,1,0:T(8,128)(2,1)S(1)} collective-permute-done((bf16[17,16,512]{2,1,0:T(8,128)(2,1)S(1)}, bf16[17,16,512]{2,1,0:T(8,128)(2,1)S(1)}, u32[]{:S(2)}, u32[]{:S(2)}) %collective-permute-start.5) | collective-permute-done | bytes 278560 | tf_op jit(solution)/shard_map/ppermute | solution.py:63
  18.9 2.8 %shard_map.88 = (f32[416,512]{1,0:T(8,128)S(1)}, f32[416,512]{1,0:T(8,128)}, s32[8,128]{1,0:T(8,128)}, bf16[64,256]{1,0:T(8,128)(2,1)}, f32[64,256]{1,0:T(8,128)}, /*index=5*/f32[64,256]{1,0:T(8,128)}) custom-call(s32[1]{0:T(128)} %bitcast.2.near_ref, s32[1]{0:T(128)} %bitcast.3.top_ref, s32[1]{0:T(128)} %bitcast.4.cls_ref, ...), custom_call_target="tpu_custom_call" | custom-call | bytes 9000000 | tf_op jit(solution)/shard_map/pallas_call | solution.py:441
  21.9 1.3 %shard_map.86 = (bf16[16,16,512]{2,1,0:T(8,128)(2,1)S(1)}, bf16[16,16,512]{2,1,0:T(8,128)(2,1)S(1)}, bf16[16,16,512]{2,1,0:T(8,128)(2,1)S(1)}) custom-call(s32[1]{0:T(128)} %bitcast.2.near_ref, s32[1]{0:T(128)} %bitcast.3.top_ref, bf16[16,2,4,16,512]{4,3,2,1,0:T(8,128)(2,1)} %bitcast.39), custom_call_target="tpu_custom_call" | custom-call | bytes 5400000 | tf_op jit(solution)/shard_map/pallas_call | solution.py:304
  23.1 1.7 %collective-permute-start = (bf16[16,16,512]{2,1,0:T(8,128)(2,1)S(1)}, bf16[16,16,512]{2,1,0:T(8,128)(2,1)S(1)}, u32[]{:S(2)}, u32[]{:S(2)}) collective-permute-start(bf16[16,16,512]{2,1,0:T(8,128)(2,1)S(1)} %get-tuple-element.25), channel_id=1, source_target_pairs={{0,4},{4,0},{8,12},{12,8},{16,20},{20,16},{24,28},{28,24},{1,5},{5... | collective-permute-start | bytes 786440 | tf_op jit(solution)/shard_map/ppermute | solution.py:63
  24.9 1.6 %collective-permute-start.1 = (bf16[16,16,512]{2,1,0:T(8,128)(2,1)S(1)}, bf16[16,16,512]{2,1,0:T(8,128)(2,1)S(1)}, u32[]{:S(2)}, u32[]{:S(2)}) collective-permute-start(bf16[16,16,512]{2,1,0:T(8,128)(2,1)S(1)} %get-tuple-element.26), channel_id=1, source_target_pairs={{0,8},{4,12},{8,0},{12,4},{16,24},{20,28},{24,16},{28,20},{1,9},{5... | collective-permute-start | bytes 786440 | tf_op jit(solution)/shard_map/ppermute | solution.py:63
  26.7 5.2 %collective-permute-done.refs_2_ = bf16[16,16,512]{2,1,0:T(8,128)(2,1)S(1)} collective-permute-done((bf16[16,16,512]{2,1,0:T(8,128)(2,1)S(1)}, bf16[16,16,512]{2,1,0:T(8,128)(2,1)S(1)}, u32[]{:S(2)}, u32[]{:S(2)}) %collective-permute-start) | collective-permute-done | bytes 262176 | tf_op jit(solution)/shard_map/ppermute | solution.py:63
  31.9 2.1 %collective-permute-done.1.refs_3_ = bf16[16,16,512]{2,1,0:T(8,128)(2,1)S(1)} collective-permute-done((bf16[16,16,512]{2,1,0:T(8,128)(2,1)S(1)}, bf16[16,16,512]{2,1,0:T(8,128)(2,1)S(1)}, u32[]{:S(2)}, u32[]{:S(2)}) %collective-permute-start.1) | collective-permute-done | bytes 262176 | tf_op jit(solution)/shard_map/ppermute | solution.py:63
  34.0 4.7 %collective-permute-done.2.refs_4_ = bf16[16,16,512]{2,1,0:T(8,128)(2,1)S(1)} collective-permute-done((bf16[16,16,512]{2,1,0:T(8,128)(2,1)S(1)}, bf16[16,16,512]{2,1,0:T(8,128)(2,1)S(1)}, u32[]{:S(2)}, u32[]{:S(2)}) %collective-permute-start.2) | collective-permute-done | bytes 262176 | tf_op jit(solution)/shard_map/ppermute | solution.py:63
  38.7 2.3 %shard_map.89 = (f32[384,512]{1,0:T(8,128)S(1)}, f32[384,512]{1,0:T(8,128)}) custom-call(s32[1]{0:T(128)} %bitcast.2.near_ref, s32[1]{0:T(128)} %bitcast.3.top_ref, s32[1]{0:T(128)} %bitcast.4.cls_ref, f32[1,128]{1,0:T(1,128)S(1)} %bitcast.34, bf16[16,2,4,16,512]{4,3,2,1,0:T(8,128)(2,1)} %bitcast.40, bf16[16,16,512]{2,1,0:T(8,128)(2,1)S(1)} %collective-permute-done.refs_2_, ...), custom_call_target="tpu_custom_call" | custom-call | bytes 9000000 | tf_op jit(solution)/shard_map/pallas_call | solution.py:441
  41.1 1.8 %collective-permute-start.11 = (bf16[12,32,512]{2,1,0:T(8,128)(2,1)}, bf16[12,32,512]{2,1,0:T(8,128)(2,1)}, u32[]{:S(2)}, u32[]{:S(2)}) collective-permute-start(bf16[12,32,512]{2,1,0:T(8,128)(2,1)} %param.10), channel_id=1, source_target_pairs={{0,2},{1,3},{2,0},{3,1},{4,6},{5,7},{6,4},{7,5},{8,10},{9,11},{10,... | collective-permute-start | bytes 1179656 | tf_op jit(solution)/shard_map/ppermute | solution.py:63
  43.1 0.4 collective-permute-start.9
  43.5 10.0 %collective-permute-done.11 = bf16[12,32,512]{2,1,0:T(8,128)(2,1)} collective-permute-done((bf16[12,32,512]{2,1,0:T(8,128)(2,1)}, bf16[12,32,512]{2,1,0:T(8,128)(2,1)}, u32[]{:S(2)}, u32[]{:S(2)}) %collective-permute-start.11) | collective-permute-done | bytes 393248 | tf_op jit(solution)/shard_map/ppermute | solution.py:63
  53.5 4.3 %collective-permute-done.9 = s16[1,224,512]{2,1,0:T(8,128)(2,1)S(1)} collective-permute-done((s16[1,224,512]{2,1,0:T(8,128)(2,1)S(1)}, s16[1,224,512]{2,1,0:T(8,128)(2,1)S(1)}, u32[]{:S(2)}, u32[]{:S(2)}) %collective-permute-start.9) | collective-permute-done | bytes 229408 | tf_op jit(solution)/shard_map/ppermute | solution.py:63
  58.1 2.8 %collective-permute-start.10 = (s16[224,512]{1,0:T(8,128)(2,1)S(1)}, s16[224,512]{1,0:T(8,128)(2,1)S(1)}, u32[]{:S(2)}, u32[]{:S(2)}) collective-permute-start(s16[224,512]{1,0:T(8,128)(2,1)S(1)} %get-tuple-element.45), channel_id=1, source_target_pairs={{0,16},{4,20},{8,24},{12,28},{16,0},{20,4},{24,8},{28,12},{1,17},{... | collective-permute-start | bytes 688136 | tf_op jit(solution)/shard_map/ppermute | solution.py:63
  61.1 1.6 %collective-permute-start.7 = (s16[1,208,512]{2,1,0:T(8,128)(2,1)S(1)}, s16[1,208,512]{2,1,0:T(8,128)(2,1)S(1)}, u32[]{:S(2)}, u32[]{:S(2)}) collective-permute-start(s16[1,208,512]{2,1,0:T(8,128)(2,1)S(1)} %get-tuple-element.39), channel_id=1, source_target_pairs={{0,2},{1,3},{2,0},{3,1},{4,6},{5,7},{6,4},{7,5},{8,10},{9,11},{10,... | collective-permute-start | bytes 638984 | tf_op jit(solution)/shard_map/ppermute | solution.py:63
  62.7 1.1 %table.1.table_ref = bf16[512,512]{1,0:T(8,128)(2,1)S(1)} custom-call(), custom_call_target="tpu_custom_call" | custom-call | bytes 7200000 | tf_op jit(solution)/shard_map/table/pallas_call | solution.py:43
  63.8 8.9 %shard_map.92 = (f32[16,128]{1,0:T(8,128)S(1)}, f32[16,128]{1,0:T(8,128)S(1)}) custom-call(bf16[16,128,512]{2,1,0:T(8,128)(2,1)} %image_ref.3, bf16[16,128]{1,0:T(8,128)(2,1)S(1)} %copy-done.2, f32[1,128]{1,0:T(1,128)S(1)} %bitcast.35, bf16[384,512]{1,0:T(8,128)(2,1)} %bitcast.20.first_ref, bf16[384,512]{1,0:T(8,128)(2,1)S(1)} %bitcast.30, ...), custom_call_target="tpu_custom_call" | custom-call | bytes 28800000 | tf_op jit(solution)/shard_map/pallas_call | solution.py:200
  72.7 9.5 %shard_map.93 = f32[1,16]{1,0:T(1,128)} custom-call(bf16[16,128,512]{2,1,0:T(8,128)(2,1)} %image_ref.3, bf16[16,128]{1,0:T(8,128)(2,1)S(1)} %copy-done.2, f32[1,128]{1,0:T(1,128)S(1)} %bitcast.36, bf16[384,512]{1,0:T(8,128)(2,1)} %bitcast.18.first_ref, bf16[384,512]{1,0:T(8,128)(2,1)S(1)} %bitcast.29, bf16[512,512]{1,0:T(8,128)(2,1)S(1)} %table.1.table_ref, ...), custom_call_target="tpu_custom_call" | custom-call | bytes 28800000 | tf_op jit(solution)/shard_map/pallas_call | solution.py:200
  82.3 1.0 %finish.1 = f32[12,16,512]{2,1,0:T(8,128)} custom-call(s32[1]{0:T(128)} %bitcast.dom_ref, f32[192,512]{1,0:T(8,128)S(1)} %bitcast.28, s16[208,512]{1,0:T(8,128)(2,1)S(1)} %bitcast.32, f32[16,128]{1,0:T(8,128)S(1)} %get-tuple-element.44.power_ref, s16[224,512]{1,0:T(8,128)(2,1)S(1)} %collective-permute-done.10.came_ref), custom_call_target="tpu_custom_call" | custom-call | bytes 3600000 | tf_op jit(solution)/shard_map/finish/pallas_call | solution.py:561
  (28 shorter events, 1.2 us)
Async XLA Ops:
  0.6 18.3 %copy-start.4 = (f32[128]{0:T(128)S(1)}, f32[128]{0:T(128)}, u32[]{:S(2)}) copy-start(f32[128]{0:T(128)} %param.9) | copy-start | bytes 1540
  2.0 9.7 %collective-permute-start.3 = (bf16[17,16,512]{2,1,0:T(8,128)(2,1)S(1)}, bf16[17,16,512]{2,1,0:T(8,128)(2,1)S(1)}, u32[]{:S(2)}, u32[]{:S(2)}) collective-permute-start(bf16[17,16,512]{2,1,0:T(8,128)(2,1)S(1)} %get-tuple-element.29), channel_id=1, source_target_pairs={{0,4},{4,0},{8,12},{12,8},{16,20},{20,16},{24,28},{28,24},{1,5},{5... | collective-permute-start | bytes 835592 | tf_op jit(solution)/shard_map/ppermute | solution.py:63
  5.0 9.5 %collective-permute-start.4 = (bf16[17,16,512]{2,1,0:T(8,128)(2,1)S(1)}, bf16[17,16,512]{2,1,0:T(8,128)(2,1)S(1)}, u32[]{:S(2)}, u32[]{:S(2)}) collective-permute-start(bf16[17,16,512]{2,1,0:T(8,128)(2,1)S(1)} %get-tuple-element.30), channel_id=1, source_target_pairs={{0,8},{4,12},{8,0},{12,4},{16,24},{20,28},{24,16},{28,20},{1,9},{5... | collective-permute-start | bytes 835592 | tf_op jit(solution)/shard_map/ppermute | solution.py:63
  6.6 12.3 %collective-permute-start.5 = (bf16[17,16,512]{2,1,0:T(8,128)(2,1)S(1)}, bf16[17,16,512]{2,1,0:T(8,128)(2,1)S(1)}, u32[]{:S(2)}, u32[]{:S(2)}) collective-permute-start(bf16[17,16,512]{2,1,0:T(8,128)(2,1)S(1)} %get-tuple-element.31), channel_id=1, source_target_pairs={{0,12},{4,8},{8,4},{12,0},{16,28},{20,24},{24,20},{28,16},{1,13},{... | collective-permute-start | bytes 835592 | tf_op jit(solution)/shard_map/ppermute | solution.py:63
  21.7 17.0 %copy-start = (f32[64,256]{1,0:T(8,128)S(1)}, f32[64,256]{1,0:T(8,128)}, u32[]{:S(2)}) copy-start(f32[64,256]{1,0:T(8,128)} %get-tuple-element.34.refs_7_) | copy-start | bytes 196612
  21.7 17.0 %copy-start.1 = (f32[64,256]{1,0:T(8,128)S(1)}, f32[64,256]{1,0:T(8,128)}, u32[]{:S(2)}) copy-start(f32[64,256]{1,0:T(8,128)} %get-tuple-element.35.refs_8_) | copy-start | bytes 196612
  21.8 17.0 %copy-start.3 = (bf16[64,256]{1,0:T(8,128)(2,1)S(1)}, bf16[64,256]{1,0:T(8,128)(2,1)}, u32[]{:S(2)}) copy-start(bf16[64,256]{1,0:T(8,128)(2,1)} %get-tuple-element.33.refs_6_) | copy-start | bytes 98308
  21.8 16.9 %copy-start.5 = (s32[8,128]{1,0:T(8,128)S(1)}, s32[8,128]{1,0:T(8,128)}, u32[]{:S(2)}) copy-start(s32[8,128]{1,0:T(8,128)} %get-tuple-element.32.refs_5_) | copy-start | bytes 12292
  21.8 21.1 %collective-permute-start.8 = (f32[416,512]{1,0:T(8,128)}, f32[416,512]{1,0:T(8,128)S(1)}, u32[]{:S(2)}, u32[]{:S(2)}) collective-permute-start(f32[416,512]{1,0:T(8,128)} %get-tuple-element.41), channel_id=1, source_target_pairs={{0,1},{1,0},{2,3},{3,2},{4,5},{5,4},{6,7},{7,6},{8,9},{9,8},{10,11... | collective-permute-start | bytes 2555912 | tf_op jit(solution)/shard_map/ppermute | solution.py:63
  23.1 8.8 %collective-permute-start = (bf16[16,16,512]{2,1,0:T(8,128)(2,1)S(1)}, bf16[16,16,512]{2,1,0:T(8,128)(2,1)S(1)}, u32[]{:S(2)}, u32[]{:S(2)}) collective-permute-start(bf16[16,16,512]{2,1,0:T(8,128)(2,1)S(1)} %get-tuple-element.25), channel_id=1, source_target_pairs={{0,4},{4,0},{8,12},{12,8},{16,20},{20,16},{24,28},{28,24},{1,5},{5... | collective-permute-start | bytes 786440 | tf_op jit(solution)/shard_map/ppermute | solution.py:63
  24.9 9.2 %collective-permute-start.1 = (bf16[16,16,512]{2,1,0:T(8,128)(2,1)S(1)}, bf16[16,16,512]{2,1,0:T(8,128)(2,1)S(1)}, u32[]{:S(2)}, u32[]{:S(2)}) collective-permute-start(bf16[16,16,512]{2,1,0:T(8,128)(2,1)S(1)} %get-tuple-element.26), channel_id=1, source_target_pairs={{0,8},{4,12},{8,0},{12,4},{16,24},{20,28},{24,16},{28,20},{1,9},{5... | collective-permute-start | bytes 786440 | tf_op jit(solution)/shard_map/ppermute | solution.py:63
  26.4 12.3 %collective-permute-start.2 = (bf16[16,16,512]{2,1,0:T(8,128)(2,1)S(1)}, bf16[16,16,512]{2,1,0:T(8,128)(2,1)S(1)}, u32[]{:S(2)}, u32[]{:S(2)}) collective-permute-start(bf16[16,16,512]{2,1,0:T(8,128)(2,1)S(1)} %get-tuple-element.27), channel_id=1, source_target_pairs={{0,12},{4,8},{8,4},{12,0},{16,28},{20,24},{24,20},{28,16},{1,13},{... | collective-permute-start | bytes 786440 | tf_op jit(solution)/shard_map/ppermute | solution.py:63
  41.0 19.8 %collective-permute-start.6 = (f32[384,512]{1,0:T(8,128)}, f32[384,512]{1,0:T(8,128)S(1)}, u32[]{:S(2)}, u32[]{:S(2)}) collective-permute-start(f32[384,512]{1,0:T(8,128)} %get-tuple-element.37), channel_id=1, source_target_pairs={{0,1},{1,0},{2,3},{3,2},{4,5},{5,4},{6,7},{7,6},{8,9},{9,8},{10,11... | collective-permute-start | bytes 2359304 | tf_op jit(solution)/shard_map/ppermute | solution.py:63
  41.1 12.4 %collective-permute-start.11 = (bf16[12,32,512]{2,1,0:T(8,128)(2,1)}, bf16[12,32,512]{2,1,0:T(8,128)(2,1)}, u32[]{:S(2)}, u32[]{:S(2)}) collective-permute-start(bf16[12,32,512]{2,1,0:T(8,128)(2,1)} %param.10), channel_id=1, source_target_pairs={{0,2},{1,3},{2,0},{3,1},{4,6},{5,7},{6,4},{7,5},{8,10},{9,11},{10,... | collective-permute-start | bytes 1179656 | tf_op jit(solution)/shard_map/ppermute | solution.py:63
  42.9 20.9 %copy-start.2 = (bf16[16,128]{1,0:T(8,128)(2,1)S(1)}, bf16[16,128]{1,0:T(8,128)(2,1)}, u32[]{:S(2)}) copy-start(bf16[16,128]{1,0:T(8,128)(2,1)} %ctf_ref.3) | copy-start | bytes 12292
  43.1 14.6 %collective-permute-start.9 = (s16[1,224,512]{2,1,0:T(8,128)(2,1)S(1)}, s16[1,224,512]{2,1,0:T(8,128)(2,1)S(1)}, u32[]{:S(2)}, u32[]{:S(2)}) collective-permute-start(s16[1,224,512]{2,1,0:T(8,128)(2,1)S(1)} %get-tuple-element.43), channel_id=1, source_target_pairs={{0,2},{1,3},{2,0},{3,1},{4,6},{5,7},{6,4},{7,5},{8,10},{9,11},{10,... | collective-permute-start | bytes 688136 | tf_op jit(solution)/shard_map/ppermute | solution.py:63
  43.5 20.3 %collective-permute-start.13 = (bf16[12,32,512]{2,1,0:T(8,128)(2,1)}, bf16[12,32,512]{2,1,0:T(8,128)(2,1)S(1)}, u32[]{:S(2)}, u32[]{:S(2)}) collective-permute-start(bf16[12,32,512]{2,1,0:T(8,128)(2,1)} %param.10), channel_id=1, source_target_pairs={{0,1},{1,0},{2,3},{3,2},{4,5},{5,4},{6,7},{7,6},{8,9},{9,8},{10,11... | collective-permute-start | bytes 1179656 | tf_op jit(solution)/shard_map/ppermute | solution.py:63
  53.5 19.2 %collective-permute-start.12 = (bf16[12,32,512]{2,1,0:T(8,128)(2,1)}, bf16[12,32,512]{2,1,0:T(8,128)(2,1)S(1)}, u32[]{:S(2)}, u32[]{:S(2)}) collective-permute-start(bf16[12,32,512]{2,1,0:T(8,128)(2,1)} %collective-permute-done.11), channel_id=1, source_target_pairs={{0,1},{1,0},{2,3},{3,2},{4,5},{5,4},{6,7},{7,6},{8,9},{9,8},{10,11... | collective-permute-start | bytes 1179656 | tf_op jit(solution)/shard_map/ppermute | solution.py:63
  58.1 24.2 %collective-permute-start.10 = (s16[224,512]{1,0:T(8,128)(2,1)S(1)}, s16[224,512]{1,0:T(8,128)(2,1)S(1)}, u32[]{:S(2)}, u32[]{:S(2)}) collective-permute-start(s16[224,512]{1,0:T(8,128)(2,1)S(1)} %get-tuple-element.45), channel_id=1, source_target_pairs={{0,16},{4,20},{8,24},{12,28},{16,0},{20,4},{24,8},{28,12},{1,17},{... | collective-permute-start | bytes 688136 | tf_op jit(solution)/shard_map/ppermute | solution.py:63
  61.1 21.1 %collective-permute-start.7 = (s16[1,208,512]{2,1,0:T(8,128)(2,1)S(1)}, s16[1,208,512]{2,1,0:T(8,128)(2,1)S(1)}, u32[]{:S(2)}, u32[]{:S(2)}) collective-permute-start(s16[1,208,512]{2,1,0:T(8,128)(2,1)S(1)} %get-tuple-element.39), channel_id=1, source_target_pairs={{0,2},{1,3},{2,0},{3,1},{4,6},{5,7},{6,4},{7,5},{8,10},{9,11},{10,... | collective-permute-start | bytes 638984 | tf_op jit(solution)/shard_map/ppermute | solution.py:63

commit v2 on v1

--- a/solution.py
+++ b/solution.py
@@ -11,7 +11,7 @@
 
 CHUNKS = 2
 GROUP = 4
-FAR_CALLS = 1
+NEAR_CALLS = 2
 SPLITS = 4
 LANES = 128
 PAD = 16
@@ -19,8 +19,18 @@
 UNIT = math.log(2.0) / STEPS
 
 
-def table_kernel(out_ref):
+def table_kernel(image_ref, out_ref, low_ref, sems):
     width, turns_all = out_ref.shape
+    count, cycles, _ = low_ref.shape
+    part = count // SPLITS
+    copies = [
+        pltpu.make_async_copy(
+            image_ref.at[pl.ds(i * part, part), :cycles, :], low_ref.at[pl.ds(i * part, part)], sems.at[i]
+        )
+        for i in range(SPLITS)
+    ]
+    for copy in copies:
+        copy.start()
     half = width // 2
     quarter = half // 2
     step = 32
@@ -37,17 +47,25 @@
         out_ref[half + at : half + at + step, :] = (-sinv).astype(jnp.bfloat16)
         at = half + quarter + at
         out_ref[at : at + step, :] = (-sin_on).astype(jnp.bfloat16)
-
-
-def rotation_table(width):
+    for copy in copies:
+        copy.wait()
+
+
+def rotation_table(spectra, cycles):
+    count, _, width = spectra.shape
     return pl.pallas_call(
         table_kernel,
-        out_shape=pltpu.VMEM((width, width), jnp.bfloat16),
-        out_specs=HERE,
+        out_shape=(
+            pltpu.VMEM((width, width), jnp.bfloat16),
+            pltpu.VMEM((count, cycles, width), spectra.dtype),
+        ),
+        in_specs=[THERE],
+        out_specs=(HERE, HERE),
+        scratch_shapes=[pltpu.SemaphoreType.DMA((SPLITS,))],
         cost_estimate=cost(2),
         compiler_params=room(((width, width), 4)),
         name="table",
-    )()
+    )(*held_far(spectra))
 
 
 def held_near(*values):
@@ -82,17 +100,15 @@
 
 
 def score_kernel(
-    image_ref, ctf_ref, noise_ref, first_ref, second_ref, table_ref, *refs, merge, start
+    low_ref, ctf_ref, noise_ref, first_ref, second_ref, table_ref, *refs, merge, start
 ):
-    before = refs[:2] if merge else None
-    row_ref = refs[2] if merge else None
-    outs = refs[3:4] if merge else refs[:2]
-    low_ref, image, image_sum, staged, classes, cross, sem = refs[4 if merge else 2 :]
-    count, cycles, width = low_ref.shape
-    fetch = pltpu.make_async_copy(image_ref.at[pl.ds(start, count), :cycles, :], low_ref, sem)
-    fetch.start()
+    before, refs = refs[:merge], refs[merge:]
+    outs, refs = refs[: 1 if merge else 2], refs[1 if merge else 2 :]
+    image, image_sum, staged, classes, cross = refs
+    _, cycles, width = low_ref.shape
     tiles = width // LANES
     pairs = tiles // 2
+    count = image.shape[1] // cycles
     kinds = cross.shape[0] // count
     part = first_ref.shape[0]
     ctf = ctf_ref[start : start + count, :].astype(jnp.float32)
@@ -120,11 +136,10 @@
             total = jnp.sum(square[r], axis=1, keepdims=True)
             norm = jnp.where(iota((8, LANES), 1) == r, total, norm)
         norms.append(norm)
-    fetch.wait()
     for n in range(count):
         row = jnp.broadcast_to(weight[n : n + 1, :], (cycles, LANES))
         column = jnp.sum(jnp.where(eye, row, 0.0), axis=1, keepdims=True)
-        low = low_ref[n].astype(jnp.float32)
+        low = low_ref[start + n].astype(jnp.float32)
         weighted = (column * low).astype(jnp.bfloat16).astype(jnp.float32)
         for f in range(tiles):
             image[f, n * cycles : (n + 1) * cycles, :] = weighted[:, f * LANES : (f + 1) * LANES]
@@ -164,7 +179,7 @@
     )
     cross[...] = scores
     inner = iota((8, LANES), 1) < cycles
-    row = row_ref[...] if merge else None
+    row = jnp.zeros(outs[0].shape, jnp.float32)
     for n in range(count):
             mine = []
             for b in range(blocks):
@@ -175,7 +190,9 @@
             mine = jnp.concatenate(mine, axis=0)
             top = jnp.max(mine, axis=(0, 1), keepdims=True)
             if merge:
-                top_before, total_before = before[0][start + n : start + n + 1, :], before[1][start + n : start + n + 1, :]
+                per = count // (merge // 2)
+                pair, i = before[n // per * 2 : n // per * 2 + 2], n % per
+                top_before, total_before = pair[0][i : i + 1, :], pair[1][i : i + 1, :]
                 top = jnp.maximum(top, jnp.max(top_before, axis=1, keepdims=True))
             total = jnp.sum(jnp.exp(mine - top), axis=(0, 1), keepdims=True)
             if merge:
@@ -189,40 +206,36 @@
         outs[0][...] = row
 
 
-def score(spectra, ctf, noise, first, second, table, before, start, count):
-    width = spectra.shape[2]
-    cycles = first.shape[1]
+def score(low, ctf, noise, first, second, table, before, start, count):
+    _, cycles, width = low.shape
     kinds = 2 * first.shape[0]
-    merge = before is not None
+    merge = len(before)
     each = pltpu.VMEM((count, LANES), jnp.float32)
-    row = jax.ShapeDtypeStruct((1, ctf.shape[0]), jnp.float32)
+    row = jax.ShapeDtypeStruct((1, count), jnp.float32)
     part = (kinds // 2 * cycles, width)
-    outs = pl.pallas_call(
+    return pl.pallas_call(
         functools.partial(score_kernel, merge=merge, start=start),
         out_shape=row if merge else (each, each),
-        in_specs=[THERE] + [HERE] * (8 if merge else 5),
+        in_specs=[HERE] * (6 + merge),
         out_specs=HERE if merge else (HERE, HERE),
         scratch_shapes=[
-            pltpu.VMEM((count, cycles, width), spectra.dtype),
             pltpu.VMEM((width // LANES, count * cycles, LANES), jnp.float32),
             pltpu.VMEM((width // LANES // 2, count * cycles, LANES), jnp.float32),
             pltpu.VMEM((width // LANES, kinds * cycles, LANES), jnp.float32),
             pltpu.VMEM((width // LANES // 2 * 3, cycles, kinds, LANES), jnp.float32),
             pltpu.VMEM((count * kinds, width), jnp.float32),
-            pltpu.SemaphoreType.DMA,
         ],
-        cost_estimate=cost(8),
+        cost_estimate=cost(count / 2),
         compiler_params=room(
-            ((count * cycles, width), 10),
+            ((count * cycles, width), 8),
             ((kinds * cycles, width), 12),
             ((count * kinds, width), 8),
             (table.shape, 2),
         ),
     )(
-        *held_far(spectra), ctf, noise, *held_near(first.reshape(part), second.reshape(part), table),
-        *(before or ()),
+        *held_near(low), ctf, noise, *held_near(first.reshape(part), second.reshape(part), table),
+        *before,
     )
-    return outs
 
 
 def part_of(view_ref, top, near):
@@ -332,8 +345,17 @@
     count = particles // GROUP
     width = 2 * half
     size = keep_ref.shape[0] // (shards // 2)
-    fetch = pltpu.make_async_copy(part_of(view_ref, side, near_ref[0]), own, sems.at[5])
-    fetch.start()
+    part = count // SPLITS
+    fetches = [
+        pltpu.make_async_copy(
+            part_of(view_ref, side, near_ref[0]).at[pl.ds(i * part, part)],
+            own.at[pl.ds(i * part, part)],
+            sems.at[5 + i],
+        )
+        for i in range(SPLITS)
+    ]
+    for fetch in fetches:
+        fetch.start()
     schedule = pltpu.make_async_copy(plan, place_ref, sems.at[0])
     if chunk == 0:
         metas[:count] = meta_ref[...]
@@ -395,7 +417,8 @@
     for g in (*range(1, GROUP), 0):
         source = given[g - 1] if g else own
         if g == 0:
-            fetch.wait()
+            for fetch in fetches:
+                fetch.wait()
         for start in range(g * count, (g + 1) * count, batch):
             done = [one(n, source) for n in range(start, start + batch)]
             for n, (re, im, power) in zip(range(start, start + batch), done):
@@ -447,7 +470,7 @@
         + [HERE] * (GROUP - 1 + len(shared)),
         out_specs=[HERE, HERE] + [THERE] * (len(shapes) - 2),
         scratch_shapes=scratch
-        + [pltpu.SMEM((8, LANES), jnp.int32), pltpu.SemaphoreType.DMA((6,))],
+        + [pltpu.SMEM((8, LANES), jnp.int32), pltpu.SemaphoreType.DMA((5 + SPLITS,))],
         cost_estimate=cost(2.5),
         compiler_params=room(((2 * rows, width), 8), ((particles * PAD, width), 4)),
     )(*scalars, *held_near(*ins), noise, *held_far(view), *held_near(*given, *shared))
@@ -457,60 +480,82 @@
     return [(at, min(LANES, rows - at)) for at in range(0, rows, LANES)]
 
 
-def encode(value, out, at):
-    rows = value.shape[0]
+def encode(value, out, rows):
     codes = jnp.zeros((PAD, LANES), jnp.float32)
-    for i, (start, size) in enumerate(spans(rows)):
+    blocks = spans(rows)
+    for i, (start, size) in enumerate(blocks):
         x = value[start : start + size]
-        top = jnp.maximum(jnp.max(jnp.abs(x), axis=1, keepdims=True), 1e-30)
-        code = jnp.floor(jnp.log(top) / UNIT) + 1.0
-        scaled = x * (jnp.exp(-code * UNIT) * 32767.0)
-        scaled = jnp.clip(jnp.round(scaled), -32767.0, 32767.0)
-        out[at + start : at + start + size, :] = scaled.astype(jnp.int32).astype(jnp.int16)
+        scaled, code = coded(x)
+        out[start : start + size, :] = scaled
         eye = iota((size, LANES), 0) == iota((size, LANES), 1)
         row = jnp.sum(jnp.where(eye, code, 0.0), axis=0, keepdims=True)
         codes = jnp.where(iota((PAD, LANES), 0) == i, row, codes)
-    for f in range(out.shape[1] // LANES):
-        out[at + rows : at + rows + PAD, f * LANES : (f + 1) * LANES] = codes.astype(
-            jnp.int32
-        ).astype(jnp.int16)
-
-
-def decode(ref, at, rows):
-    codes = ref[at + rows : at + rows + PAD, :LANES].astype(jnp.int32).astype(jnp.float32)
+    out[rows:, :] = jnp.zeros((PAD, out.shape[1]), jnp.int16)
+    if value.shape[0] > rows:
+        scaled, code = coded(value[rows:, :LANES])
+        out[rows:, :LANES] = scaled
+        eye = iota((PAD, LANES), 0) == iota((PAD, LANES), 1)
+        row = jnp.sum(jnp.where(eye, code, 0.0), axis=0, keepdims=True)
+        codes = jnp.where(iota((PAD, LANES), 0) == len(blocks), row, codes)
+    out[rows:, LANES : 2 * LANES] = codes.astype(jnp.int32).astype(jnp.int16)
+
+
+def coded(x):
+    top = jnp.maximum(jnp.max(jnp.abs(x), axis=1, keepdims=True), 1e-30)
+    code = jnp.floor(jnp.log(top) / UNIT) + 1.0
+    scaled = jnp.round(x * (jnp.exp(-code * UNIT) * 32767.0))
+    return jnp.clip(scaled, -32767.0, 32767.0).astype(jnp.int32).astype(jnp.int16), code
+
+
+def decode(ref):
+    rows = ref.shape[0] - PAD
+    codes = ref[rows:, LANES : 2 * LANES].astype(jnp.int32).astype(jnp.float32)
     parts = []
     for i, (start, size) in enumerate(spans(rows)):
-        eye = iota((size, LANES), 0) == iota((size, LANES), 1)
-        row = jnp.broadcast_to(codes[i : i + 1], (size, LANES))
-        code = jnp.sum(jnp.where(eye, row, 0.0), axis=1, keepdims=True)
-        x = ref[at + start : at + start + size, :].astype(jnp.int32).astype(jnp.float32)
-        parts.append(x * (jnp.exp(code * UNIT) * (1.0 / 32767.0)))
+        parts.append(ref[start : start + size, :].astype(jnp.int32).astype(jnp.float32) * scale(codes, i, size))
     return jnp.concatenate(parts, axis=0)
 
 
-def shard_kernel(bit_ref, keep_ref, get_ref, own_ref, code_ref, *, coded):
+def decode_power(ref):
+    rows = ref.shape[0] - PAD
+    codes = ref[rows:, LANES : 2 * LANES].astype(jnp.int32).astype(jnp.float32)
+    x = ref[rows:, :LANES].astype(jnp.int32).astype(jnp.float32)
+    return x * scale(codes, len(spans(rows)), PAD)
+
+
+def scale(codes, i, size):
+    eye = iota((size, LANES), 0) == iota((size, LANES), 1)
+    row = jnp.broadcast_to(codes[i : i + 1], (size, LANES))
+    code = jnp.sum(jnp.where(eye, row, 0.0), axis=1, keepdims=True)
+    return jnp.exp(code * UNIT) * (1.0 / 32767.0)
+
+
+def shard_kernel(bit_ref, keep_ref, get_ref, own_ref, code_ref, *, was_coded):
     parts, rows, _ = own_ref.shape
-    if coded:
+    full = code_ref.shape[1] - PAD
+    if was_coded:
         for p in range(2 * parts):
-            keep_ref[p] = keep_ref[p] + decode(get_ref.at[p], 0, rows)
+            keep_ref[p, :full] = keep_ref[p, :full] + decode(get_ref.at[p])
+            if rows > full:
+                keep_ref[p, full:, :LANES] = keep_ref[p, full:, :LANES] + decode_power(get_ref.at[p])
     bit = bit_ref[0]
     for p in range(parts):
         mine, other = bit * parts + p, (1 - bit) * parts + p
-        if coded:
-            encode(keep_ref[other], code_ref.at[p], 0)
+        if was_coded:
+            encode(keep_ref[other], code_ref.at[p], full)
             own_ref[p] = keep_ref[mine]
         else:
-            encode(keep_ref[other] + get_ref[other], code_ref.at[p], 0)
+            encode(keep_ref[other] + get_ref[other], code_ref.at[p], full)
             own_ref[p] = keep_ref[mine] + get_ref[mine]
 
 
-def split_shards(bit, keep, get):
+def split_shards(bit, keep, get, full):
     parts, rows, width = keep.shape
     parts = parts // 2
     own = pltpu.VMEM((parts, rows, width), jnp.float32)
-    code = pltpu.VMEM((parts, rows + PAD, width), jnp.int16)
+    code = pltpu.VMEM((parts, full + PAD, width), jnp.int16)
     return pl.pallas_call(
-        functools.partial(shard_kernel, coded=get.dtype == jnp.int16),
+        functools.partial(shard_kernel, was_coded=get.dtype == jnp.int16),
         out_shape=(own, code),
         in_specs=[SCALARS, HERE, HERE],
         out_specs=(HERE, HERE),
@@ -519,11 +564,13 @@
     )(bit, *held_near(keep, get))
 
 
-def ahead_kernel(keep_ref, get_ref, power_ref, code_ref):
-    rows = keep_ref.shape[0]
-    total = keep_ref[...] + decode(get_ref, 0, rows)
-    power_ref[...] = total[rows - PAD :, :LANES]
-    encode(total, code_ref, 0)
+def ahead_kernel(keep_ref, get_ref, power_ref, code_ref, total):
+    full = keep_ref.shape[0] - PAD
+    total[:full] = keep_ref[:full] + decode(get_ref)
+    total[full:, :] = jnp.zeros((PAD, total.shape[1]), jnp.float32)
+    total[full:, :LANES] = keep_ref[full:, :LANES] + decode_power(get_ref)
+    power_ref[...] = total[full:, :LANES]
+    encode(total, code_ref, full)
 
 
 def ahead(keep, get):
@@ -532,22 +579,21 @@
         ahead_kernel,
         out_shape=(
             pltpu.VMEM((PAD, LANES), jnp.float32),
-            pltpu.VMEM((rows + PAD, width), jnp.int16),
+            pltpu.VMEM((rows, width), jnp.int16),
         ),
         in_specs=[HERE, HERE],
         out_specs=(HERE, HERE),
+        scratch_shapes=[pltpu.VMEM((rows, width), jnp.float32)],
         cost_estimate=cost(1),
-        compiler_params=room((keep.shape, 16)),
+        compiler_params=room((keep.shape, 20)),
         name="ahead",
     )(*held_near(keep, get))
 
 
 def final_kernel(dom_ref, keep_ref, get_ref, power_ref, came_ref, out):
     classes, cycles, _ = out.shape
-    rows = classes * cycles
-    came = decode(came_ref, 0, rows + PAD)
-    sums = keep_ref[...] + decode(get_ref, 0, rows) + came[:rows]
-    powers = power_ref[...] + came[rows:, :LANES]
+    sums = keep_ref[...] + decode(get_ref) + decode(came_ref)
+    powers = power_ref[...] + decode_power(came_ref)
     r = iota((cycles, LANES), 0)
     pick = iota((cycles, LANES), 1) == dom_ref[0] * cycles + r
     for k in range(classes):
@@ -569,17 +615,19 @@
     )(dom, *held_near(keep, get, power, came))
 
 
-def decoded(keep, get):
-    rows = keep.shape[0]
-    code = get[rows:, :LANES].astype(jnp.float32).reshape(-1)[:rows]
-    scale = jnp.exp(code * UNIT) * (1.0 / 32767.0)
-    return keep + get[:rows].astype(jnp.float32) * scale[:, None]
+def decoded(get):
+    rows = get.shape[0] - PAD
+    codes = get[rows:, LANES : 2 * LANES].astype(jnp.float32)
+    values = get.astype(jnp.float32)
+    scales = jnp.exp(codes * UNIT) * (1.0 / 32767.0)
+    blocks = len(spans(rows))
+    full = values[:rows] * scales[:blocks].reshape(-1)[:rows, None]
+    return full, values[rows:, :LANES] * scales[blocks, :PAD, None]
 
 
 def per_device(spectra, ctf, noise_power, references, owner, sub_class, rotation):
     count, cycles, width = spectra.shape
     k_local = references.shape[0]
-    turns_all = width
     domains, shards = lax.axis_size("dom"), lax.axis_size("cls")
     dom, cls = lax.axis_index("dom"), lax.axis_index("cls")
     far = domains // GROUP
@@ -605,16 +653,14 @@
         other_side = new if other_side is None else jnp.concatenate([other_side, new], axis=0)
         held = jnp.concatenate([held, new], axis=0) if 2 * mask < shards else held
         mask *= 2
-    table = rotation_table(turns_all)
+    table, low = rotation_table(spectra, references.shape[1])
     near_refs = swap(own_side, "cls", 1)
-    before = score(spectra, ctf, noise, own_side, near_refs, table, None, 0, count)
+    per = count // NEAR_CALLS
+    before = []
+    for i in range(NEAR_CALLS):
+        before += score(low, ctf, noise, own_side, near_refs, table, (), i * per, per)
     far_refs = swap(other_side, "cls", 1)
-    size = count // FAR_CALLS
-    row = jnp.zeros((1, count), jnp.float32)
-    for i in range(FAR_CALLS):
-        row = score(
-            spectra, ctf, noise, other_side, far_refs, table, (*before, row), i * size, size,
-        )
+    row = score(low, ctf, noise, other_side, far_refs, table, before, 0, count)
     log_evidence = row.reshape(count)
 
     scalars = (near, top, cls.reshape(1))
@@ -632,7 +678,7 @@
         mask = shards // 2
         while mask >= 2:
             bit = ((cls // mask) & 1).reshape(1)
-            keep, code = split_shards(bit, keep, get)
+            keep, code = split_shards(bit, keep, get, k_local * PAD)
             get = swap(code, "cls", mask)
             mask //= 2
         ends.append((keep[0], get[0]))
@@ -642,10 +688,10 @@
         new_refs = finish(dom.reshape(1), *ends[1], power, came, k_local, slice_cycles, width)
         return (new_refs, log_evidence)
 
-    came = decoded(jnp.zeros((came.shape[0] - PAD, width), jnp.float32), came)
-    numer = decoded(*ends[1]) + came[: k_local * PAD]
-    numer = numer.reshape(k_local, PAD, width)
-    power = power + came[k_local * PAD :, :LANES]
+    came, came_power = decoded(came)
+    keep, get = ends[1]
+    numer = (keep + decoded(get)[0] + came).reshape(k_local, PAD, width)
+    power = power + came_power
     left, mask = PAD, domains // 4
     while mask >= GROUP:
         bit = (dom // mask) & 1

time: 83.7 us -> 78 us (0.932)
  waiting for transfers between devices: 38.6 us -> 34.8 us
  Pallas kernels: 28.9 us -> 27 us
    ppermute x14, waiting for transfers between devices: 38.6 us -> 34.8 us  [swap(): return lax.ppermute(value, axis, [(i, i ^ mask) for i in range(size)])]
    pallas_call x2 -> x3, Pallas kernels: 18.4 us -> 15.2 us  [score(): pl.pallas_call(functools.partial(score_kernel, merge=merge, start=start),...]
    pallas_call x3, Pallas kernels: 1.54 us -> 2.73 us  [the longest x2 1.6 us: split_shards(): pl.pallas_call(functools.partial(shard_kernel, was_coded=get.dtype == jnp...]
  transfers between devices with their start and end apart: 14 -> 14, of which waited for: 8 -> 8; matrix products, arithmetic and copies ran while one was open for 0% -> 0% of each run, Pallas kernels for 29% -> 28%
where the time goes in v2:
time: 78 us; the launch traced here: 77.8 us
  waiting for transfers between devices  34.8 us (45%)
  Pallas kernels  27 us (35%)
  starting transfers between devices  15 us (19%)
  between operations  0.85 us (1%)
    ppermute x14, waiting for transfers between devices, swap(): return lax.ppermute(value, axis, [(i, i ^ mask) for i in range(size)])  34.8 us
    pallas_call x3, Pallas kernels, score(): pl.pallas_call(functools.partial(score_kernel, merge=merge, start=start),...  15.2 us
    ppermute x14, starting transfers between devices, swap(): return lax.ppermute(value, axis, [(i, i ^ mask) for i in range(size)])  15 us
    pallas_call x2, Pallas kernels, class_sums(): pl.pallas_call(functools.partial(sums_kernel, slice_cycles=slice_cycles,...  5.18 us
    pallas_call x2, Pallas kernels, pieces(): pl.pallas_call(functools.partial(pieces_kernel, chunk=chunk), out_shape=s...  2.65 us
    pallas_call x2, Pallas kernels, split_shards(): pl.pallas_call(functools.partial(shard_kernel, was_coded=get.dtype == jnp...  1.6 us
  transfers between devices with their start and end apart: 14, of which 8 were waited for; matrix products, arithmetic and copies ran while one was open for 0% of the time, Pallas kernels for 28%

profile of v2, /device:TPU:0, one launch (start us, length us, event | category | flops | bytes accessed | tf_op | source)
XLA Modules:
  0.0 77.8 jit_solution(1591002659040608823)
XLA Ops:
  0.7 1.3 %shard_map.87 = (bf16[16,256]{1,0:T(8,128)(2,1)S(1)}, bf16[17,16,512]{2,1,0:T(8,128)(2,1)S(1)}, bf16[17,16,512]{2,1,0:T(8,128)(2,1)S(1)}, bf16[17,16,512]{2,1,0:T(8,128)(2,1)S(1)}) custom-call(s32[1]{0:T(128)} %bitcast.2.near_ref, s32[1]{0:T(128)} %bitcast.3.top_ref, bf16[16,2,4,16,512]{4,3,2,1,0:T(8,128)(2,1)} %bitcast.41, bf16[16,128]{1,0:T(8,128)(2,1)} %ctf_ref.5, ...), custom_call_target="tpu_custom_call" | custom-call | bytes 5400000 | tf_op jit(solution)/shard_map/pallas_call | solution.py:317
  2.0 3.0 %collective-permute-start.3 = (bf16[17,16,512]{2,1,0:T(8,128)(2,1)S(1)}, bf16[17,16,512]{2,1,0:T(8,128)(2,1)S(1)}, u32[]{:S(2)}, u32[]{:S(2)}) collective-permute-start(bf16[17,16,512]{2,1,0:T(8,128)(2,1)S(1)} %get-tuple-element.33), channel_id=1, source_target_pairs={{0,4},{4,0},{8,12},{12,8},{16,20},{20,16},{24,28},{28,24},{1,5},{5... | collective-permute-start | bytes 835592 | tf_op jit(solution)/shard_map/ppermute | solution.py:81
  5.0 1.6 %collective-permute-start.4 = (bf16[17,16,512]{2,1,0:T(8,128)(2,1)S(1)}, bf16[17,16,512]{2,1,0:T(8,128)(2,1)S(1)}, u32[]{:S(2)}, u32[]{:S(2)}) collective-permute-start(bf16[17,16,512]{2,1,0:T(8,128)(2,1)S(1)} %get-tuple-element.34), channel_id=1, source_target_pairs={{0,8},{4,12},{8,0},{12,4},{16,24},{20,28},{24,16},{28,20},{1,9},{5... | collective-permute-start | bytes 835592 | tf_op jit(solution)/shard_map/ppermute | solution.py:81
  6.6 5.1 %collective-permute-done.3.refs_3_ = bf16[17,16,512]{2,1,0:T(8,128)(2,1)S(1)} collective-permute-done((bf16[17,16,512]{2,1,0:T(8,128)(2,1)S(1)}, bf16[17,16,512]{2,1,0:T(8,128)(2,1)S(1)}, u32[]{:S(2)}, u32[]{:S(2)}) %collective-permute-start.3) | collective-permute-done | bytes 278560 | tf_op jit(solution)/shard_map/ppermute | solution.py:81
  11.7 2.9 %collective-permute-done.4.refs_4_ = bf16[17,16,512]{2,1,0:T(8,128)(2,1)S(1)} collective-permute-done((bf16[17,16,512]{2,1,0:T(8,128)(2,1)S(1)}, bf16[17,16,512]{2,1,0:T(8,128)(2,1)S(1)}, u32[]{:S(2)}, u32[]{:S(2)}) %collective-permute-start.4) | collective-permute-done | bytes 278560 | tf_op jit(solution)/shard_map/ppermute | solution.py:81
  14.6 4.4 %collective-permute-done.5.refs_5_ = bf16[17,16,512]{2,1,0:T(8,128)(2,1)S(1)} collective-permute-done((bf16[17,16,512]{2,1,0:T(8,128)(2,1)S(1)}, bf16[17,16,512]{2,1,0:T(8,128)(2,1)S(1)}, u32[]{:S(2)}, u32[]{:S(2)}) %collective-permute-start.5) | collective-permute-done | bytes 278560 | tf_op jit(solution)/shard_map/ppermute | solution.py:81
  18.9 2.8 %shard_map.88 = (f32[416,512]{1,0:T(8,128)S(1)}, f32[416,512]{1,0:T(8,128)}, s32[8,128]{1,0:T(8,128)}, bf16[64,256]{1,0:T(8,128)(2,1)}, f32[64,256]{1,0:T(8,128)}, /*index=5*/f32[64,256]{1,0:T(8,128)}) custom-call(s32[1]{0:T(128)} %bitcast.2.near_ref, s32[1]{0:T(128)} %bitcast.3.top_ref, s32[1]{0:T(128)} %bitcast.4.cls_ref, ...), custom_call_target="tpu_custom_call" | custom-call | bytes 9000000 | tf_op jit(solution)/shard_map/pallas_call | solution.py:464
  21.9 1.3 %shard_map.86 = (bf16[16,16,512]{2,1,0:T(8,128)(2,1)S(1)}, bf16[16,16,512]{2,1,0:T(8,128)(2,1)S(1)}, bf16[16,16,512]{2,1,0:T(8,128)(2,1)S(1)}) custom-call(s32[1]{0:T(128)} %bitcast.2.near_ref, s32[1]{0:T(128)} %bitcast.3.top_ref, bf16[16,2,4,16,512]{4,3,2,1,0:T(8,128)(2,1)} %bitcast.43), custom_call_target="tpu_custom_call" | custom-call | bytes 5400000 | tf_op jit(solution)/shard_map/pallas_call | solution.py:317
  23.2 1.7 %collective-permute-start = (bf16[16,16,512]{2,1,0:T(8,128)(2,1)S(1)}, bf16[16,16,512]{2,1,0:T(8,128)(2,1)S(1)}, u32[]{:S(2)}, u32[]{:S(2)}) collective-permute-start(bf16[16,16,512]{2,1,0:T(8,128)(2,1)S(1)} %get-tuple-element.29), channel_id=1, source_target_pairs={{0,4},{4,0},{8,12},{12,8},{16,20},{20,16},{24,28},{28,24},{1,5},{5... | collective-permute-start | bytes 786440 | tf_op jit(solution)/shard_map/ppermute | solution.py:81
  25.0 1.6 %collective-permute-start.1 = (bf16[16,16,512]{2,1,0:T(8,128)(2,1)S(1)}, bf16[16,16,512]{2,1,0:T(8,128)(2,1)S(1)}, u32[]{:S(2)}, u32[]{:S(2)}) collective-permute-start(bf16[16,16,512]{2,1,0:T(8,128)(2,1)S(1)} %get-tuple-element.30), channel_id=1, source_target_pairs={{0,8},{4,12},{8,0},{12,4},{16,24},{20,28},{24,16},{28,20},{1,9},{5... | collective-permute-start | bytes 786440 | tf_op jit(solution)/shard_map/ppermute | solution.py:81
  26.8 5.2 %collective-permute-done.refs_2_ = bf16[16,16,512]{2,1,0:T(8,128)(2,1)S(1)} collective-permute-done((bf16[16,16,512]{2,1,0:T(8,128)(2,1)S(1)}, bf16[16,16,512]{2,1,0:T(8,128)(2,1)S(1)}, u32[]{:S(2)}, u32[]{:S(2)}) %collective-permute-start) | collective-permute-done | bytes 262176 | tf_op jit(solution)/shard_map/ppermute | solution.py:81
  31.9 2.2 %collective-permute-done.1.refs_3_ = bf16[16,16,512]{2,1,0:T(8,128)(2,1)S(1)} collective-permute-done((bf16[16,16,512]{2,1,0:T(8,128)(2,1)S(1)}, bf16[16,16,512]{2,1,0:T(8,128)(2,1)S(1)}, u32[]{:S(2)}, u32[]{:S(2)}) %collective-permute-start.1) | collective-permute-done | bytes 262176 | tf_op jit(solution)/shard_map/ppermute | solution.py:81
  34.1 4.6 %collective-permute-done.2.refs_4_ = bf16[16,16,512]{2,1,0:T(8,128)(2,1)S(1)} collective-permute-done((bf16[16,16,512]{2,1,0:T(8,128)(2,1)S(1)}, bf16[16,16,512]{2,1,0:T(8,128)(2,1)S(1)}, u32[]{:S(2)}, u32[]{:S(2)}) %collective-permute-start.2) | collective-permute-done | bytes 262176 | tf_op jit(solution)/shard_map/ppermute | solution.py:81
  38.8 2.3 %shard_map.89 = (f32[384,512]{1,0:T(8,128)S(1)}, f32[384,512]{1,0:T(8,128)}) custom-call(s32[1]{0:T(128)} %bitcast.2.near_ref, s32[1]{0:T(128)} %bitcast.3.top_ref, s32[1]{0:T(128)} %bitcast.4.cls_ref, f32[1,128]{1,0:T(1,128)S(1)} %bitcast.37, bf16[16,2,4,16,512]{4,3,2,1,0:T(8,128)(2,1)} %bitcast.44, bf16[16,16,512]{2,1,0:T(8,128)(2,1)S(1)} %collective-permute-done.refs_2_, ...), custom_call_target="tpu_custom_call" | custom-call | bytes 9000000 | tf_op jit(solution)/shard_map/pallas_call | solution.py:464
  41.2 1.8 %collective-permute-start.11 = (bf16[12,32,512]{2,1,0:T(8,128)(2,1)S(1)}, bf16[12,32,512]{2,1,0:T(8,128)(2,1)S(1)}, u32[]{:S(2)}, u32[]{:S(2)}) collective-permute-start(bf16[12,32,512]{2,1,0:T(8,128)(2,1)S(1)} %copy-done), channel_id=1, source_target_pairs={{0,2},{1,3},{2,0},{3,1},{4,6},{5,7},{6,4},{7,5},{8,10},{9,11},{10,... | collective-permute-start | bytes 1179656 | tf_op jit(solution)/shard_map/ppermute | solution.py:81
  43.6 9.7 %collective-permute-done.11 = bf16[12,32,512]{2,1,0:T(8,128)(2,1)S(1)} collective-permute-done((bf16[12,32,512]{2,1,0:T(8,128)(2,1)S(1)}, bf16[12,32,512]{2,1,0:T(8,128)(2,1)S(1)}, u32[]{:S(2)}, u32[]{:S(2)}) %collective-permute-start.11) | collective-permute-done | bytes 393248 | tf_op jit(solution)/shard_map/ppermute | solution.py:81
  53.3 1.4 %shard_map.90 = (f32[1,192,512]{2,1,0:T(8,128)S(1)}, s16[1,208,512]{2,1,0:T(8,128)(2,1)S(1)}) custom-call(s32[1]{0:T(128)} %bitcast.1.bit_ref, f32[2,192,512]{2,1,0:T(8,128)S(1)} %bitcast.29, f32[2,192,512]{2,1,0:T(8,128)} %bitcast.11.get_ref), custom_call_target="tpu_custom_call" | custom-call | bytes 5400000 | tf_op jit(solution)/shard_map/pallas_call | solution.py:557
  54.6 1.8 %collective-permute-start.7 = (s16[1,208,512]{2,1,0:T(8,128)(2,1)S(1)}, s16[1,208,512]{2,1,0:T(8,128)(2,1)S(1)}, u32[]{:S(2)}, u32[]{:S(2)}) collective-permute-start(s16[1,208,512]{2,1,0:T(8,128)(2,1)S(1)} %get-tuple-element.43), channel_id=1, source_target_pairs={{0,2},{1,3},{2,0},{3,1},{4,6},{5,7},{6,4},{7,5},{8,10},{9,11},{10,... | collective-permute-start | bytes 638984 | tf_op jit(solution)/shard_map/ppermute | solution.py:81
  57.6 2.8 %collective-permute-start.10 = (s16[208,512]{1,0:T(8,128)(2,1)S(1)}, s16[208,512]{1,0:T(8,128)(2,1)S(1)}, u32[]{:S(2)}, u32[]{:S(2)}) collective-permute-start(s16[208,512]{1,0:T(8,128)(2,1)S(1)} %get-tuple-element.49), channel_id=1, source_target_pairs={{0,16},{4,20},{8,24},{12,28},{16,0},{20,4},{24,8},{28,12},{1,17},{... | collective-permute-start | bytes 638984 | tf_op jit(solution)/shard_map/ppermute | solution.py:81
  60.4 1.1 %table.1 = (bf16[512,512]{1,0:T(8,128)(2,1)S(1)}, bf16[16,32,512]{2,1,0:T(8,128)(2,1)S(1)}) custom-call(bf16[16,128,512]{2,1,0:T(8,128)(2,1)} %image_ref.1), custom_call_target="tpu_custom_call" | custom-call | bytes 7200000 | tf_op jit(solution)/shard_map/table/pallas_call | solution.py:56
  61.5 3.8 %shard_map.92 = (f32[8,128]{1,0:T(8,128)S(1)}, f32[8,128]{1,0:T(8,128)S(1)}) custom-call(bf16[16,32,512]{2,1,0:T(8,128)(2,1)S(1)} %get-tuple-element.50.low_ref, bf16[16,128]{1,0:T(8,128)(2,1)S(1)} %copy-done.1, f32[1,128]{1,0:T(1,128)S(1)} %bitcast.38, bf16[384,512]{1,0:T(8,128)(2,1)S(1)} %bitcast.23, bf16[384,512]{1,0:T(8,128)(2,1)S(1)} %bitcast.25, ...), custom_call_target="tpu_custom_call" | custom-call | bytes 14400000 | tf_op jit(solution)/shard_map/pallas_call | solution.py:216
  65.4 3.8 %shard_map.93 = (f32[8,128]{1,0:T(8,128)S(1)}, f32[8,128]{1,0:T(8,128)S(1)}) custom-call(bf16[16,32,512]{2,1,0:T(8,128)(2,1)S(1)} %get-tuple-element.50.low_ref, bf16[16,128]{1,0:T(8,128)(2,1)S(1)} %copy-done.1, f32[1,128]{1,0:T(1,128)S(1)} %bitcast.39, bf16[384,512]{1,0:T(8,128)(2,1)S(1)} %bitcast.24, bf16[384,512]{1,0:T(8,128)(2,1)S(1)} %bitcast.26, ...), custom_call_target="tpu_custom_call" | custom-call | bytes 14400000 | tf_op jit(solution)/shard_map/pallas_call | solution.py:216
  69.3 7.5 %shard_map.94 = f32[1,16]{1,0:T(1,128)} custom-call(bf16[16,32,512]{2,1,0:T(8,128)(2,1)S(1)} %get-tuple-element.50.low_ref, bf16[16,128]{1,0:T(8,128)(2,1)S(1)} %copy-done.1, f32[1,128]{1,0:T(1,128)S(1)} %bitcast.40, bf16[384,512]{1,0:T(8,128)(2,1)S(1)} %bitcast.31, bf16[384,512]{1,0:T(8,128)(2,1)S(1)} %bitcast.33, ...), custom_call_target="tpu_custom_call" | custom-call | bytes 28800000 | tf_op jit(solution)/shard_map/pallas_call | solution.py:216
  76.8 1.0 %finish.1 = f32[12,16,512]{2,1,0:T(8,128)} custom-call(s32[1]{0:T(128)} %bitcast.dom_ref, f32[192,512]{1,0:T(8,128)S(1)} %bitcast.32, s16[208,512]{1,0:T(8,128)(2,1)S(1)} %bitcast.35, f32[16,128]{1,0:T(8,128)S(1)} %get-tuple-element.48.power_ref, s16[208,512]{1,0:T(8,128)(2,1)S(1)} %collective-permute-done.10.came_ref), custom_call_target="tpu_custom_call" | custom-call | bytes 3600000 | tf_op jit(solution)/shard_map/finish/pallas_call | solution.py:607
  (30 shorter events, 2.3 us)
Async XLA Ops:
  0.6 18.3 %copy-start.5 = (f32[128]{0:T(128)S(1)}, f32[128]{0:T(128)}, u32[]{:S(2)}) copy-start(f32[128]{0:T(128)} %param.9) | copy-start | bytes 1540
  2.0 9.7 %collective-permute-start.3 = (bf16[17,16,512]{2,1,0:T(8,128)(2,1)S(1)}, bf16[17,16,512]{2,1,0:T(8,128)(2,1)S(1)}, u32[]{:S(2)}, u32[]{:S(2)}) collective-permute-start(bf16[17,16,512]{2,1,0:T(8,128)(2,1)S(1)} %get-tuple-element.33), channel_id=1, source_target_pairs={{0,4},{4,0},{8,12},{12,8},{16,20},{20,16},{24,28},{28,24},{1,5},{5... | collective-permute-start | bytes 835592 | tf_op jit(solution)/shard_map/ppermute | solution.py:81
  5.0 9.5 %collective-permute-start.4 = (bf16[17,16,512]{2,1,0:T(8,128)(2,1)S(1)}, bf16[17,16,512]{2,1,0:T(8,128)(2,1)S(1)}, u32[]{:S(2)}, u32[]{:S(2)}) collective-permute-start(bf16[17,16,512]{2,1,0:T(8,128)(2,1)S(1)} %get-tuple-element.34), channel_id=1, source_target_pairs={{0,8},{4,12},{8,0},{12,4},{16,24},{20,28},{24,16},{28,20},{1,9},{5... | collective-permute-start | bytes 835592 | tf_op jit(solution)/shard_map/ppermute | solution.py:81
  6.6 12.3 %collective-permute-start.5 = (bf16[17,16,512]{2,1,0:T(8,128)(2,1)S(1)}, bf16[17,16,512]{2,1,0:T(8,128)(2,1)S(1)}, u32[]{:S(2)}, u32[]{:S(2)}) collective-permute-start(bf16[17,16,512]{2,1,0:T(8,128)(2,1)S(1)} %get-tuple-element.35), channel_id=1, source_target_pairs={{0,12},{4,8},{8,4},{12,0},{16,28},{20,24},{24,20},{28,16},{1,13},{... | collective-permute-start | bytes 835592 | tf_op jit(solution)/shard_map/ppermute | solution.py:81
  21.8 17.0 %copy-start.2 = (f32[64,256]{1,0:T(8,128)S(1)}, f32[64,256]{1,0:T(8,128)}, u32[]{:S(2)}) copy-start(f32[64,256]{1,0:T(8,128)} %get-tuple-element.38.refs_7_) | copy-start | bytes 196612
  21.8 17.0 %copy-start.3 = (f32[64,256]{1,0:T(8,128)S(1)}, f32[64,256]{1,0:T(8,128)}, u32[]{:S(2)}) copy-start(f32[64,256]{1,0:T(8,128)} %get-tuple-element.39.refs_8_) | copy-start | bytes 196612
  21.8 17.0 %copy-start.4 = (bf16[64,256]{1,0:T(8,128)(2,1)S(1)}, bf16[64,256]{1,0:T(8,128)(2,1)}, u32[]{:S(2)}) copy-start(bf16[64,256]{1,0:T(8,128)(2,1)} %get-tuple-element.37.refs_6_) | copy-start | bytes 98308
  21.8 17.0 %copy-start.6 = (s32[8,128]{1,0:T(8,128)S(1)}, s32[8,128]{1,0:T(8,128)}, u32[]{:S(2)}) copy-start(s32[8,128]{1,0:T(8,128)} %get-tuple-element.36.refs_5_) | copy-start | bytes 12292
  21.8 19.4 %copy-start = (bf16[12,32,512]{2,1,0:T(8,128)(2,1)S(1)}, bf16[12,32,512]{2,1,0:T(8,128)(2,1)}, u32[]{:S(2)}) copy-start(bf16[12,32,512]{2,1,0:T(8,128)(2,1)} %param.10) | copy-start | bytes 1179652
  21.8 21.1 %collective-permute-start.8 = (f32[416,512]{1,0:T(8,128)}, f32[416,512]{1,0:T(8,128)S(1)}, u32[]{:S(2)}, u32[]{:S(2)}) collective-permute-start(f32[416,512]{1,0:T(8,128)} %get-tuple-element.45), channel_id=1, source_target_pairs={{0,1},{1,0},{2,3},{3,2},{4,5},{5,4},{6,7},{7,6},{8,9},{9,8},{10,11... | collective-permute-start | bytes 2555912 | tf_op jit(solution)/shard_map/ppermute | solution.py:81
  23.2 8.7 %collective-permute-start = (bf16[16,16,512]{2,1,0:T(8,128)(2,1)S(1)}, bf16[16,16,512]{2,1,0:T(8,128)(2,1)S(1)}, u32[]{:S(2)}, u32[]{:S(2)}) collective-permute-start(bf16[16,16,512]{2,1,0:T(8,128)(2,1)S(1)} %get-tuple-element.29), channel_id=1, source_target_pairs={{0,4},{4,0},{8,12},{12,8},{16,20},{20,16},{24,28},{28,24},{1,5},{5... | collective-permute-start | bytes 786440 | tf_op jit(solution)/shard_map/ppermute | solution.py:81
  25.0 9.2 %collective-permute-start.1 = (bf16[16,16,512]{2,1,0:T(8,128)(2,1)S(1)}, bf16[16,16,512]{2,1,0:T(8,128)(2,1)S(1)}, u32[]{:S(2)}, u32[]{:S(2)}) collective-permute-start(bf16[16,16,512]{2,1,0:T(8,128)(2,1)S(1)} %get-tuple-element.30), channel_id=1, source_target_pairs={{0,8},{4,12},{8,0},{12,4},{16,24},{20,28},{24,16},{28,20},{1,9},{5... | collective-permute-start | bytes 786440 | tf_op jit(solution)/shard_map/ppermute | solution.py:81
  26.5 12.2 %collective-permute-start.2 = (bf16[16,16,512]{2,1,0:T(8,128)(2,1)S(1)}, bf16[16,16,512]{2,1,0:T(8,128)(2,1)S(1)}, u32[]{:S(2)}, u32[]{:S(2)}) collective-permute-start(bf16[16,16,512]{2,1,0:T(8,128)(2,1)S(1)} %get-tuple-element.31), channel_id=1, source_target_pairs={{0,12},{4,8},{8,4},{12,0},{16,28},{20,24},{24,20},{28,16},{1,13},{... | collective-permute-start | bytes 786440 | tf_op jit(solution)/shard_map/ppermute | solution.py:81
  41.1 12.1 %collective-permute-start.6 = (f32[384,512]{1,0:T(8,128)}, f32[384,512]{1,0:T(8,128)}, u32[]{:S(2)}, u32[]{:S(2)}) collective-permute-start(f32[384,512]{1,0:T(8,128)} %get-tuple-element.41), channel_id=1, source_target_pairs={{0,1},{1,0},{2,3},{3,2},{4,5},{5,4},{6,7},{7,6},{8,9},{9,8},{10,11... | collective-permute-start | bytes 2359304 | tf_op jit(solution)/shard_map/ppermute | solution.py:81
  41.2 12.1 %collective-permute-start.11 = (bf16[12,32,512]{2,1,0:T(8,128)(2,1)S(1)}, bf16[12,32,512]{2,1,0:T(8,128)(2,1)S(1)}, u32[]{:S(2)}, u32[]{:S(2)}) collective-permute-start(bf16[12,32,512]{2,1,0:T(8,128)(2,1)S(1)} %copy-done), channel_id=1, source_target_pairs={{0,2},{1,3},{2,0},{3,1},{4,6},{5,7},{6,4},{7,5},{8,10},{9,11},{10,... | collective-permute-start | bytes 1179656 | tf_op jit(solution)/shard_map/ppermute | solution.py:81
  43.2 14.1 %collective-permute-start.9 = (s16[1,208,512]{2,1,0:T(8,128)(2,1)S(1)}, s16[1,208,512]{2,1,0:T(8,128)(2,1)S(1)}, u32[]{:S(2)}, u32[]{:S(2)}) collective-permute-start(s16[1,208,512]{2,1,0:T(8,128)(2,1)S(1)} %get-tuple-element.47), channel_id=1, source_target_pairs={{0,2},{1,3},{2,0},{3,1},{4,6},{5,7},{6,4},{7,5},{8,10},{9,11},{10,... | collective-permute-start | bytes 638984 | tf_op jit(solution)/shard_map/ppermute | solution.py:81
  43.6 17.9 %collective-permute-start.13 = (bf16[12,32,512]{2,1,0:T(8,128)(2,1)S(1)}, bf16[12,32,512]{2,1,0:T(8,128)(2,1)S(1)}, u32[]{:S(2)}, u32[]{:S(2)}) collective-permute-start(bf16[12,32,512]{2,1,0:T(8,128)(2,1)S(1)} %copy-done), channel_id=1, source_target_pairs={{0,1},{1,0},{2,3},{3,2},{4,5},{5,4},{6,7},{7,6},{8,9},{9,8},{10,11... | collective-permute-start | bytes 1179656 | tf_op jit(solution)/shard_map/ppermute | solution.py:81
  53.3 16.0 %collective-permute-start.12 = (bf16[12,32,512]{2,1,0:T(8,128)(2,1)S(1)}, bf16[12,32,512]{2,1,0:T(8,128)(2,1)S(1)}, u32[]{:S(2)}, u32[]{:S(2)}) collective-permute-start(bf16[12,32,512]{2,1,0:T(8,128)(2,1)S(1)} %collective-permute-done.11), channel_id=1, source_target_pairs={{0,1},{1,0},{2,3},{3,2},{4,5},{5,4},{6,7},{7,6},{8,9},{9,8},{10,11... | collective-permute-start | bytes 1179656 | tf_op jit(solution)/shard_map/ppermute | solution.py:81
  53.3 8.3 %copy-start.1 = (bf16[16,128]{1,0:T(8,128)(2,1)S(1)}, bf16[16,128]{1,0:T(8,128)(2,1)}, u32[]{:S(2)}) copy-start(bf16[16,128]{1,0:T(8,128)(2,1)} %ctf_ref.5) | copy-start | bytes 12292
  54.6 22.1 %collective-permute-start.7 = (s16[1,208,512]{2,1,0:T(8,128)(2,1)S(1)}, s16[1,208,512]{2,1,0:T(8,128)(2,1)S(1)}, u32[]{:S(2)}, u32[]{:S(2)}) collective-permute-start(s16[1,208,512]{2,1,0:T(8,128)(2,1)S(1)} %get-tuple-element.43), channel_id=1, source_target_pairs={{0,2},{1,3},{2,0},{3,1},{4,6},{5,7},{6,4},{7,5},{8,10},{9,11},{10,... | collective-permute-start | bytes 638984 | tf_op jit(solution)/shard_map/ppermute | solution.py:81
  57.6 19.2 %collective-permute-start.10 = (s16[208,512]{1,0:T(8,128)(2,1)S(1)}, s16[208,512]{1,0:T(8,128)(2,1)S(1)}, u32[]{:S(2)}, u32[]{:S(2)}) collective-permute-start(s16[208,512]{1,0:T(8,128)(2,1)S(1)} %get-tuple-element.49), channel_id=1, source_target_pairs={{0,16},{4,20},{8,24},{12,28},{16,0},{20,4},{24,8},{28,12},{1,17},{... | collective-permute-start | bytes 638984 | tf_op jit(solution)/shard_map/ppermute | solution.py:81

commit v3 on v2

--- a/solution.py
+++ b/solution.py
@@ -251,7 +251,7 @@
 
 
 def pieces_kernel(near_ref, top_ref, view_ref, *refs, chunk):
-    outs, sems = refs[-GROUP:-1], refs[-1]
+    outs, sems = refs[:-1], refs[-1]
     if chunk == 0:
         ctf_ref, owner_ref, sub_ref, turn_ref, meta_ref = refs[:5]
         outs = refs[5 : 5 + GROUP - 1]
@@ -266,9 +266,10 @@
             fetch.start()
     count = view_ref.shape[2] if view_ref.shape[0] == 2 else view_ref.shape[0]
     part = count // SPLITS
+    first = 1 if chunk == 0 else 0
     copies = [
         pltpu.make_async_copy(
-            part_of(view_ref, top_ref[0] ^ (1 - chunk), near_ref[0] ^ (i + 1)).at[
+            part_of(view_ref, top_ref[0] ^ (1 - chunk), near_ref[0] ^ (i + first)).at[
                 pl.ds(j * part, part)
             ],
             out.at[pl.ds(j * part, part)],
@@ -302,11 +303,15 @@
 def pieces(near, top, view, chunk, others):
     count, width = view.shape[2] if view.shape[0] == 2 else view.shape[0], view.shape[-1]
     out = pltpu.VMEM((count + (chunk == 0), PAD, width), view.dtype)
-    shapes = [out] * (GROUP - 1)
-    scratch = [pltpu.SemaphoreType.DMA(((GROUP - 1) * SPLITS,))]
+    shapes, specs = [out] * (GROUP - 1), [HERE] * (GROUP - 1)
+    scratch = [pltpu.SemaphoreType.DMA((GROUP * SPLITS,))]
+    if chunk == 1:
+        shapes = [pltpu.HBM((count, PAD, width), view.dtype)] + shapes
+        specs = [THERE] + specs
     if chunk == 0:
         ctf = others[0]
         shapes = [pltpu.VMEM((count, 2 * ctf.shape[1]), view.dtype)] + shapes
+        specs = [HERE] + specs
         scratch = [
             pltpu.VMEM(ctf.shape, ctf.dtype),
             pltpu.VMEM((1, count), jnp.int32),
@@ -318,7 +323,7 @@
         functools.partial(pieces_kernel, chunk=chunk),
         out_shape=shapes,
         in_specs=[SCALARS] * 2 + [THERE] * (1 + len(others)),
-        out_specs=[HERE] * len(shapes),
+        out_specs=specs,
         scratch_shapes=scratch,
         cost_estimate=cost(1.5),
         compiler_params=room(((count * PAD, width), 2 * GROUP)),
@@ -337,8 +342,8 @@
         shared, refs = refs[2:6], refs[6:]
         total, own, powers, plan, metas, cos_ref, sin_ref, place_ref, sems = refs
     else:
-        plan, metas, cos_ref, sin_ref = refs[:4]
-        keep_ref, give_ref, total, own, place_ref, sems = refs[4:]
+        plan, metas, cos_ref, sin_ref, own = refs[:5]
+        keep_ref, give_ref, total, place_ref, sems = refs[5:]
     cycles, half = PAD, cos_ref.shape[1]
     side = top_ref[0] ^ (1 - chunk)
     particles = cos_ref.shape[0]
@@ -352,7 +357,7 @@
             own.at[pl.ds(i * part, part)],
             sems.at[5 + i],
         )
-        for i in range(SPLITS)
+        for i in range(SPLITS if chunk == 0 else 0)
     ]
     for fetch in fetches:
         fetch.start()
@@ -453,11 +458,9 @@
         ((particles, width // 2), jnp.float32),
     ]
     shapes = [out, out] + ([pltpu.HBM(shape, dtype) for shape, dtype in kinds] if first else [])
-    scratch = [
-        pltpu.VMEM((2 * rows, width), jnp.float32),
-        pltpu.VMEM((count, PAD, width), view.dtype),
-    ]
+    scratch = [pltpu.VMEM((2 * rows, width), jnp.float32)]
     if first:
+        scratch += [pltpu.VMEM((count, PAD, width), view.dtype)]
         scratch += [pltpu.VMEM((shards * PAD, LANES), jnp.float32)]
         scratch += [pltpu.VMEM(shape, dtype) for shape, dtype in kinds]
     ins = [meta] if first else []
@@ -643,7 +646,8 @@
         view = view.transpose(1, 3, 0, 2, 4, 5).reshape(2, GROUP, count, PAD, width)
     rows_of = [v.reshape(1, count) for v in (owner, sub_class, rotation)]
     meta, *sent_0 = pieces(near, top, view, 0, (ctf, *rows_of))
-    sent = (sent_0, pieces(near, top, view, 1, ()))
+    own_1, *sent_1 = pieces(near, top, view, 1, ())
+    sent = (sent_0, sent_1)
     got = [[swap(sent[c][m - 1], "dom", m) for m in range(1, GROUP)] for c in range(CHUNKS)]
 
     held, mask = references, 2
@@ -671,7 +675,7 @@
             scalars, view, chunk, got[chunk], meta, noise, shared, slice_cycles, far,
             shards // 2 * size, shards,
         )
-        shared = more
+        shared = [*more, own_1]
         get = swap(give, "cls", 1)
         shape = (shards // 2, size, width)
         keep, get = keep.reshape(shape), get.reshape(shape)

time: 78 us -> 86.8 us (1.11)
  Pallas kernels: 27 us -> 34.8 us
  local copies, waits for them, and re-layouts: 0.03 us -> 0.98 us
    pallas_call x2, Pallas kernels: 2.65 us -> 10.6 us  [pieces(): pl.pallas_call(functools.partial(pieces_kernel, chunk=chunk), out_shape=s...]
    unnamed x14 -> x16, local copies, waits for them, and re-layouts: 0.03 us -> 0.98 us
  transfers between devices with their start and end apart: 14 -> 14, of which waited for: 8 -> 8; matrix products, arithmetic and copies ran while one was open for 0% -> 0% of each run, Pallas kernels for 28% -> 34%
where the time goes in v3:
time: 86.8 us; the launch traced here: 86.6 us
  waiting for transfers between devices  34.9 us (40%)
  Pallas kernels  34.8 us (40%)
  starting transfers between devices  15 us (17%)
  local copies, waits for them, and re-layouts  0.98 us (1%)
    ppermute x14, waiting for transfers between devices, swap(): return lax.ppermute(value, axis, [(i, i ^ mask) for i in range(size)])  34.9 us
    pallas_call x3, Pallas kernels, score(): pl.pallas_call(functools.partial(score_kernel, merge=merge, start=start),...  15.2 us
    ppermute x14, starting transfers between devices, swap(): return lax.ppermute(value, axis, [(i, i ^ mask) for i in range(size)])  15 us
    pallas_call x2, Pallas kernels, pieces(): pl.pallas_call(functools.partial(pieces_kernel, chunk=chunk), out_shape=s...  10.6 us
    pallas_call x2, Pallas kernels, class_sums(): pl.pallas_call(functools.partial(sums_kernel, slice_cycles=slice_cycles,...  5.07 us
  transfers between devices with their start and end apart: 14, of which 8 were waited for; matrix products, arithmetic and copies ran while one was open for 0% of the time, Pallas kernels for 34%

profile of v3, /device:TPU:0, one launch (start us, length us, event | category | flops | bytes accessed | tf_op | source)
XLA Modules:
  0.0 86.6 jit_solution(8440914346826924059)
XLA Ops:
  0.7 1.4 %shard_map.87 = (bf16[16,256]{1,0:T(8,128)(2,1)S(1)}, bf16[17,16,512]{2,1,0:T(8,128)(2,1)S(1)}, bf16[17,16,512]{2,1,0:T(8,128)(2,1)S(1)}, bf16[17,16,512]{2,1,0:T(8,128)(2,1)S(1)}) custom-call(s32[1]{0:T(128)} %bitcast.2.near_ref, s32[1]{0:T(128)} %bitcast.3.top_ref, bf16[16,2,4,16,512]{4,3,2,1,0:T(8,128)(2,1)} %bitcast.41, bf16[16,128]{1,0:T(8,128)(2,1)} %ctf_ref.5, ...), custom_call_target="tpu_custom_call" | custom-call | bytes 5400000 | tf_op jit(solution)/shard_map/pallas_call | solution.py:322
  2.0 3.0 %collective-permute-start.3 = (bf16[17,16,512]{2,1,0:T(8,128)(2,1)S(1)}, bf16[17,16,512]{2,1,0:T(8,128)(2,1)S(1)}, u32[]{:S(2)}, u32[]{:S(2)}) collective-permute-start(bf16[17,16,512]{2,1,0:T(8,128)(2,1)S(1)} %get-tuple-element.34), channel_id=1, source_target_pairs={{0,4},{4,0},{8,12},{12,8},{16,20},{20,16},{24,28},{28,24},{1,5},{5... | collective-permute-start | bytes 835592 | tf_op jit(solution)/shard_map/ppermute | solution.py:81
  5.1 1.6 %collective-permute-start.4 = (bf16[17,16,512]{2,1,0:T(8,128)(2,1)S(1)}, bf16[17,16,512]{2,1,0:T(8,128)(2,1)S(1)}, u32[]{:S(2)}, u32[]{:S(2)}) collective-permute-start(bf16[17,16,512]{2,1,0:T(8,128)(2,1)S(1)} %get-tuple-element.35), channel_id=1, source_target_pairs={{0,8},{4,12},{8,0},{12,4},{16,24},{20,28},{24,16},{28,20},{1,9},{5... | collective-permute-start | bytes 835592 | tf_op jit(solution)/shard_map/ppermute | solution.py:81
  6.6 5.1 %collective-permute-done.3.refs_3_ = bf16[17,16,512]{2,1,0:T(8,128)(2,1)S(1)} collective-permute-done((bf16[17,16,512]{2,1,0:T(8,128)(2,1)S(1)}, bf16[17,16,512]{2,1,0:T(8,128)(2,1)S(1)}, u32[]{:S(2)}, u32[]{:S(2)}) %collective-permute-start.3) | collective-permute-done | bytes 278560 | tf_op jit(solution)/shard_map/ppermute | solution.py:81
  11.7 2.9 %collective-permute-done.4.refs_4_ = bf16[17,16,512]{2,1,0:T(8,128)(2,1)S(1)} collective-permute-done((bf16[17,16,512]{2,1,0:T(8,128)(2,1)S(1)}, bf16[17,16,512]{2,1,0:T(8,128)(2,1)S(1)}, u32[]{:S(2)}, u32[]{:S(2)}) %collective-permute-start.4) | collective-permute-done | bytes 278560 | tf_op jit(solution)/shard_map/ppermute | solution.py:81
  14.6 4.4 %collective-permute-done.5.refs_5_ = bf16[17,16,512]{2,1,0:T(8,128)(2,1)S(1)} collective-permute-done((bf16[17,16,512]{2,1,0:T(8,128)(2,1)S(1)}, bf16[17,16,512]{2,1,0:T(8,128)(2,1)S(1)}, u32[]{:S(2)}, u32[]{:S(2)}) %collective-permute-start.5) | collective-permute-done | bytes 278560 | tf_op jit(solution)/shard_map/ppermute | solution.py:81
  19.0 2.8 %shard_map.88 = (f32[416,512]{1,0:T(8,128)S(1)}, f32[416,512]{1,0:T(8,128)}, s32[8,128]{1,0:T(8,128)}, bf16[64,256]{1,0:T(8,128)(2,1)}, f32[64,256]{1,0:T(8,128)}, /*index=5*/f32[64,256]{1,0:T(8,128)}) custom-call(s32[1]{0:T(128)} %bitcast.2.near_ref, s32[1]{0:T(128)} %bitcast.3.top_ref, s32[1]{0:T(128)} %bitcast.4.cls_ref, ...), custom_call_target="tpu_custom_call" | custom-call | bytes 9000000 | tf_op jit(solution)/shard_map/pallas_call | solution.py:467
  21.9 9.2 %shard_map.86 = (bf16[16,16,512]{2,1,0:T(8,128)(2,1)}, bf16[16,16,512]{2,1,0:T(8,128)(2,1)S(1)}, bf16[16,16,512]{2,1,0:T(8,128)(2,1)S(1)}, bf16[16,16,512]{2,1,0:T(8,128)(2,1)S(1)}) custom-call(s32[1]{0:T(128)} %bitcast.2.near_ref, s32[1]{0:T(128)} %bitcast.3.top_ref, bf16[16,2,4,16,512]{4,3,2,1,0:T(8,128)(2,1)} %bitcast.43), custom_call_target="tpu_custom_call" | custom-call | bytes 5400000 | tf_op jit(solution)/shard_map/pallas_call | solution.py:322
  31.1 1.7 %collective-permute-start = (bf16[16,16,512]{2,1,0:T(8,128)(2,1)S(1)}, bf16[16,16,512]{2,1,0:T(8,128)(2,1)S(1)}, u32[]{:S(2)}, u32[]{:S(2)}) collective-permute-start(bf16[16,16,512]{2,1,0:T(8,128)(2,1)S(1)} %get-tuple-element.30), channel_id=1, source_target_pairs={{0,4},{4,0},{8,12},{12,8},{16,20},{20,16},{24,28},{28,24},{1,5},{5... | collective-permute-start | bytes 786440 | tf_op jit(solution)/shard_map/ppermute | solution.py:81
  32.9 1.6 %collective-permute-start.1 = (bf16[16,16,512]{2,1,0:T(8,128)(2,1)S(1)}, bf16[16,16,512]{2,1,0:T(8,128)(2,1)S(1)}, u32[]{:S(2)}, u32[]{:S(2)}) collective-permute-start(bf16[16,16,512]{2,1,0:T(8,128)(2,1)S(1)} %get-tuple-element.31), channel_id=1, source_target_pairs={{0,8},{4,12},{8,0},{12,4},{16,24},{20,28},{24,16},{28,20},{1,9},{5... | collective-permute-start | bytes 786440 | tf_op jit(solution)/shard_map/ppermute | solution.py:81
  34.7 5.2 %collective-permute-done.refs_2_ = bf16[16,16,512]{2,1,0:T(8,128)(2,1)S(1)} collective-permute-done((bf16[16,16,512]{2,1,0:T(8,128)(2,1)S(1)}, bf16[16,16,512]{2,1,0:T(8,128)(2,1)S(1)}, u32[]{:S(2)}, u32[]{:S(2)}) %collective-permute-start) | collective-permute-done | bytes 262176 | tf_op jit(solution)/shard_map/ppermute | solution.py:81
  39.9 2.1 %collective-permute-done.1.refs_3_ = bf16[16,16,512]{2,1,0:T(8,128)(2,1)S(1)} collective-permute-done((bf16[16,16,512]{2,1,0:T(8,128)(2,1)S(1)}, bf16[16,16,512]{2,1,0:T(8,128)(2,1)S(1)}, u32[]{:S(2)}, u32[]{:S(2)}) %collective-permute-start.1) | collective-permute-done | bytes 262176 | tf_op jit(solution)/shard_map/ppermute | solution.py:81
  42.0 4.7 %collective-permute-done.2.refs_4_ = bf16[16,16,512]{2,1,0:T(8,128)(2,1)S(1)} collective-permute-done((bf16[16,16,512]{2,1,0:T(8,128)(2,1)S(1)}, bf16[16,16,512]{2,1,0:T(8,128)(2,1)S(1)}, u32[]{:S(2)}, u32[]{:S(2)}) %collective-permute-start.2) | collective-permute-done | bytes 262176 | tf_op jit(solution)/shard_map/ppermute | solution.py:81
  47.7 2.2 %shard_map.89 = (f32[384,512]{1,0:T(8,128)S(1)}, f32[384,512]{1,0:T(8,128)}) custom-call(s32[1]{0:T(128)} %bitcast.2.near_ref, s32[1]{0:T(128)} %bitcast.3.top_ref, s32[1]{0:T(128)} %bitcast.4.cls_ref, f32[1,128]{1,0:T(1,128)S(1)} %bitcast.37, bf16[16,2,4,16,512]{4,3,2,1,0:T(8,128)(2,1)} %bitcast.44, bf16[16,16,512]{2,1,0:T(8,128)(2,1)S(1)} %collective-permute-done.refs_2_, ...), custom_call_target="tpu_custom_call" | custom-call | bytes 9000000 | tf_op jit(solution)/shard_map/pallas_call | solution.py:467
  50.0 1.8 %collective-permute-start.11 = (bf16[12,32,512]{2,1,0:T(8,128)(2,1)S(1)}, bf16[12,32,512]{2,1,0:T(8,128)(2,1)S(1)}, u32[]{:S(2)}, u32[]{:S(2)}) collective-permute-start(bf16[12,32,512]{2,1,0:T(8,128)(2,1)S(1)} %copy-done), channel_id=1, source_target_pairs={{0,2},{1,3},{2,0},{3,1},{4,6},{5,7},{6,4},{7,5},{8,10},{9,11},{10,... | collective-permute-start | bytes 1179656 | tf_op jit(solution)/shard_map/ppermute | solution.py:81
  52.4 9.7 %collective-permute-done.11 = bf16[12,32,512]{2,1,0:T(8,128)(2,1)S(1)} collective-permute-done((bf16[12,32,512]{2,1,0:T(8,128)(2,1)S(1)}, bf16[12,32,512]{2,1,0:T(8,128)(2,1)S(1)}, u32[]{:S(2)}, u32[]{:S(2)}) %collective-permute-start.11) | collective-permute-done | bytes 393248 | tf_op jit(solution)/shard_map/ppermute | solution.py:81
  62.1 1.4 %shard_map.90 = (f32[1,192,512]{2,1,0:T(8,128)S(1)}, s16[1,208,512]{2,1,0:T(8,128)(2,1)S(1)}) custom-call(s32[1]{0:T(128)} %bitcast.1.bit_ref, f32[2,192,512]{2,1,0:T(8,128)S(1)} %bitcast.29, f32[2,192,512]{2,1,0:T(8,128)} %bitcast.11.get_ref), custom_call_target="tpu_custom_call" | custom-call | bytes 5400000 | tf_op jit(solution)/shard_map/pallas_call | solution.py:560
  63.5 1.8 %collective-permute-start.7 = (s16[1,208,512]{2,1,0:T(8,128)(2,1)S(1)}, s16[1,208,512]{2,1,0:T(8,128)(2,1)S(1)}, u32[]{:S(2)}, u32[]{:S(2)}) collective-permute-start(s16[1,208,512]{2,1,0:T(8,128)(2,1)S(1)} %get-tuple-element.45), channel_id=1, source_target_pairs={{0,2},{1,3},{2,0},{3,1},{4,6},{5,7},{6,4},{7,5},{8,10},{9,11},{10,... | collective-permute-start | bytes 638984 | tf_op jit(solution)/shard_map/ppermute | solution.py:81
  66.4 2.8 %collective-permute-start.10 = (s16[208,512]{1,0:T(8,128)(2,1)S(1)}, s16[208,512]{1,0:T(8,128)(2,1)S(1)}, u32[]{:S(2)}, u32[]{:S(2)}) collective-permute-start(s16[208,512]{1,0:T(8,128)(2,1)S(1)} %get-tuple-element.51), channel_id=1, source_target_pairs={{0,16},{4,20},{8,24},{12,28},{16,0},{20,4},{24,8},{28,12},{1,17},{... | collective-permute-start | bytes 638984 | tf_op jit(solution)/shard_map/ppermute | solution.py:81
  69.2 1.1 %table.1 = (bf16[512,512]{1,0:T(8,128)(2,1)S(1)}, bf16[16,32,512]{2,1,0:T(8,128)(2,1)S(1)}) custom-call(bf16[16,128,512]{2,1,0:T(8,128)(2,1)} %image_ref.1), custom_call_target="tpu_custom_call" | custom-call | bytes 7200000 | tf_op jit(solution)/shard_map/table/pallas_call | solution.py:56
  70.4 3.8 %shard_map.92 = (f32[8,128]{1,0:T(8,128)S(1)}, f32[8,128]{1,0:T(8,128)S(1)}) custom-call(bf16[16,32,512]{2,1,0:T(8,128)(2,1)S(1)} %get-tuple-element.52.low_ref, bf16[16,128]{1,0:T(8,128)(2,1)S(1)} %copy-done.2, f32[1,128]{1,0:T(1,128)S(1)} %bitcast.38, bf16[384,512]{1,0:T(8,128)(2,1)S(1)} %bitcast.23, bf16[384,512]{1,0:T(8,128)(2,1)S(1)} %bitcast.25, ...), custom_call_target="tpu_custom_call" | custom-call | bytes 14400000 | tf_op jit(solution)/shard_map/pallas_call | solution.py:216
  74.2 3.8 %shard_map.93 = (f32[8,128]{1,0:T(8,128)S(1)}, f32[8,128]{1,0:T(8,128)S(1)}) custom-call(bf16[16,32,512]{2,1,0:T(8,128)(2,1)S(1)} %get-tuple-element.52.low_ref, bf16[16,128]{1,0:T(8,128)(2,1)S(1)} %copy-done.2, f32[1,128]{1,0:T(1,128)S(1)} %bitcast.39, bf16[384,512]{1,0:T(8,128)(2,1)S(1)} %bitcast.24, bf16[384,512]{1,0:T(8,128)(2,1)S(1)} %bitcast.26, ...), custom_call_target="tpu_custom_call" | custom-call | bytes 14400000 | tf_op jit(solution)/shard_map/pallas_call | solution.py:216
  78.1 7.5 %shard_map.94 = f32[1,16]{1,0:T(1,128)} custom-call(bf16[16,32,512]{2,1,0:T(8,128)(2,1)S(1)} %get-tuple-element.52.low_ref, bf16[16,128]{1,0:T(8,128)(2,1)S(1)} %copy-done.2, f32[1,128]{1,0:T(1,128)S(1)} %bitcast.40, bf16[384,512]{1,0:T(8,128)(2,1)S(1)} %bitcast.31, bf16[384,512]{1,0:T(8,128)(2,1)S(1)} %bitcast.33, ...), custom_call_target="tpu_custom_call" | custom-call | bytes 28800000 | tf_op jit(solution)/shard_map/pallas_call | solution.py:216
  85.6 1.0 %finish.1 = f32[12,16,512]{2,1,0:T(8,128)} custom-call(s32[1]{0:T(128)} %bitcast.dom_ref, f32[192,512]{1,0:T(8,128)S(1)} %bitcast.32, s16[208,512]{1,0:T(8,128)(2,1)S(1)} %bitcast.35, f32[16,128]{1,0:T(8,128)S(1)} %get-tuple-element.50.power_ref, s16[208,512]{1,0:T(8,128)(2,1)S(1)} %collective-permute-done.10.came_ref), custom_call_target="tpu_custom_call" | custom-call | bytes 3600000 | tf_op jit(solution)/shard_map/finish/pallas_call | solution.py:610
  (32 shorter events, 3.2 us)
Async XLA Ops:
  0.6 18.3 %copy-start.6 = (f32[128]{0:T(128)S(1)}, f32[128]{0:T(128)}, u32[]{:S(2)}) copy-start(f32[128]{0:T(128)} %param.9) | copy-start | bytes 1540
  2.0 9.7 %collective-permute-start.3 = (bf16[17,16,512]{2,1,0:T(8,128)(2,1)S(1)}, bf16[17,16,512]{2,1,0:T(8,128)(2,1)S(1)}, u32[]{:S(2)}, u32[]{:S(2)}) collective-permute-start(bf16[17,16,512]{2,1,0:T(8,128)(2,1)S(1)} %get-tuple-element.34), channel_id=1, source_target_pairs={{0,4},{4,0},{8,12},{12,8},{16,20},{20,16},{24,28},{28,24},{1,5},{5... | collective-permute-start | bytes 835592 | tf_op jit(solution)/shard_map/ppermute | solution.py:81
  5.1 9.5 %collective-permute-start.4 = (bf16[17,16,512]{2,1,0:T(8,128)(2,1)S(1)}, bf16[17,16,512]{2,1,0:T(8,128)(2,1)S(1)}, u32[]{:S(2)}, u32[]{:S(2)}) collective-permute-start(bf16[17,16,512]{2,1,0:T(8,128)(2,1)S(1)} %get-tuple-element.35), channel_id=1, source_target_pairs={{0,8},{4,12},{8,0},{12,4},{16,24},{20,28},{24,16},{28,20},{1,9},{5... | collective-permute-start | bytes 835592 | tf_op jit(solution)/shard_map/ppermute | solution.py:81
  6.6 12.3 %collective-permute-start.5 = (bf16[17,16,512]{2,1,0:T(8,128)(2,1)S(1)}, bf16[17,16,512]{2,1,0:T(8,128)(2,1)S(1)}, u32[]{:S(2)}, u32[]{:S(2)}) collective-permute-start(bf16[17,16,512]{2,1,0:T(8,128)(2,1)S(1)} %get-tuple-element.36), channel_id=1, source_target_pairs={{0,12},{4,8},{8,4},{12,0},{16,28},{20,24},{24,20},{28,16},{1,13},{... | collective-permute-start | bytes 835592 | tf_op jit(solution)/shard_map/ppermute | solution.py:81
  21.8 24.9 %copy-start.3 = (f32[64,256]{1,0:T(8,128)S(1)}, f32[64,256]{1,0:T(8,128)}, u32[]{:S(2)}) copy-start(f32[64,256]{1,0:T(8,128)} %get-tuple-element.39.refs_7_) | copy-start | bytes 196612
  21.8 24.9 %copy-start.4 = (f32[64,256]{1,0:T(8,128)S(1)}, f32[64,256]{1,0:T(8,128)}, u32[]{:S(2)}) copy-start(f32[64,256]{1,0:T(8,128)} %get-tuple-element.40.refs_8_) | copy-start | bytes 196612
  21.8 24.9 %copy-start.5 = (bf16[64,256]{1,0:T(8,128)(2,1)S(1)}, bf16[64,256]{1,0:T(8,128)(2,1)}, u32[]{:S(2)}) copy-start(bf16[64,256]{1,0:T(8,128)(2,1)} %get-tuple-element.38.refs_6_) | copy-start | bytes 98308
  21.8 24.9 %copy-start.7 = (s32[8,128]{1,0:T(8,128)S(1)}, s32[8,128]{1,0:T(8,128)}, u32[]{:S(2)}) copy-start(s32[8,128]{1,0:T(8,128)} %get-tuple-element.37.refs_5_) | copy-start | bytes 12292
  21.8 29.9 %collective-permute-start.8 = (f32[416,512]{1,0:T(8,128)}, f32[416,512]{1,0:T(8,128)S(1)}, u32[]{:S(2)}, u32[]{:S(2)}) collective-permute-start(f32[416,512]{1,0:T(8,128)} %get-tuple-element.47), channel_id=1, source_target_pairs={{0,1},{1,0},{2,3},{3,2},{4,5},{5,4},{6,7},{7,6},{8,9},{9,8},{10,11... | collective-permute-start | bytes 2555912 | tf_op jit(solution)/shard_map/ppermute | solution.py:81
  31.1 18.9 %copy-start = (bf16[12,32,512]{2,1,0:T(8,128)(2,1)S(1)}, bf16[12,32,512]{2,1,0:T(8,128)(2,1)}, u32[]{:S(2)}) copy-start(bf16[12,32,512]{2,1,0:T(8,128)(2,1)} %param.10) | copy-start | bytes 1179652
  31.1 8.8 %collective-permute-start = (bf16[16,16,512]{2,1,0:T(8,128)(2,1)S(1)}, bf16[16,16,512]{2,1,0:T(8,128)(2,1)S(1)}, u32[]{:S(2)}, u32[]{:S(2)}) collective-permute-start(bf16[16,16,512]{2,1,0:T(8,128)(2,1)S(1)} %get-tuple-element.30), channel_id=1, source_target_pairs={{0,4},{4,0},{8,12},{12,8},{16,20},{20,16},{24,28},{28,24},{1,5},{5... | collective-permute-start | bytes 786440 | tf_op jit(solution)/shard_map/ppermute | solution.py:81
  32.9 9.2 %collective-permute-start.1 = (bf16[16,16,512]{2,1,0:T(8,128)(2,1)S(1)}, bf16[16,16,512]{2,1,0:T(8,128)(2,1)S(1)}, u32[]{:S(2)}, u32[]{:S(2)}) collective-permute-start(bf16[16,16,512]{2,1,0:T(8,128)(2,1)S(1)} %get-tuple-element.31), channel_id=1, source_target_pairs={{0,8},{4,12},{8,0},{12,4},{16,24},{20,28},{24,16},{28,20},{1,9},{5... | collective-permute-start | bytes 786440 | tf_op jit(solution)/shard_map/ppermute | solution.py:81
  34.4 12.3 %collective-permute-start.2 = (bf16[16,16,512]{2,1,0:T(8,128)(2,1)S(1)}, bf16[16,16,512]{2,1,0:T(8,128)(2,1)S(1)}, u32[]{:S(2)}, u32[]{:S(2)}) collective-permute-start(bf16[16,16,512]{2,1,0:T(8,128)(2,1)S(1)} %get-tuple-element.32), channel_id=1, source_target_pairs={{0,12},{4,8},{8,4},{12,0},{16,28},{20,24},{24,20},{28,16},{1,13},{... | collective-permute-start | bytes 786440 | tf_op jit(solution)/shard_map/ppermute | solution.py:81
  46.7 1.0 %copy-start.1 = (bf16[16,16,512]{2,1,0:T(8,128)(2,1)S(1)}, bf16[16,16,512]{2,1,0:T(8,128)(2,1)}, u32[]{:S(2)}) copy-start(bf16[16,16,512]{2,1,0:T(8,128)(2,1)} %get-tuple-element.41.refs_9_) | copy-start | bytes 786436
  49.9 12.1 %collective-permute-start.6 = (f32[384,512]{1,0:T(8,128)}, f32[384,512]{1,0:T(8,128)}, u32[]{:S(2)}, u32[]{:S(2)}) collective-permute-start(f32[384,512]{1,0:T(8,128)} %get-tuple-element.43), channel_id=1, source_target_pairs={{0,1},{1,0},{2,3},{3,2},{4,5},{5,4},{6,7},{7,6},{8,9},{9,8},{10,11... | collective-permute-start | bytes 2359304 | tf_op jit(solution)/shard_map/ppermute | solution.py:81
  50.0 12.1 %collective-permute-start.11 = (bf16[12,32,512]{2,1,0:T(8,128)(2,1)S(1)}, bf16[12,32,512]{2,1,0:T(8,128)(2,1)S(1)}, u32[]{:S(2)}, u32[]{:S(2)}) collective-permute-start(bf16[12,32,512]{2,1,0:T(8,128)(2,1)S(1)} %copy-done), channel_id=1, source_target_pairs={{0,2},{1,3},{2,0},{3,1},{4,6},{5,7},{6,4},{7,5},{8,10},{9,11},{10,... | collective-permute-start | bytes 1179656 | tf_op jit(solution)/shard_map/ppermute | solution.py:81
  52.0 14.1 %collective-permute-start.9 = (s16[1,208,512]{2,1,0:T(8,128)(2,1)S(1)}, s16[1,208,512]{2,1,0:T(8,128)(2,1)S(1)}, u32[]{:S(2)}, u32[]{:S(2)}) collective-permute-start(s16[1,208,512]{2,1,0:T(8,128)(2,1)S(1)} %get-tuple-element.49), channel_id=1, source_target_pairs={{0,2},{1,3},{2,0},{3,1},{4,6},{5,7},{6,4},{7,5},{8,10},{9,11},{10,... | collective-permute-start | bytes 638984 | tf_op jit(solution)/shard_map/ppermute | solution.py:81
  52.4 17.9 %collective-permute-start.13 = (bf16[12,32,512]{2,1,0:T(8,128)(2,1)S(1)}, bf16[12,32,512]{2,1,0:T(8,128)(2,1)S(1)}, u32[]{:S(2)}, u32[]{:S(2)}) collective-permute-start(bf16[12,32,512]{2,1,0:T(8,128)(2,1)S(1)} %copy-done), channel_id=1, source_target_pairs={{0,1},{1,0},{2,3},{3,2},{4,5},{5,4},{6,7},{7,6},{8,9},{9,8},{10,11... | collective-permute-start | bytes 1179656 | tf_op jit(solution)/shard_map/ppermute | solution.py:81
  62.1 16.0 %collective-permute-start.12 = (bf16[12,32,512]{2,1,0:T(8,128)(2,1)S(1)}, bf16[12,32,512]{2,1,0:T(8,128)(2,1)S(1)}, u32[]{:S(2)}, u32[]{:S(2)}) collective-permute-start(bf16[12,32,512]{2,1,0:T(8,128)(2,1)S(1)} %collective-permute-done.11), channel_id=1, source_target_pairs={{0,1},{1,0},{2,3},{3,2},{4,5},{5,4},{6,7},{7,6},{8,9},{9,8},{10,11... | collective-permute-start | bytes 1179656 | tf_op jit(solution)/shard_map/ppermute | solution.py:81
  62.1 8.3 %copy-start.2 = (bf16[16,128]{1,0:T(8,128)(2,1)S(1)}, bf16[16,128]{1,0:T(8,128)(2,1)}, u32[]{:S(2)}) copy-start(bf16[16,128]{1,0:T(8,128)(2,1)} %ctf_ref.5) | copy-start | bytes 12292
  63.5 22.1 %collective-permute-start.7 = (s16[1,208,512]{2,1,0:T(8,128)(2,1)S(1)}, s16[1,208,512]{2,1,0:T(8,128)(2,1)S(1)}, u32[]{:S(2)}, u32[]{:S(2)}) collective-permute-start(s16[1,208,512]{2,1,0:T(8,128)(2,1)S(1)} %get-tuple-element.45), channel_id=1, source_target_pairs={{0,2},{1,3},{2,0},{3,1},{4,6},{5,7},{6,4},{7,5},{8,10},{9,11},{10,... | collective-permute-start | bytes 638984 | tf_op jit(solution)/shard_map/ppermute | solution.py:81
  66.4 19.2 %collective-permute-start.10 = (s16[208,512]{1,0:T(8,128)(2,1)S(1)}, s16[208,512]{1,0:T(8,128)(2,1)S(1)}, u32[]{:S(2)}, u32[]{:S(2)}) collective-permute-start(s16[208,512]{1,0:T(8,128)(2,1)S(1)} %get-tuple-element.51), channel_id=1, source_target_pairs={{0,16},{4,20},{8,24},{12,28},{16,0},{20,4},{24,8},{28,12},{1,17},{... | collective-permute-start | bytes 638984 | tf_op jit(solution)/shard_map/ppermute | solution.py:81

commit v4 on v2

--- a/solution.py
+++ b/solution.py
@@ -104,7 +104,19 @@
 ):
     before, refs = refs[:merge], refs[merge:]
     outs, refs = refs[: 1 if merge else 2], refs[1 if merge else 2 :]
-    image, image_sum, staged, classes, cross = refs
+    image, image_sum, staged, classes, cross = refs[:5]
+    copies = []
+    if merge:
+        there, first_ref, sems = first_ref, refs[5], refs[6]
+        part = there.shape[0] // SPLITS
+        copies = [
+            pltpu.make_async_copy(
+                there.at[pl.ds(i * part, part)], first_ref.at[pl.ds(i * part, part)], sems.at[i]
+            )
+            for i in range(SPLITS)
+        ]
+    for copy in copies:
+        copy.start()
     _, cycles, width = low_ref.shape
     tiles = width // LANES
     pairs = tiles // 2
@@ -115,6 +127,19 @@
     weight = ctf / noise_ref[...]
     power = ctf * weight
     eye = iota((cycles, LANES), 0) == iota((cycles, LANES), 1)
+    for n in range(count):
+        row = jnp.broadcast_to(weight[n : n + 1, :], (cycles, LANES))
+        column = jnp.sum(jnp.where(eye, row, 0.0), axis=1, keepdims=True)
+        low = low_ref[start + n].astype(jnp.float32)
+        weighted = (column * low).astype(jnp.bfloat16).astype(jnp.float32)
+        for f in range(tiles):
+            image[f, n * cycles : (n + 1) * cycles, :] = weighted[:, f * LANES : (f + 1) * LANES]
+        for f in range(pairs):
+            re = weighted[:, f * LANES : (f + 1) * LANES]
+            im = weighted[:, (f + pairs) * LANES : (f + pairs + 1) * LANES]
+            image_sum[f, n * cycles : (n + 1) * cycles, :] = re + im
+    for copy in copies:
+        copy.wait()
     for at, ref in ((0, first_ref), (part, second_ref)):
         for f in range(tiles):
             staged[f, at : at + part, :] = ref[:, f * LANES : (f + 1) * LANES].astype(jnp.float32)
@@ -136,17 +161,6 @@
             total = jnp.sum(square[r], axis=1, keepdims=True)
             norm = jnp.where(iota((8, LANES), 1) == r, total, norm)
         norms.append(norm)
-    for n in range(count):
-        row = jnp.broadcast_to(weight[n : n + 1, :], (cycles, LANES))
-        column = jnp.sum(jnp.where(eye, row, 0.0), axis=1, keepdims=True)
-        low = low_ref[start + n].astype(jnp.float32)
-        weighted = (column * low).astype(jnp.bfloat16).astype(jnp.float32)
-        for f in range(tiles):
-            image[f, n * cycles : (n + 1) * cycles, :] = weighted[:, f * LANES : (f + 1) * LANES]
-        for f in range(pairs):
-            re = weighted[:, f * LANES : (f + 1) * LANES]
-            im = weighted[:, (f + pairs) * LANES : (f + pairs + 1) * LANES]
-            image_sum[f, n * cycles : (n + 1) * cycles, :] = re + im
     group = 2
     for f in range(pairs):
 
@@ -216,7 +230,7 @@
     return pl.pallas_call(
         functools.partial(score_kernel, merge=merge, start=start),
         out_shape=row if merge else (each, each),
-        in_specs=[HERE] * (6 + merge),
+        in_specs=[HERE] * 3 + [THERE if merge else HERE] + [HERE] * (2 + merge),
         out_specs=HERE if merge else (HERE, HERE),
         scratch_shapes=[
             pltpu.VMEM((width // LANES, count * cycles, LANES), jnp.float32),
@@ -224,7 +238,8 @@
             pltpu.VMEM((width // LANES, kinds * cycles, LANES), jnp.float32),
             pltpu.VMEM((width // LANES // 2 * 3, cycles, kinds, LANES), jnp.float32),
             pltpu.VMEM((count * kinds, width), jnp.float32),
-        ],
+        ]
+        + ([pltpu.VMEM(part, first.dtype), pltpu.SemaphoreType.DMA((SPLITS,))] if merge else []),
         cost_estimate=cost(count / 2),
         compiler_params=room(
             ((count * cycles, width), 8),
@@ -233,7 +248,8 @@
             (table.shape, 2),
         ),
     )(
-        *held_near(low), ctf, noise, *held_near(first.reshape(part), second.reshape(part), table),
+        *held_near(low), ctf, noise, *(held_far if merge else held_near)(first.reshape(part)),
+        *held_near(second.reshape(part), table),
         *before,
     )
 

time: 78 us -> 79.1 us (1.014)
  Pallas kernels: 27 us -> 28.2 us
    pallas_call x3, Pallas kernels: 15.2 us -> 16.3 us  [score(): pl.pallas_call(functools.partial(score_kernel, merge=merge, start=start),...]
  transfers between devices with their start and end apart: 14 -> 14, of which waited for: 8 -> 8; matrix products, arithmetic and copies ran while one was open for 0% -> 0% of each run, Pallas kernels for 28% -> 29%
where the time goes in v4:
time: 79.1 us; the launch traced here: 78.8 us
  waiting for transfers between devices  34.7 us (44%)
  Pallas kernels  28.2 us (36%)
  starting transfers between devices  15 us (19%)
  between operations  0.88 us (1%)
    ppermute x14, waiting for transfers between devices, swap(): return lax.ppermute(value, axis, [(i, i ^ mask) for i in range(size)])  34.7 us
    pallas_call x3, Pallas kernels, score(): pl.pallas_call(functools.partial(score_kernel, merge=merge, start=start),...  16.3 us
    ppermute x14, starting transfers between devices, swap(): return lax.ppermute(value, axis, [(i, i ^ mask) for i in range(size)])  15 us
    pallas_call x2, Pallas kernels, class_sums(): pl.pallas_call(functools.partial(sums_kernel, slice_cycles=slice_cycles,...  5.16 us
    pallas_call x2, Pallas kernels, pieces(): pl.pallas_call(functools.partial(pieces_kernel, chunk=chunk), out_shape=s...  2.65 us
    pallas_call x2, Pallas kernels, split_shards(): pl.pallas_call(functools.partial(shard_kernel, was_coded=get.dtype == jnp...  1.73 us
  transfers between devices with their start and end apart: 14, of which 8 were waited for; matrix products, arithmetic and copies ran while one was open for 0% of the time, Pallas kernels for 29%

profile of v4, /device:TPU:0, one launch (start us, length us, event | category | flops | bytes accessed | tf_op | source)
XLA Modules:
  0.0 78.8 jit_solution(2836443216777624554)
XLA Ops:
  0.7 1.3 %shard_map.87 = (bf16[16,256]{1,0:T(8,128)(2,1)S(1)}, bf16[17,16,512]{2,1,0:T(8,128)(2,1)S(1)}, bf16[17,16,512]{2,1,0:T(8,128)(2,1)S(1)}, bf16[17,16,512]{2,1,0:T(8,128)(2,1)S(1)}) custom-call(s32[1]{0:T(128)} %bitcast.2.near_ref, s32[1]{0:T(128)} %bitcast.3.top_ref, bf16[16,2,4,16,512]{4,3,2,1,0:T(8,128)(2,1)} %bitcast.40, bf16[16,128]{1,0:T(8,128)(2,1)} %ctf_ref.5, ...), custom_call_target="tpu_custom_call" | custom-call | bytes 5400000 | tf_op jit(solution)/shard_map/pallas_call | solution.py:333
  2.0 3.0 %collective-permute-start.3 = (bf16[17,16,512]{2,1,0:T(8,128)(2,1)S(1)}, bf16[17,16,512]{2,1,0:T(8,128)(2,1)S(1)}, u32[]{:S(2)}, u32[]{:S(2)}) collective-permute-start(bf16[17,16,512]{2,1,0:T(8,128)(2,1)S(1)} %get-tuple-element.33), channel_id=1, source_target_pairs={{0,4},{4,0},{8,12},{12,8},{16,20},{20,16},{24,28},{28,24},{1,5},{5... | collective-permute-start | bytes 835592 | tf_op jit(solution)/shard_map/ppermute | solution.py:81
  5.0 1.6 %collective-permute-start.4 = (bf16[17,16,512]{2,1,0:T(8,128)(2,1)S(1)}, bf16[17,16,512]{2,1,0:T(8,128)(2,1)S(1)}, u32[]{:S(2)}, u32[]{:S(2)}) collective-permute-start(bf16[17,16,512]{2,1,0:T(8,128)(2,1)S(1)} %get-tuple-element.34), channel_id=1, source_target_pairs={{0,8},{4,12},{8,0},{12,4},{16,24},{20,28},{24,16},{28,20},{1,9},{5... | collective-permute-start | bytes 835592 | tf_op jit(solution)/shard_map/ppermute | solution.py:81
  6.6 5.1 %collective-permute-done.3.refs_3_ = bf16[17,16,512]{2,1,0:T(8,128)(2,1)S(1)} collective-permute-done((bf16[17,16,512]{2,1,0:T(8,128)(2,1)S(1)}, bf16[17,16,512]{2,1,0:T(8,128)(2,1)S(1)}, u32[]{:S(2)}, u32[]{:S(2)}) %collective-permute-start.3) | collective-permute-done | bytes 278560 | tf_op jit(solution)/shard_map/ppermute | solution.py:81
  11.7 2.9 %collective-permute-done.4.refs_4_ = bf16[17,16,512]{2,1,0:T(8,128)(2,1)S(1)} collective-permute-done((bf16[17,16,512]{2,1,0:T(8,128)(2,1)S(1)}, bf16[17,16,512]{2,1,0:T(8,128)(2,1)S(1)}, u32[]{:S(2)}, u32[]{:S(2)}) %collective-permute-start.4) | collective-permute-done | bytes 278560 | tf_op jit(solution)/shard_map/ppermute | solution.py:81
  14.6 4.4 %collective-permute-done.5.refs_5_ = bf16[17,16,512]{2,1,0:T(8,128)(2,1)S(1)} collective-permute-done((bf16[17,16,512]{2,1,0:T(8,128)(2,1)S(1)}, bf16[17,16,512]{2,1,0:T(8,128)(2,1)S(1)}, u32[]{:S(2)}, u32[]{:S(2)}) %collective-permute-start.5) | collective-permute-done | bytes 278560 | tf_op jit(solution)/shard_map/ppermute | solution.py:81
  18.9 2.8 %shard_map.88 = (f32[416,512]{1,0:T(8,128)S(1)}, f32[416,512]{1,0:T(8,128)}, s32[8,128]{1,0:T(8,128)}, bf16[64,256]{1,0:T(8,128)(2,1)}, f32[64,256]{1,0:T(8,128)}, /*index=5*/f32[64,256]{1,0:T(8,128)}) custom-call(s32[1]{0:T(128)} %bitcast.2.near_ref, s32[1]{0:T(128)} %bitcast.3.top_ref, s32[1]{0:T(128)} %bitcast.4.cls_ref, ...), custom_call_target="tpu_custom_call" | custom-call | bytes 9000000 | tf_op jit(solution)/shard_map/pallas_call | solution.py:480
  21.9 1.3 %shard_map.86 = (bf16[16,16,512]{2,1,0:T(8,128)(2,1)S(1)}, bf16[16,16,512]{2,1,0:T(8,128)(2,1)S(1)}, bf16[16,16,512]{2,1,0:T(8,128)(2,1)S(1)}) custom-call(s32[1]{0:T(128)} %bitcast.2.near_ref, s32[1]{0:T(128)} %bitcast.3.top_ref, bf16[16,2,4,16,512]{4,3,2,1,0:T(8,128)(2,1)} %bitcast.42), custom_call_target="tpu_custom_call" | custom-call | bytes 5400000 | tf_op jit(solution)/shard_map/pallas_call | solution.py:333
  23.2 1.7 %collective-permute-start = (bf16[16,16,512]{2,1,0:T(8,128)(2,1)S(1)}, bf16[16,16,512]{2,1,0:T(8,128)(2,1)S(1)}, u32[]{:S(2)}, u32[]{:S(2)}) collective-permute-start(bf16[16,16,512]{2,1,0:T(8,128)(2,1)S(1)} %get-tuple-element.29), channel_id=1, source_target_pairs={{0,4},{4,0},{8,12},{12,8},{16,20},{20,16},{24,28},{28,24},{1,5},{5... | collective-permute-start | bytes 786440 | tf_op jit(solution)/shard_map/ppermute | solution.py:81
  25.0 1.6 %collective-permute-start.1 = (bf16[16,16,512]{2,1,0:T(8,128)(2,1)S(1)}, bf16[16,16,512]{2,1,0:T(8,128)(2,1)S(1)}, u32[]{:S(2)}, u32[]{:S(2)}) collective-permute-start(bf16[16,16,512]{2,1,0:T(8,128)(2,1)S(1)} %get-tuple-element.30), channel_id=1, source_target_pairs={{0,8},{4,12},{8,0},{12,4},{16,24},{20,28},{24,16},{28,20},{1,9},{5... | collective-permute-start | bytes 786440 | tf_op jit(solution)/shard_map/ppermute | solution.py:81
  26.8 5.2 %collective-permute-done.refs_2_ = bf16[16,16,512]{2,1,0:T(8,128)(2,1)S(1)} collective-permute-done((bf16[16,16,512]{2,1,0:T(8,128)(2,1)S(1)}, bf16[16,16,512]{2,1,0:T(8,128)(2,1)S(1)}, u32[]{:S(2)}, u32[]{:S(2)}) %collective-permute-start) | collective-permute-done | bytes 262176 | tf_op jit(solution)/shard_map/ppermute | solution.py:81
  31.9 2.2 %collective-permute-done.1.refs_3_ = bf16[16,16,512]{2,1,0:T(8,128)(2,1)S(1)} collective-permute-done((bf16[16,16,512]{2,1,0:T(8,128)(2,1)S(1)}, bf16[16,16,512]{2,1,0:T(8,128)(2,1)S(1)}, u32[]{:S(2)}, u32[]{:S(2)}) %collective-permute-start.1) | collective-permute-done | bytes 262176 | tf_op jit(solution)/shard_map/ppermute | solution.py:81
  34.1 4.6 %collective-permute-done.2.refs_4_ = bf16[16,16,512]{2,1,0:T(8,128)(2,1)S(1)} collective-permute-done((bf16[16,16,512]{2,1,0:T(8,128)(2,1)S(1)}, bf16[16,16,512]{2,1,0:T(8,128)(2,1)S(1)}, u32[]{:S(2)}, u32[]{:S(2)}) %collective-permute-start.2) | collective-permute-done | bytes 262176 | tf_op jit(solution)/shard_map/ppermute | solution.py:81
  38.8 2.3 %shard_map.89 = (f32[384,512]{1,0:T(8,128)S(1)}, f32[384,512]{1,0:T(8,128)}) custom-call(s32[1]{0:T(128)} %bitcast.2.near_ref, s32[1]{0:T(128)} %bitcast.3.top_ref, s32[1]{0:T(128)} %bitcast.4.cls_ref, f32[1,128]{1,0:T(1,128)S(1)} %bitcast.36, bf16[16,2,4,16,512]{4,3,2,1,0:T(8,128)(2,1)} %bitcast.43, bf16[16,16,512]{2,1,0:T(8,128)(2,1)S(1)} %collective-permute-done.refs_2_, ...), custom_call_target="tpu_custom_call" | custom-call | bytes 9000000 | tf_op jit(solution)/shard_map/pallas_call | solution.py:480
  41.2 1.8 %collective-permute-start.11 = (bf16[12,32,512]{2,1,0:T(8,128)(2,1)S(1)}, bf16[12,32,512]{2,1,0:T(8,128)(2,1)S(1)}, u32[]{:S(2)}, u32[]{:S(2)}) collective-permute-start(bf16[12,32,512]{2,1,0:T(8,128)(2,1)S(1)} %copy-done), channel_id=1, source_target_pairs={{0,2},{1,3},{2,0},{3,1},{4,6},{5,7},{6,4},{7,5},{8,10},{9,11},{10,... | collective-permute-start | bytes 1179656 | tf_op jit(solution)/shard_map/ppermute | solution.py:81
  43.6 9.7 %collective-permute-done.11 = bf16[12,32,512]{2,1,0:T(8,128)(2,1)S(1)} collective-permute-done((bf16[12,32,512]{2,1,0:T(8,128)(2,1)S(1)}, bf16[12,32,512]{2,1,0:T(8,128)(2,1)S(1)}, u32[]{:S(2)}, u32[]{:S(2)}) %collective-permute-start.11) | collective-permute-done | bytes 393248 | tf_op jit(solution)/shard_map/ppermute | solution.py:81
  53.3 1.5 %shard_map.90 = (f32[1,192,512]{2,1,0:T(8,128)S(1)}, s16[1,208,512]{2,1,0:T(8,128)(2,1)S(1)}) custom-call(s32[1]{0:T(128)} %bitcast.1.bit_ref, f32[2,192,512]{2,1,0:T(8,128)S(1)} %bitcast.29, f32[2,192,512]{2,1,0:T(8,128)} %bitcast.11.get_ref), custom_call_target="tpu_custom_call" | custom-call | bytes 5400000 | tf_op jit(solution)/shard_map/pallas_call | solution.py:573
  54.8 1.8 %collective-permute-start.7 = (s16[1,208,512]{2,1,0:T(8,128)(2,1)S(1)}, s16[1,208,512]{2,1,0:T(8,128)(2,1)S(1)}, u32[]{:S(2)}, u32[]{:S(2)}) collective-permute-start(s16[1,208,512]{2,1,0:T(8,128)(2,1)S(1)} %get-tuple-element.43), channel_id=1, source_target_pairs={{0,2},{1,3},{2,0},{3,1},{4,6},{5,7},{6,4},{7,5},{8,10},{9,11},{10,... | collective-permute-start | bytes 638984 | tf_op jit(solution)/shard_map/ppermute | solution.py:81
  57.5 2.8 %collective-permute-start.10 = (s16[208,512]{1,0:T(8,128)(2,1)S(1)}, s16[208,512]{1,0:T(8,128)(2,1)S(1)}, u32[]{:S(2)}, u32[]{:S(2)}) collective-permute-start(s16[208,512]{1,0:T(8,128)(2,1)S(1)} %get-tuple-element.49), channel_id=1, source_target_pairs={{0,16},{4,20},{8,24},{12,28},{16,0},{20,4},{24,8},{28,12},{1,17},{... | collective-permute-start | bytes 638984 | tf_op jit(solution)/shard_map/ppermute | solution.py:81
  60.4 1.1 %table.1 = (bf16[512,512]{1,0:T(8,128)(2,1)S(1)}, bf16[16,32,512]{2,1,0:T(8,128)(2,1)S(1)}) custom-call(bf16[16,128,512]{2,1,0:T(8,128)(2,1)} %image_ref.1), custom_call_target="tpu_custom_call" | custom-call | bytes 7200000 | tf_op jit(solution)/shard_map/table/pallas_call | solution.py:56
  61.5 3.9 %shard_map.92 = (f32[8,128]{1,0:T(8,128)S(1)}, f32[8,128]{1,0:T(8,128)S(1)}) custom-call(bf16[16,32,512]{2,1,0:T(8,128)(2,1)S(1)} %get-tuple-element.50.low_ref, bf16[16,128]{1,0:T(8,128)(2,1)S(1)} %copy-done.1, f32[1,128]{1,0:T(1,128)S(1)} %bitcast.37, bf16[384,512]{1,0:T(8,128)(2,1)S(1)} %bitcast.23, bf16[384,512]{1,0:T(8,128)(2,1)S(1)} %bitcast.25, ...), custom_call_target="tpu_custom_call" | custom-call | bytes 14400000 | tf_op jit(solution)/shard_map/pallas_call | solution.py:230
  65.4 3.9 %shard_map.93 = (f32[8,128]{1,0:T(8,128)S(1)}, f32[8,128]{1,0:T(8,128)S(1)}) custom-call(bf16[16,32,512]{2,1,0:T(8,128)(2,1)S(1)} %get-tuple-element.50.low_ref, bf16[16,128]{1,0:T(8,128)(2,1)S(1)} %copy-done.1, f32[1,128]{1,0:T(1,128)S(1)} %bitcast.38, bf16[384,512]{1,0:T(8,128)(2,1)S(1)} %bitcast.24, bf16[384,512]{1,0:T(8,128)(2,1)S(1)} %bitcast.26, ...), custom_call_target="tpu_custom_call" | custom-call | bytes 14400000 | tf_op jit(solution)/shard_map/pallas_call | solution.py:230
  69.4 8.4 %shard_map.94 = f32[1,16]{1,0:T(1,128)} custom-call(bf16[16,32,512]{2,1,0:T(8,128)(2,1)S(1)} %get-tuple-element.50.low_ref, bf16[16,128]{1,0:T(8,128)(2,1)S(1)} %copy-done.1, f32[1,128]{1,0:T(1,128)S(1)} %bitcast.39, bf16[384,512]{1,0:T(8,128)(2,1)} %bitcast.44, bf16[384,512]{1,0:T(8,128)(2,1)S(1)} %bitcast.32, ...), custom_call_target="tpu_custom_call" | custom-call | bytes 28800000 | tf_op jit(solution)/shard_map/pallas_call | solution.py:230
  77.8 1.0 %finish.1 = f32[12,16,512]{2,1,0:T(8,128)} custom-call(s32[1]{0:T(128)} %bitcast.dom_ref, f32[192,512]{1,0:T(8,128)S(1)} %bitcast.31, s16[208,512]{1,0:T(8,128)(2,1)S(1)} %bitcast.34, f32[16,128]{1,0:T(8,128)S(1)} %get-tuple-element.48.power_ref, s16[208,512]{1,0:T(8,128)(2,1)S(1)} %collective-permute-done.10.came_ref), custom_call_target="tpu_custom_call" | custom-call | bytes 3600000 | tf_op jit(solution)/shard_map/finish/pallas_call | solution.py:623
  (32 shorter events, 2.1 us)
Async XLA Ops:
  0.6 18.3 %copy-start.5 = (f32[128]{0:T(128)S(1)}, f32[128]{0:T(128)}, u32[]{:S(2)}) copy-start(f32[128]{0:T(128)} %param.9) | copy-start | bytes 1540
  2.0 9.7 %collective-permute-start.3 = (bf16[17,16,512]{2,1,0:T(8,128)(2,1)S(1)}, bf16[17,16,512]{2,1,0:T(8,128)(2,1)S(1)}, u32[]{:S(2)}, u32[]{:S(2)}) collective-permute-start(bf16[17,16,512]{2,1,0:T(8,128)(2,1)S(1)} %get-tuple-element.33), channel_id=1, source_target_pairs={{0,4},{4,0},{8,12},{12,8},{16,20},{20,16},{24,28},{28,24},{1,5},{5... | collective-permute-start | bytes 835592 | tf_op jit(solution)/shard_map/ppermute | solution.py:81
  5.0 9.5 %collective-permute-start.4 = (bf16[17,16,512]{2,1,0:T(8,128)(2,1)S(1)}, bf16[17,16,512]{2,1,0:T(8,128)(2,1)S(1)}, u32[]{:S(2)}, u32[]{:S(2)}) collective-permute-start(bf16[17,16,512]{2,1,0:T(8,128)(2,1)S(1)} %get-tuple-element.34), channel_id=1, source_target_pairs={{0,8},{4,12},{8,0},{12,4},{16,24},{20,28},{24,16},{28,20},{1,9},{5... | collective-permute-start | bytes 835592 | tf_op jit(solution)/shard_map/ppermute | solution.py:81
  6.6 12.3 %collective-permute-start.5 = (bf16[17,16,512]{2,1,0:T(8,128)(2,1)S(1)}, bf16[17,16,512]{2,1,0:T(8,128)(2,1)S(1)}, u32[]{:S(2)}, u32[]{:S(2)}) collective-permute-start(bf16[17,16,512]{2,1,0:T(8,128)(2,1)S(1)} %get-tuple-element.35), channel_id=1, source_target_pairs={{0,12},{4,8},{8,4},{12,0},{16,28},{20,24},{24,20},{28,16},{1,13},{... | collective-permute-start | bytes 835592 | tf_op jit(solution)/shard_map/ppermute | solution.py:81
  21.8 17.0 %copy-start.2 = (f32[64,256]{1,0:T(8,128)S(1)}, f32[64,256]{1,0:T(8,128)}, u32[]{:S(2)}) copy-start(f32[64,256]{1,0:T(8,128)} %get-tuple-element.38.refs_7_) | copy-start | bytes 196612
  21.8 17.0 %copy-start.3 = (f32[64,256]{1,0:T(8,128)S(1)}, f32[64,256]{1,0:T(8,128)}, u32[]{:S(2)}) copy-start(f32[64,256]{1,0:T(8,128)} %get-tuple-element.39.refs_8_) | copy-start | bytes 196612
  21.8 17.0 %copy-start.4 = (bf16[64,256]{1,0:T(8,128)(2,1)S(1)}, bf16[64,256]{1,0:T(8,128)(2,1)}, u32[]{:S(2)}) copy-start(bf16[64,256]{1,0:T(8,128)(2,1)} %get-tuple-element.37.refs_6_) | copy-start | bytes 98308
  21.8 17.0 %copy-start.6 = (s32[8,128]{1,0:T(8,128)S(1)}, s32[8,128]{1,0:T(8,128)}, u32[]{:S(2)}) copy-start(s32[8,128]{1,0:T(8,128)} %get-tuple-element.36.refs_5_) | copy-start | bytes 12292
  21.8 19.4 %copy-start = (bf16[12,32,512]{2,1,0:T(8,128)(2,1)S(1)}, bf16[12,32,512]{2,1,0:T(8,128)(2,1)}, u32[]{:S(2)}) copy-start(bf16[12,32,512]{2,1,0:T(8,128)(2,1)} %param.10) | copy-start | bytes 1179652
  21.8 21.1 %collective-permute-start.8 = (f32[416,512]{1,0:T(8,128)}, f32[416,512]{1,0:T(8,128)S(1)}, u32[]{:S(2)}, u32[]{:S(2)}) collective-permute-start(f32[416,512]{1,0:T(8,128)} %get-tuple-element.45), channel_id=1, source_target_pairs={{0,1},{1,0},{2,3},{3,2},{4,5},{5,4},{6,7},{7,6},{8,9},{9,8},{10,11... | collective-permute-start | bytes 2555912 | tf_op jit(solution)/shard_map/ppermute | solution.py:81
  23.2 8.7 %collective-permute-start = (bf16[16,16,512]{2,1,0:T(8,128)(2,1)S(1)}, bf16[16,16,512]{2,1,0:T(8,128)(2,1)S(1)}, u32[]{:S(2)}, u32[]{:S(2)}) collective-permute-start(bf16[16,16,512]{2,1,0:T(8,128)(2,1)S(1)} %get-tuple-element.29), channel_id=1, source_target_pairs={{0,4},{4,0},{8,12},{12,8},{16,20},{20,16},{24,28},{28,24},{1,5},{5... | collective-permute-start | bytes 786440 | tf_op jit(solution)/shard_map/ppermute | solution.py:81
  25.0 9.2 %collective-permute-start.1 = (bf16[16,16,512]{2,1,0:T(8,128)(2,1)S(1)}, bf16[16,16,512]{2,1,0:T(8,128)(2,1)S(1)}, u32[]{:S(2)}, u32[]{:S(2)}) collective-permute-start(bf16[16,16,512]{2,1,0:T(8,128)(2,1)S(1)} %get-tuple-element.30), channel_id=1, source_target_pairs={{0,8},{4,12},{8,0},{12,4},{16,24},{20,28},{24,16},{28,20},{1,9},{5... | collective-permute-start | bytes 786440 | tf_op jit(solution)/shard_map/ppermute | solution.py:81
  26.5 12.2 %collective-permute-start.2 = (bf16[16,16,512]{2,1,0:T(8,128)(2,1)S(1)}, bf16[16,16,512]{2,1,0:T(8,128)(2,1)S(1)}, u32[]{:S(2)}, u32[]{:S(2)}) collective-permute-start(bf16[16,16,512]{2,1,0:T(8,128)(2,1)S(1)} %get-tuple-element.31), channel_id=1, source_target_pairs={{0,12},{4,8},{8,4},{12,0},{16,28},{20,24},{24,20},{28,16},{1,13},{... | collective-permute-start | bytes 786440 | tf_op jit(solution)/shard_map/ppermute | solution.py:81
  41.1 12.2 %collective-permute-start.6 = (f32[384,512]{1,0:T(8,128)}, f32[384,512]{1,0:T(8,128)}, u32[]{:S(2)}, u32[]{:S(2)}) collective-permute-start(f32[384,512]{1,0:T(8,128)} %get-tuple-element.41), channel_id=1, source_target_pairs={{0,1},{1,0},{2,3},{3,2},{4,5},{5,4},{6,7},{7,6},{8,9},{9,8},{10,11... | collective-permute-start | bytes 2359304 | tf_op jit(solution)/shard_map/ppermute | solution.py:81
  41.2 12.1 %collective-permute-start.11 = (bf16[12,32,512]{2,1,0:T(8,128)(2,1)S(1)}, bf16[12,32,512]{2,1,0:T(8,128)(2,1)S(1)}, u32[]{:S(2)}, u32[]{:S(2)}) collective-permute-start(bf16[12,32,512]{2,1,0:T(8,128)(2,1)S(1)} %copy-done), channel_id=1, source_target_pairs={{0,2},{1,3},{2,0},{3,1},{4,6},{5,7},{6,4},{7,5},{8,10},{9,11},{10,... | collective-permute-start | bytes 1179656 | tf_op jit(solution)/shard_map/ppermute | solution.py:81
  43.2 14.1 %collective-permute-start.9 = (s16[1,208,512]{2,1,0:T(8,128)(2,1)S(1)}, s16[1,208,512]{2,1,0:T(8,128)(2,1)S(1)}, u32[]{:S(2)}, u32[]{:S(2)}) collective-permute-start(s16[1,208,512]{2,1,0:T(8,128)(2,1)S(1)} %get-tuple-element.47), channel_id=1, source_target_pairs={{0,2},{1,3},{2,0},{3,1},{4,6},{5,7},{6,4},{7,5},{8,10},{9,11},{10,... | collective-permute-start | bytes 638984 | tf_op jit(solution)/shard_map/ppermute | solution.py:81
  43.6 17.9 %collective-permute-start.13 = (bf16[12,32,512]{2,1,0:T(8,128)(2,1)S(1)}, bf16[12,32,512]{2,1,0:T(8,128)(2,1)S(1)}, u32[]{:S(2)}, u32[]{:S(2)}) collective-permute-start(bf16[12,32,512]{2,1,0:T(8,128)(2,1)S(1)} %copy-done), channel_id=1, source_target_pairs={{0,1},{1,0},{2,3},{3,2},{4,5},{5,4},{6,7},{7,6},{8,9},{9,8},{10,11... | collective-permute-start | bytes 1179656 | tf_op jit(solution)/shard_map/ppermute | solution.py:81
  53.2 8.3 %copy-start.7 = (bf16[12,32,512]{2,1,0:T(8,128)(2,1)}, bf16[12,32,512]{2,1,0:T(8,128)(2,1)S(1)}, u32[]{:S(2)}) copy-start(bf16[12,32,512]{2,1,0:T(8,128)(2,1)S(1)} %collective-permute-done.11) | copy-start | bytes 1179652
  53.2 16.1 %collective-permute-start.12 = (bf16[12,32,512]{2,1,0:T(8,128)(2,1)S(1)}, bf16[12,32,512]{2,1,0:T(8,128)(2,1)S(1)}, u32[]{:S(2)}, u32[]{:S(2)}) collective-permute-start(bf16[12,32,512]{2,1,0:T(8,128)(2,1)S(1)} %collective-permute-done.11), channel_id=1, source_target_pairs={{0,1},{1,0},{2,3},{3,2},{4,5},{5,4},{6,7},{7,6},{8,9},{9,8},{10,11... | collective-permute-start | bytes 1179656 | tf_op jit(solution)/shard_map/ppermute | solution.py:81
  53.2 8.3 %copy-start.1 = (bf16[16,128]{1,0:T(8,128)(2,1)S(1)}, bf16[16,128]{1,0:T(8,128)(2,1)}, u32[]{:S(2)}) copy-start(bf16[16,128]{1,0:T(8,128)(2,1)} %ctf_ref.5) | copy-start | bytes 12292
  54.8 23.1 %collective-permute-start.7 = (s16[1,208,512]{2,1,0:T(8,128)(2,1)S(1)}, s16[1,208,512]{2,1,0:T(8,128)(2,1)S(1)}, u32[]{:S(2)}, u32[]{:S(2)}) collective-permute-start(s16[1,208,512]{2,1,0:T(8,128)(2,1)S(1)} %get-tuple-element.43), channel_id=1, source_target_pairs={{0,2},{1,3},{2,0},{3,1},{4,6},{5,7},{6,4},{7,5},{8,10},{9,11},{10,... | collective-permute-start | bytes 638984 | tf_op jit(solution)/shard_map/ppermute | solution.py:81
  57.5 20.3 %collective-permute-start.10 = (s16[208,512]{1,0:T(8,128)(2,1)S(1)}, s16[208,512]{1,0:T(8,128)(2,1)S(1)}, u32[]{:S(2)}, u32[]{:S(2)}) collective-permute-start(s16[208,512]{1,0:T(8,128)(2,1)S(1)} %get-tuple-element.49), channel_id=1, source_target_pairs={{0,16},{4,20},{8,24},{12,28},{16,0},{20,4},{24,8},{28,12},{1,17},{... | collective-permute-start | bytes 638984 | tf_op jit(solution)/shard_map/ppermute | solution.py:81

commit v5 on v4

--- a/solution.py
+++ b/solution.py
@@ -178,7 +178,7 @@
                         new[j + 2] = new[j + 2] + classes[3 * f + 2, r, at, :] * a_re
                 return tuple(new)
 
-            sums = lax.fori_loop(0, cycles, cycle, (zero,) * (3 * group * blocks), unroll=4)
+            sums = lax.fori_loop(0, cycles, cycle, (zero,) * (3 * group * blocks), unroll=16)
             for i in range(group):
                 for b in range(blocks):
                     s1, s2, s3 = sums[3 * (i * blocks + b) : 3 * (i * blocks + b) + 3]
@@ -193,31 +193,43 @@
     )
     cross[...] = scores
     inner = iota((8, LANES), 1) < cycles
-    row = jnp.zeros(outs[0].shape, jnp.float32)
+    tops, totals = [], []
     for n in range(count):
-            mine = []
-            for b in range(blocks):
-                powers = jnp.where(inner, jnp.broadcast_to(power[n : n + 1, :], (8, LANES)), 0.0)
-                energy = jnp.sum(powers * norms[b], axis=1, keepdims=True)
-                at = n * kinds + b * 8
-                mine.append(cross[at : at + 8, :] - 0.5 * energy)
-            mine = jnp.concatenate(mine, axis=0)
-            top = jnp.max(mine, axis=(0, 1), keepdims=True)
-            if merge:
-                per = count // (merge // 2)
-                pair, i = before[n // per * 2 : n // per * 2 + 2], n % per
-                top_before, total_before = pair[0][i : i + 1, :], pair[1][i : i + 1, :]
-                top = jnp.maximum(top, jnp.max(top_before, axis=1, keepdims=True))
-            total = jnp.sum(jnp.exp(mine - top), axis=(0, 1), keepdims=True)
-            if merge:
-                total = total + (total_before * jnp.exp(top_before - top))[:, :1]
-                here = iota(row.shape, 1) == start + n
-                row = jnp.where(here, jnp.broadcast_to(top + jnp.log(total), row.shape), row)
-            else:
-                outs[0][n : n + 1, :] = jnp.broadcast_to(top, (1, LANES))
-                outs[1][n : n + 1, :] = jnp.broadcast_to(total, (1, LANES))
+        powers = jnp.where(inner, jnp.broadcast_to(power[n : n + 1, :], (8, LANES)), 0.0)
+        most = None
+        for b in range(blocks):
+            energy = jnp.sum(powers * norms[b], axis=1, keepdims=True)
+            at = n * kinds + b * 8
+            mine = cross[at : at + 8, :] - 0.5 * energy
+            cross[at : at + 8, :] = mine
+            most = mine if most is None else jnp.maximum(most, mine)
+        tops.append(jnp.max(most, axis=(0, 1), keepdims=True))
     if merge:
-        outs[0][...] = row
+        per = count // (merge // 2)
+        old = [
+            [before[n // per * 2 + i][n % per : n % per + 1, :1] for n in range(count)] for i in range(2)
+        ]
+        tops = [jnp.maximum(top, was) for top, was in zip(tops, old[0])]
+    for n in range(count):
+        mine = jnp.exp(cross[n * kinds : (n + 1) * kinds, :] - tops[n])
+        part_sum = mine[:8]
+        for b in range(1, blocks):
+            part_sum = part_sum + mine[b * 8 : b * 8 + 8]
+        totals.append(jnp.sum(part_sum, axis=(0, 1), keepdims=True))
+    if not merge:
+        for n in range(count):
+            outs[0][n : n + 1, :] = jnp.broadcast_to(tops[n], (1, LANES))
+            outs[1][n : n + 1, :] = jnp.broadcast_to(totals[n], (1, LANES))
+        return
+    row_top = jnp.zeros(outs[0].shape, jnp.float32)
+    row_was, row_total, row_old = row_top, row_top, row_top
+    for n in range(count):
+        here = iota(row_top.shape, 1) == n
+        row_top = jnp.where(here, tops[n], row_top)
+        row_total = jnp.where(here, totals[n], row_total)
+        row_was = jnp.where(here, old[0][n], row_was)
+        row_old = jnp.where(here, old[1][n], row_old)
+    outs[0][...] = row_top + jnp.log(row_total + row_old * jnp.exp(row_was - row_top))
 
 
 def score(low, ctf, noise, first, second, table, before, start, count):

time: 79.1 us -> 75.8 us (0.958)
  Pallas kernels: 28.2 us -> 24.9 us
    pallas_call x3, Pallas kernels: 16.3 us -> 13 us  [score(): pl.pallas_call(functools.partial(score_kernel, merge=merge, start=start),...]
  transfers between devices with their start and end apart: 14 -> 14, of which waited for: 8 -> 8; matrix products, arithmetic and copies ran while one was open for 0% -> 0% of each run, Pallas kernels for 29% -> 26%
where the time goes in v5:
time: 75.8 us; the launch traced here: 75.5 us
  waiting for transfers between devices  34.7 us (46%)
  Pallas kernels  24.9 us (33%)
  starting transfers between devices  15 us (20%)
  between operations  0.88 us (1%)
    ppermute x14, waiting for transfers between devices, swap(): return lax.ppermute(value, axis, [(i, i ^ mask) for i in range(size)])  34.7 us
    ppermute x14, starting transfers between devices, swap(): return lax.ppermute(value, axis, [(i, i ^ mask) for i in range(size)])  15 us
    pallas_call x3, Pallas kernels, score(): pl.pallas_call(functools.partial(score_kernel, merge=merge, start=start),...  13 us
    pallas_call x2, Pallas kernels, class_sums(): pl.pallas_call(functools.partial(sums_kernel, slice_cycles=slice_cycles,...  5.16 us
    pallas_call x2, Pallas kernels, pieces(): pl.pallas_call(functools.partial(pieces_kernel, chunk=chunk), out_shape=s...  2.65 us
    pallas_call x2, Pallas kernels, split_shards(): pl.pallas_call(functools.partial(shard_kernel, was_coded=get.dtype == jnp...  1.73 us
  transfers between devices with their start and end apart: 14, of which 8 were waited for; matrix products, arithmetic and copies ran while one was open for 0% of the time, Pallas kernels for 26%

profile of v5, /device:TPU:0, one launch (start us, length us, event | category | flops | bytes accessed | tf_op | source)
XLA Modules:
  0.0 75.5 jit_solution(5571659765653285776)
XLA Ops:
  0.7 1.3 %shard_map.87 = (bf16[16,256]{1,0:T(8,128)(2,1)S(1)}, bf16[17,16,512]{2,1,0:T(8,128)(2,1)S(1)}, bf16[17,16,512]{2,1,0:T(8,128)(2,1)S(1)}, bf16[17,16,512]{2,1,0:T(8,128)(2,1)S(1)}) custom-call(s32[1]{0:T(128)} %bitcast.2.near_ref, s32[1]{0:T(128)} %bitcast.3.top_ref, bf16[16,2,4,16,512]{4,3,2,1,0:T(8,128)(2,1)} %bitcast.40, bf16[16,128]{1,0:T(8,128)(2,1)} %ctf_ref.5, ...), custom_call_target="tpu_custom_call" | custom-call | bytes 5400000 | tf_op jit(solution)/shard_map/pallas_call | solution.py:345
  2.0 3.0 %collective-permute-start.3 = (bf16[17,16,512]{2,1,0:T(8,128)(2,1)S(1)}, bf16[17,16,512]{2,1,0:T(8,128)(2,1)S(1)}, u32[]{:S(2)}, u32[]{:S(2)}) collective-permute-start(bf16[17,16,512]{2,1,0:T(8,128)(2,1)S(1)} %get-tuple-element.33), channel_id=1, source_target_pairs={{0,4},{4,0},{8,12},{12,8},{16,20},{20,16},{24,28},{28,24},{1,5},{5... | collective-permute-start | bytes 835592 | tf_op jit(solution)/shard_map/ppermute | solution.py:81
  5.0 1.6 %collective-permute-start.4 = (bf16[17,16,512]{2,1,0:T(8,128)(2,1)S(1)}, bf16[17,16,512]{2,1,0:T(8,128)(2,1)S(1)}, u32[]{:S(2)}, u32[]{:S(2)}) collective-permute-start(bf16[17,16,512]{2,1,0:T(8,128)(2,1)S(1)} %get-tuple-element.34), channel_id=1, source_target_pairs={{0,8},{4,12},{8,0},{12,4},{16,24},{20,28},{24,16},{28,20},{1,9},{5... | collective-permute-start | bytes 835592 | tf_op jit(solution)/shard_map/ppermute | solution.py:81
  6.6 5.1 %collective-permute-done.3.refs_3_ = bf16[17,16,512]{2,1,0:T(8,128)(2,1)S(1)} collective-permute-done((bf16[17,16,512]{2,1,0:T(8,128)(2,1)S(1)}, bf16[17,16,512]{2,1,0:T(8,128)(2,1)S(1)}, u32[]{:S(2)}, u32[]{:S(2)}) %collective-permute-start.3) | collective-permute-done | bytes 278560 | tf_op jit(solution)/shard_map/ppermute | solution.py:81
  11.7 2.9 %collective-permute-done.4.refs_4_ = bf16[17,16,512]{2,1,0:T(8,128)(2,1)S(1)} collective-permute-done((bf16[17,16,512]{2,1,0:T(8,128)(2,1)S(1)}, bf16[17,16,512]{2,1,0:T(8,128)(2,1)S(1)}, u32[]{:S(2)}, u32[]{:S(2)}) %collective-permute-start.4) | collective-permute-done | bytes 278560 | tf_op jit(solution)/shard_map/ppermute | solution.py:81
  14.6 4.4 %collective-permute-done.5.refs_5_ = bf16[17,16,512]{2,1,0:T(8,128)(2,1)S(1)} collective-permute-done((bf16[17,16,512]{2,1,0:T(8,128)(2,1)S(1)}, bf16[17,16,512]{2,1,0:T(8,128)(2,1)S(1)}, u32[]{:S(2)}, u32[]{:S(2)}) %collective-permute-start.5) | collective-permute-done | bytes 278560 | tf_op jit(solution)/shard_map/ppermute | solution.py:81
  18.9 2.8 %shard_map.88 = (f32[416,512]{1,0:T(8,128)S(1)}, f32[416,512]{1,0:T(8,128)}, s32[8,128]{1,0:T(8,128)}, bf16[64,256]{1,0:T(8,128)(2,1)}, f32[64,256]{1,0:T(8,128)}, /*index=5*/f32[64,256]{1,0:T(8,128)}) custom-call(s32[1]{0:T(128)} %bitcast.2.near_ref, s32[1]{0:T(128)} %bitcast.3.top_ref, s32[1]{0:T(128)} %bitcast.4.cls_ref, ...), custom_call_target="tpu_custom_call" | custom-call | bytes 9000000 | tf_op jit(solution)/shard_map/pallas_call | solution.py:492
  21.9 1.3 %shard_map.86 = (bf16[16,16,512]{2,1,0:T(8,128)(2,1)S(1)}, bf16[16,16,512]{2,1,0:T(8,128)(2,1)S(1)}, bf16[16,16,512]{2,1,0:T(8,128)(2,1)S(1)}) custom-call(s32[1]{0:T(128)} %bitcast.2.near_ref, s32[1]{0:T(128)} %bitcast.3.top_ref, bf16[16,2,4,16,512]{4,3,2,1,0:T(8,128)(2,1)} %bitcast.42), custom_call_target="tpu_custom_call" | custom-call | bytes 5400000 | tf_op jit(solution)/shard_map/pallas_call | solution.py:345
  23.2 1.7 %collective-permute-start = (bf16[16,16,512]{2,1,0:T(8,128)(2,1)S(1)}, bf16[16,16,512]{2,1,0:T(8,128)(2,1)S(1)}, u32[]{:S(2)}, u32[]{:S(2)}) collective-permute-start(bf16[16,16,512]{2,1,0:T(8,128)(2,1)S(1)} %get-tuple-element.29), channel_id=1, source_target_pairs={{0,4},{4,0},{8,12},{12,8},{16,20},{20,16},{24,28},{28,24},{1,5},{5... | collective-permute-start | bytes 786440 | tf_op jit(solution)/shard_map/ppermute | solution.py:81
  25.0 1.6 %collective-permute-start.1 = (bf16[16,16,512]{2,1,0:T(8,128)(2,1)S(1)}, bf16[16,16,512]{2,1,0:T(8,128)(2,1)S(1)}, u32[]{:S(2)}, u32[]{:S(2)}) collective-permute-start(bf16[16,16,512]{2,1,0:T(8,128)(2,1)S(1)} %get-tuple-element.30), channel_id=1, source_target_pairs={{0,8},{4,12},{8,0},{12,4},{16,24},{20,28},{24,16},{28,20},{1,9},{5... | collective-permute-start | bytes 786440 | tf_op jit(solution)/shard_map/ppermute | solution.py:81
  26.8 5.2 %collective-permute-done.refs_2_ = bf16[16,16,512]{2,1,0:T(8,128)(2,1)S(1)} collective-permute-done((bf16[16,16,512]{2,1,0:T(8,128)(2,1)S(1)}, bf16[16,16,512]{2,1,0:T(8,128)(2,1)S(1)}, u32[]{:S(2)}, u32[]{:S(2)}) %collective-permute-start) | collective-permute-done | bytes 262176 | tf_op jit(solution)/shard_map/ppermute | solution.py:81
  31.9 2.2 %collective-permute-done.1.refs_3_ = bf16[16,16,512]{2,1,0:T(8,128)(2,1)S(1)} collective-permute-done((bf16[16,16,512]{2,1,0:T(8,128)(2,1)S(1)}, bf16[16,16,512]{2,1,0:T(8,128)(2,1)S(1)}, u32[]{:S(2)}, u32[]{:S(2)}) %collective-permute-start.1) | collective-permute-done | bytes 262176 | tf_op jit(solution)/shard_map/ppermute | solution.py:81
  34.1 4.6 %collective-permute-done.2.refs_4_ = bf16[16,16,512]{2,1,0:T(8,128)(2,1)S(1)} collective-permute-done((bf16[16,16,512]{2,1,0:T(8,128)(2,1)S(1)}, bf16[16,16,512]{2,1,0:T(8,128)(2,1)S(1)}, u32[]{:S(2)}, u32[]{:S(2)}) %collective-permute-start.2) | collective-permute-done | bytes 262176 | tf_op jit(solution)/shard_map/ppermute | solution.py:81
  38.8 2.3 %shard_map.89 = (f32[384,512]{1,0:T(8,128)S(1)}, f32[384,512]{1,0:T(8,128)}) custom-call(s32[1]{0:T(128)} %bitcast.2.near_ref, s32[1]{0:T(128)} %bitcast.3.top_ref, s32[1]{0:T(128)} %bitcast.4.cls_ref, f32[1,128]{1,0:T(1,128)S(1)} %bitcast.36, bf16[16,2,4,16,512]{4,3,2,1,0:T(8,128)(2,1)} %bitcast.43, bf16[16,16,512]{2,1,0:T(8,128)(2,1)S(1)} %collective-permute-done.refs_2_, ...), custom_call_target="tpu_custom_call" | custom-call | bytes 9000000 | tf_op jit(solution)/shard_map/pallas_call | solution.py:492
  41.2 1.8 %collective-permute-start.11 = (bf16[12,32,512]{2,1,0:T(8,128)(2,1)S(1)}, bf16[12,32,512]{2,1,0:T(8,128)(2,1)S(1)}, u32[]{:S(2)}, u32[]{:S(2)}) collective-permute-start(bf16[12,32,512]{2,1,0:T(8,128)(2,1)S(1)} %copy-done), channel_id=1, source_target_pairs={{0,2},{1,3},{2,0},{3,1},{4,6},{5,7},{6,4},{7,5},{8,10},{9,11},{10,... | collective-permute-start | bytes 1179656 | tf_op jit(solution)/shard_map/ppermute | solution.py:81
  43.6 9.7 %collective-permute-done.11 = bf16[12,32,512]{2,1,0:T(8,128)(2,1)S(1)} collective-permute-done((bf16[12,32,512]{2,1,0:T(8,128)(2,1)S(1)}, bf16[12,32,512]{2,1,0:T(8,128)(2,1)S(1)}, u32[]{:S(2)}, u32[]{:S(2)}) %collective-permute-start.11) | collective-permute-done | bytes 393248 | tf_op jit(solution)/shard_map/ppermute | solution.py:81
  53.3 1.5 %shard_map.90 = (f32[1,192,512]{2,1,0:T(8,128)S(1)}, s16[1,208,512]{2,1,0:T(8,128)(2,1)S(1)}) custom-call(s32[1]{0:T(128)} %bitcast.1.bit_ref, f32[2,192,512]{2,1,0:T(8,128)S(1)} %bitcast.29, f32[2,192,512]{2,1,0:T(8,128)} %bitcast.11.get_ref), custom_call_target="tpu_custom_call" | custom-call | bytes 5400000 | tf_op jit(solution)/shard_map/pallas_call | solution.py:585
  54.8 1.8 %collective-permute-start.7 = (s16[1,208,512]{2,1,0:T(8,128)(2,1)S(1)}, s16[1,208,512]{2,1,0:T(8,128)(2,1)S(1)}, u32[]{:S(2)}, u32[]{:S(2)}) collective-permute-start(s16[1,208,512]{2,1,0:T(8,128)(2,1)S(1)} %get-tuple-element.43), channel_id=1, source_target_pairs={{0,2},{1,3},{2,0},{3,1},{4,6},{5,7},{6,4},{7,5},{8,10},{9,11},{10,... | collective-permute-start | bytes 638984 | tf_op jit(solution)/shard_map/ppermute | solution.py:81
  57.5 2.8 %collective-permute-start.10 = (s16[208,512]{1,0:T(8,128)(2,1)S(1)}, s16[208,512]{1,0:T(8,128)(2,1)S(1)}, u32[]{:S(2)}, u32[]{:S(2)}) collective-permute-start(s16[208,512]{1,0:T(8,128)(2,1)S(1)} %get-tuple-element.49), channel_id=1, source_target_pairs={{0,16},{4,20},{8,24},{12,28},{16,0},{20,4},{24,8},{28,12},{1,17},{... | collective-permute-start | bytes 638984 | tf_op jit(solution)/shard_map/ppermute | solution.py:81
  60.4 1.1 %table.1 = (bf16[512,512]{1,0:T(8,128)(2,1)S(1)}, bf16[16,32,512]{2,1,0:T(8,128)(2,1)S(1)}) custom-call(bf16[16,128,512]{2,1,0:T(8,128)(2,1)} %image_ref.1), custom_call_target="tpu_custom_call" | custom-call | bytes 7200000 | tf_op jit(solution)/shard_map/table/pallas_call | solution.py:56
  61.5 2.6 %shard_map.92 = (f32[8,128]{1,0:T(8,128)S(1)}, f32[8,128]{1,0:T(8,128)S(1)}) custom-call(bf16[16,32,512]{2,1,0:T(8,128)(2,1)S(1)} %get-tuple-element.50.low_ref, bf16[16,128]{1,0:T(8,128)(2,1)S(1)} %copy-done.1, f32[1,128]{1,0:T(1,128)S(1)} %bitcast.37, bf16[384,512]{1,0:T(8,128)(2,1)S(1)} %bitcast.23, bf16[384,512]{1,0:T(8,128)(2,1)S(1)} %bitcast.25, ...), custom_call_target="tpu_custom_call" | custom-call | bytes 14400000 | tf_op jit(solution)/shard_map/pallas_call | solution.py:242
  64.2 2.6 %shard_map.93 = (f32[8,128]{1,0:T(8,128)S(1)}, f32[8,128]{1,0:T(8,128)S(1)}) custom-call(bf16[16,32,512]{2,1,0:T(8,128)(2,1)S(1)} %get-tuple-element.50.low_ref, bf16[16,128]{1,0:T(8,128)(2,1)S(1)} %copy-done.1, f32[1,128]{1,0:T(1,128)S(1)} %bitcast.38, bf16[384,512]{1,0:T(8,128)(2,1)S(1)} %bitcast.24, bf16[384,512]{1,0:T(8,128)(2,1)S(1)} %bitcast.26, ...), custom_call_target="tpu_custom_call" | custom-call | bytes 14400000 | tf_op jit(solution)/shard_map/pallas_call | solution.py:242
  66.8 7.7 %shard_map.94 = f32[1,16]{1,0:T(1,128)} custom-call(bf16[16,32,512]{2,1,0:T(8,128)(2,1)S(1)} %get-tuple-element.50.low_ref, bf16[16,128]{1,0:T(8,128)(2,1)S(1)} %copy-done.1, f32[1,128]{1,0:T(1,128)S(1)} %bitcast.39, bf16[384,512]{1,0:T(8,128)(2,1)} %bitcast.44, bf16[384,512]{1,0:T(8,128)(2,1)S(1)} %bitcast.32, ...), custom_call_target="tpu_custom_call" | custom-call | bytes 28800000 | tf_op jit(solution)/shard_map/pallas_call | solution.py:242
  74.5 1.0 %finish.1 = f32[12,16,512]{2,1,0:T(8,128)} custom-call(s32[1]{0:T(128)} %bitcast.dom_ref, f32[192,512]{1,0:T(8,128)S(1)} %bitcast.31, s16[208,512]{1,0:T(8,128)(2,1)S(1)} %bitcast.34, f32[16,128]{1,0:T(8,128)S(1)} %get-tuple-element.48.power_ref, s16[208,512]{1,0:T(8,128)(2,1)S(1)} %collective-permute-done.10.came_ref), custom_call_target="tpu_custom_call" | custom-call | bytes 3600000 | tf_op jit(solution)/shard_map/finish/pallas_call | solution.py:635
  (32 shorter events, 2.1 us)
Async XLA Ops:
  0.6 18.3 %copy-start.5 = (f32[128]{0:T(128)S(1)}, f32[128]{0:T(128)}, u32[]{:S(2)}) copy-start(f32[128]{0:T(128)} %param.9) | copy-start | bytes 1540
  2.0 9.7 %collective-permute-start.3 = (bf16[17,16,512]{2,1,0:T(8,128)(2,1)S(1)}, bf16[17,16,512]{2,1,0:T(8,128)(2,1)S(1)}, u32[]{:S(2)}, u32[]{:S(2)}) collective-permute-start(bf16[17,16,512]{2,1,0:T(8,128)(2,1)S(1)} %get-tuple-element.33), channel_id=1, source_target_pairs={{0,4},{4,0},{8,12},{12,8},{16,20},{20,16},{24,28},{28,24},{1,5},{5... | collective-permute-start | bytes 835592 | tf_op jit(solution)/shard_map/ppermute | solution.py:81
  5.0 9.5 %collective-permute-start.4 = (bf16[17,16,512]{2,1,0:T(8,128)(2,1)S(1)}, bf16[17,16,512]{2,1,0:T(8,128)(2,1)S(1)}, u32[]{:S(2)}, u32[]{:S(2)}) collective-permute-start(bf16[17,16,512]{2,1,0:T(8,128)(2,1)S(1)} %get-tuple-element.34), channel_id=1, source_target_pairs={{0,8},{4,12},{8,0},{12,4},{16,24},{20,28},{24,16},{28,20},{1,9},{5... | collective-permute-start | bytes 835592 | tf_op jit(solution)/shard_map/ppermute | solution.py:81
  6.6 12.3 %collective-permute-start.5 = (bf16[17,16,512]{2,1,0:T(8,128)(2,1)S(1)}, bf16[17,16,512]{2,1,0:T(8,128)(2,1)S(1)}, u32[]{:S(2)}, u32[]{:S(2)}) collective-permute-start(bf16[17,16,512]{2,1,0:T(8,128)(2,1)S(1)} %get-tuple-element.35), channel_id=1, source_target_pairs={{0,12},{4,8},{8,4},{12,0},{16,28},{20,24},{24,20},{28,16},{1,13},{... | collective-permute-start | bytes 835592 | tf_op jit(solution)/shard_map/ppermute | solution.py:81
  21.8 17.0 %copy-start.2 = (f32[64,256]{1,0:T(8,128)S(1)}, f32[64,256]{1,0:T(8,128)}, u32[]{:S(2)}) copy-start(f32[64,256]{1,0:T(8,128)} %get-tuple-element.38.refs_7_) | copy-start | bytes 196612
  21.8 17.0 %copy-start.3 = (f32[64,256]{1,0:T(8,128)S(1)}, f32[64,256]{1,0:T(8,128)}, u32[]{:S(2)}) copy-start(f32[64,256]{1,0:T(8,128)} %get-tuple-element.39.refs_8_) | copy-start | bytes 196612
  21.8 17.0 %copy-start.4 = (bf16[64,256]{1,0:T(8,128)(2,1)S(1)}, bf16[64,256]{1,0:T(8,128)(2,1)}, u32[]{:S(2)}) copy-start(bf16[64,256]{1,0:T(8,128)(2,1)} %get-tuple-element.37.refs_6_) | copy-start | bytes 98308
  21.8 17.0 %copy-start.6 = (s32[8,128]{1,0:T(8,128)S(1)}, s32[8,128]{1,0:T(8,128)}, u32[]{:S(2)}) copy-start(s32[8,128]{1,0:T(8,128)} %get-tuple-element.36.refs_5_) | copy-start | bytes 12292
  21.8 19.4 %copy-start = (bf16[12,32,512]{2,1,0:T(8,128)(2,1)S(1)}, bf16[12,32,512]{2,1,0:T(8,128)(2,1)}, u32[]{:S(2)}) copy-start(bf16[12,32,512]{2,1,0:T(8,128)(2,1)} %param.10) | copy-start | bytes 1179652
  21.8 21.1 %collective-permute-start.8 = (f32[416,512]{1,0:T(8,128)}, f32[416,512]{1,0:T(8,128)S(1)}, u32[]{:S(2)}, u32[]{:S(2)}) collective-permute-start(f32[416,512]{1,0:T(8,128)} %get-tuple-element.45), channel_id=1, source_target_pairs={{0,1},{1,0},{2,3},{3,2},{4,5},{5,4},{6,7},{7,6},{8,9},{9,8},{10,11... | collective-permute-start | bytes 2555912 | tf_op jit(solution)/shard_map/ppermute | solution.py:81
  23.2 8.7 %collective-permute-start = (bf16[16,16,512]{2,1,0:T(8,128)(2,1)S(1)}, bf16[16,16,512]{2,1,0:T(8,128)(2,1)S(1)}, u32[]{:S(2)}, u32[]{:S(2)}) collective-permute-start(bf16[16,16,512]{2,1,0:T(8,128)(2,1)S(1)} %get-tuple-element.29), channel_id=1, source_target_pairs={{0,4},{4,0},{8,12},{12,8},{16,20},{20,16},{24,28},{28,24},{1,5},{5... | collective-permute-start | bytes 786440 | tf_op jit(solution)/shard_map/ppermute | solution.py:81
  25.0 9.2 %collective-permute-start.1 = (bf16[16,16,512]{2,1,0:T(8,128)(2,1)S(1)}, bf16[16,16,512]{2,1,0:T(8,128)(2,1)S(1)}, u32[]{:S(2)}, u32[]{:S(2)}) collective-permute-start(bf16[16,16,512]{2,1,0:T(8,128)(2,1)S(1)} %get-tuple-element.30), channel_id=1, source_target_pairs={{0,8},{4,12},{8,0},{12,4},{16,24},{20,28},{24,16},{28,20},{1,9},{5... | collective-permute-start | bytes 786440 | tf_op jit(solution)/shard_map/ppermute | solution.py:81
  26.5 12.2 %collective-permute-start.2 = (bf16[16,16,512]{2,1,0:T(8,128)(2,1)S(1)}, bf16[16,16,512]{2,1,0:T(8,128)(2,1)S(1)}, u32[]{:S(2)}, u32[]{:S(2)}) collective-permute-start(bf16[16,16,512]{2,1,0:T(8,128)(2,1)S(1)} %get-tuple-element.31), channel_id=1, source_target_pairs={{0,12},{4,8},{8,4},{12,0},{16,28},{20,24},{24,20},{28,16},{1,13},{... | collective-permute-start | bytes 786440 | tf_op jit(solution)/shard_map/ppermute | solution.py:81
  41.1 12.2 %collective-permute-start.6 = (f32[384,512]{1,0:T(8,128)}, f32[384,512]{1,0:T(8,128)}, u32[]{:S(2)}, u32[]{:S(2)}) collective-permute-start(f32[384,512]{1,0:T(8,128)} %get-tuple-element.41), channel_id=1, source_target_pairs={{0,1},{1,0},{2,3},{3,2},{4,5},{5,4},{6,7},{7,6},{8,9},{9,8},{10,11... | collective-permute-start | bytes 2359304 | tf_op jit(solution)/shard_map/ppermute | solution.py:81
  41.2 12.1 %collective-permute-start.11 = (bf16[12,32,512]{2,1,0:T(8,128)(2,1)S(1)}, bf16[12,32,512]{2,1,0:T(8,128)(2,1)S(1)}, u32[]{:S(2)}, u32[]{:S(2)}) collective-permute-start(bf16[12,32,512]{2,1,0:T(8,128)(2,1)S(1)} %copy-done), channel_id=1, source_target_pairs={{0,2},{1,3},{2,0},{3,1},{4,6},{5,7},{6,4},{7,5},{8,10},{9,11},{10,... | collective-permute-start | bytes 1179656 | tf_op jit(solution)/shard_map/ppermute | solution.py:81
  43.2 14.1 %collective-permute-start.9 = (s16[1,208,512]{2,1,0:T(8,128)(2,1)S(1)}, s16[1,208,512]{2,1,0:T(8,128)(2,1)S(1)}, u32[]{:S(2)}, u32[]{:S(2)}) collective-permute-start(s16[1,208,512]{2,1,0:T(8,128)(2,1)S(1)} %get-tuple-element.47), channel_id=1, source_target_pairs={{0,2},{1,3},{2,0},{3,1},{4,6},{5,7},{6,4},{7,5},{8,10},{9,11},{10,... | collective-permute-start | bytes 638984 | tf_op jit(solution)/shard_map/ppermute | solution.py:81
  43.6 17.9 %collective-permute-start.13 = (bf16[12,32,512]{2,1,0:T(8,128)(2,1)S(1)}, bf16[12,32,512]{2,1,0:T(8,128)(2,1)S(1)}, u32[]{:S(2)}, u32[]{:S(2)}) collective-permute-start(bf16[12,32,512]{2,1,0:T(8,128)(2,1)S(1)} %copy-done), channel_id=1, source_target_pairs={{0,1},{1,0},{2,3},{3,2},{4,5},{5,4},{6,7},{7,6},{8,9},{9,8},{10,11... | collective-permute-start | bytes 1179656 | tf_op jit(solution)/shard_map/ppermute | solution.py:81
  53.2 8.3 %copy-start.7 = (bf16[12,32,512]{2,1,0:T(8,128)(2,1)}, bf16[12,32,512]{2,1,0:T(8,128)(2,1)S(1)}, u32[]{:S(2)}) copy-start(bf16[12,32,512]{2,1,0:T(8,128)(2,1)S(1)} %collective-permute-done.11) | copy-start | bytes 1179652
  53.2 13.6 %collective-permute-start.12 = (bf16[12,32,512]{2,1,0:T(8,128)(2,1)S(1)}, bf16[12,32,512]{2,1,0:T(8,128)(2,1)S(1)}, u32[]{:S(2)}, u32[]{:S(2)}) collective-permute-start(bf16[12,32,512]{2,1,0:T(8,128)(2,1)S(1)} %collective-permute-done.11), channel_id=1, source_target_pairs={{0,1},{1,0},{2,3},{3,2},{4,5},{5,4},{6,7},{7,6},{8,9},{9,8},{10,11... | collective-permute-start | bytes 1179656 | tf_op jit(solution)/shard_map/ppermute | solution.py:81
  53.2 8.3 %copy-start.1 = (bf16[16,128]{1,0:T(8,128)(2,1)S(1)}, bf16[16,128]{1,0:T(8,128)(2,1)}, u32[]{:S(2)}) copy-start(bf16[16,128]{1,0:T(8,128)(2,1)} %ctf_ref.5) | copy-start | bytes 12292
  54.8 19.8 %collective-permute-start.7 = (s16[1,208,512]{2,1,0:T(8,128)(2,1)S(1)}, s16[1,208,512]{2,1,0:T(8,128)(2,1)S(1)}, u32[]{:S(2)}, u32[]{:S(2)}) collective-permute-start(s16[1,208,512]{2,1,0:T(8,128)(2,1)S(1)} %get-tuple-element.43), channel_id=1, source_target_pairs={{0,2},{1,3},{2,0},{3,1},{4,6},{5,7},{6,4},{7,5},{8,10},{9,11},{10,... | collective-permute-start | bytes 638984 | tf_op jit(solution)/shard_map/ppermute | solution.py:81
  57.5 17.0 %collective-permute-start.10 = (s16[208,512]{1,0:T(8,128)(2,1)S(1)}, s16[208,512]{1,0:T(8,128)(2,1)S(1)}, u32[]{:S(2)}, u32[]{:S(2)}) collective-permute-start(s16[208,512]{1,0:T(8,128)(2,1)S(1)} %get-tuple-element.49), channel_id=1, source_target_pairs={{0,16},{4,20},{8,24},{12,28},{16,0},{20,4},{24,8},{28,12},{1,17},{... | collective-permute-start | bytes 638984 | tf_op jit(solution)/shard_map/ppermute | solution.py:81

commit v6 on v5

--- a/solution.py
+++ b/solution.py
@@ -103,6 +103,9 @@
     low_ref, ctf_ref, noise_ref, first_ref, second_ref, table_ref, *refs, merge, start
 ):
     before, refs = refs[:merge], refs[merge:]
+    found = None
+    if merge and start:
+        found, refs = refs[0], refs[1:]
     outs, refs = refs[: 1 if merge else 2], refs[1 if merge else 2 :]
     image, image_sum, staged, classes, cross = refs[:5]
     copies = []
@@ -224,25 +227,28 @@
     row_top = jnp.zeros(outs[0].shape, jnp.float32)
     row_was, row_total, row_old = row_top, row_top, row_top
     for n in range(count):
-        here = iota(row_top.shape, 1) == n
+        here = iota(row_top.shape, 1) == start + n
         row_top = jnp.where(here, tops[n], row_top)
         row_total = jnp.where(here, totals[n], row_total)
         row_was = jnp.where(here, old[0][n], row_was)
         row_old = jnp.where(here, old[1][n], row_old)
-    outs[0][...] = row_top + jnp.log(row_total + row_old * jnp.exp(row_was - row_top))
-
-
-def score(low, ctf, noise, first, second, table, before, start, count):
+    result = row_top + jnp.log(row_total + row_old * jnp.exp(row_was - row_top))
+    at = iota(row_top.shape, 1)
+    earlier = row_top if found is None else found[...]
+    outs[0][...] = jnp.where((at >= start) & (at < start + count), result, earlier)
+
+
+def score(low, ctf, noise, first, second, table, before, found, start, count):
     _, cycles, width = low.shape
     kinds = 2 * first.shape[0]
     merge = len(before)
     each = pltpu.VMEM((count, LANES), jnp.float32)
-    row = jax.ShapeDtypeStruct((1, count), jnp.float32)
+    row = jax.ShapeDtypeStruct((1, ctf.shape[0]), jnp.float32)
     part = (kinds // 2 * cycles, width)
     return pl.pallas_call(
         functools.partial(score_kernel, merge=merge, start=start),
         out_shape=row if merge else (each, each),
-        in_specs=[HERE] * 3 + [THERE if merge else HERE] + [HERE] * (2 + merge),
+        in_specs=[HERE] * 3 + [THERE if merge else HERE] + [HERE] * (2 + merge + len(found)),
         out_specs=HERE if merge else (HERE, HERE),
         scratch_shapes=[
             pltpu.VMEM((width // LANES, count * cycles, LANES), jnp.float32),
@@ -262,7 +268,7 @@
     )(
         *held_near(low), ctf, noise, *(held_far if merge else held_near)(first.reshape(part)),
         *held_near(second.reshape(part), table),
-        *before,
+        *before, *found,
     )
 
 
@@ -686,10 +692,17 @@
     per = count // NEAR_CALLS
     before = []
     for i in range(NEAR_CALLS):
-        before += score(low, ctf, noise, own_side, near_refs, table, (), i * per, per)
+        before += score(low, ctf, noise, own_side, near_refs, table, (), (), i * per, per)
     far_refs = swap(other_side, "cls", 1)
-    row = score(low, ctf, noise, other_side, far_refs, table, before, 0, count)
-    log_evidence = row.reshape(count)
+    row = ()
+    for i in range(NEAR_CALLS):
+        row = (
+            score(
+                low, ctf, noise, other_side, far_refs, table, before[2 * i : 2 * i + 2], row, i * per,
+                per,
+            ),
+        )
+    log_evidence = row[0].reshape(count)
 
     scalars = (near, top, cls.reshape(1))
     ends, shared = [], []

time: 75.8 us -> 77.8 us (1.026)
  Pallas kernels: 24.9 us -> 26.8 us
    pallas_call x3 -> x4, Pallas kernels: 13 us -> 14.9 us  [score(): pl.pallas_call(functools.partial(score_kernel, merge=merge, start=start),...]
  transfers between devices with their start and end apart: 14 -> 14, of which waited for: 8 -> 8; matrix products, arithmetic and copies ran while one was open for 0% -> 0% of each run, Pallas kernels for 26% -> 28%
where the time goes in v6:
time: 77.8 us; the launch traced here: 77.4 us
  waiting for transfers between devices  34.7 us (45%)
  Pallas kernels  26.8 us (34%)
  starting transfers between devices  15 us (19%)
  between operations  0.89 us (1%)
    ppermute x14, waiting for transfers between devices, swap(): return lax.ppermute(value, axis, [(i, i ^ mask) for i in range(size)])  34.7 us
    ppermute x14, starting transfers between devices, swap(): return lax.ppermute(value, axis, [(i, i ^ mask) for i in range(size)])  15 us
    pallas_call x4, Pallas kernels, score(): pl.pallas_call(functools.partial(score_kernel, merge=merge, start=start),...  14.9 us
    pallas_call x2, Pallas kernels, class_sums(): pl.pallas_call(functools.partial(sums_kernel, slice_cycles=slice_cycles,...  5.16 us
    pallas_call x2, Pallas kernels, pieces(): pl.pallas_call(functools.partial(pieces_kernel, chunk=chunk), out_shape=s...  2.65 us
    pallas_call x2, Pallas kernels, split_shards(): pl.pallas_call(functools.partial(shard_kernel, was_coded=get.dtype == jnp...  1.73 us
  transfers between devices with their start and end apart: 14, of which 8 were waited for; matrix products, arithmetic and copies ran while one was open for 0% of the time, Pallas kernels for 28%

profile of v6, /device:TPU:0, one launch (start us, length us, event | category | flops | bytes accessed | tf_op | source)
XLA Modules:
  0.0 77.4 jit_solution(10178434329923568322)
XLA Ops:
  0.7 1.3 %shard_map.87 = (bf16[16,256]{1,0:T(8,128)(2,1)S(1)}, bf16[17,16,512]{2,1,0:T(8,128)(2,1)S(1)}, bf16[17,16,512]{2,1,0:T(8,128)(2,1)S(1)}, bf16[17,16,512]{2,1,0:T(8,128)(2,1)S(1)}) custom-call(s32[1]{0:T(128)} %bitcast.2.near_ref, s32[1]{0:T(128)} %bitcast.3.top_ref, bf16[16,2,4,16,512]{4,3,2,1,0:T(8,128)(2,1)} %bitcast.42, bf16[16,128]{1,0:T(8,128)(2,1)} %ctf_ref.7, ...), custom_call_target="tpu_custom_call" | custom-call | bytes 5400000 | tf_op jit(solution)/shard_map/pallas_call | solution.py:351
  2.0 3.0 %collective-permute-start.3 = (bf16[17,16,512]{2,1,0:T(8,128)(2,1)S(1)}, bf16[17,16,512]{2,1,0:T(8,128)(2,1)S(1)}, u32[]{:S(2)}, u32[]{:S(2)}) collective-permute-start(bf16[17,16,512]{2,1,0:T(8,128)(2,1)S(1)} %get-tuple-element.33), channel_id=1, source_target_pairs={{0,4},{4,0},{8,12},{12,8},{16,20},{20,16},{24,28},{28,24},{1,5},{5... | collective-permute-start | bytes 835592 | tf_op jit(solution)/shard_map/ppermute | solution.py:81
  5.0 1.6 %collective-permute-start.4 = (bf16[17,16,512]{2,1,0:T(8,128)(2,1)S(1)}, bf16[17,16,512]{2,1,0:T(8,128)(2,1)S(1)}, u32[]{:S(2)}, u32[]{:S(2)}) collective-permute-start(bf16[17,16,512]{2,1,0:T(8,128)(2,1)S(1)} %get-tuple-element.34), channel_id=1, source_target_pairs={{0,8},{4,12},{8,0},{12,4},{16,24},{20,28},{24,16},{28,20},{1,9},{5... | collective-permute-start | bytes 835592 | tf_op jit(solution)/shard_map/ppermute | solution.py:81
  6.6 5.1 %collective-permute-done.3.refs_3_ = bf16[17,16,512]{2,1,0:T(8,128)(2,1)S(1)} collective-permute-done((bf16[17,16,512]{2,1,0:T(8,128)(2,1)S(1)}, bf16[17,16,512]{2,1,0:T(8,128)(2,1)S(1)}, u32[]{:S(2)}, u32[]{:S(2)}) %collective-permute-start.3) | collective-permute-done | bytes 278560 | tf_op jit(solution)/shard_map/ppermute | solution.py:81
  11.7 2.9 %collective-permute-done.4.refs_4_ = bf16[17,16,512]{2,1,0:T(8,128)(2,1)S(1)} collective-permute-done((bf16[17,16,512]{2,1,0:T(8,128)(2,1)S(1)}, bf16[17,16,512]{2,1,0:T(8,128)(2,1)S(1)}, u32[]{:S(2)}, u32[]{:S(2)}) %collective-permute-start.4) | collective-permute-done | bytes 278560 | tf_op jit(solution)/shard_map/ppermute | solution.py:81
  14.6 4.4 %collective-permute-done.5.refs_5_ = bf16[17,16,512]{2,1,0:T(8,128)(2,1)S(1)} collective-permute-done((bf16[17,16,512]{2,1,0:T(8,128)(2,1)S(1)}, bf16[17,16,512]{2,1,0:T(8,128)(2,1)S(1)}, u32[]{:S(2)}, u32[]{:S(2)}) %collective-permute-start.5) | collective-permute-done | bytes 278560 | tf_op jit(solution)/shard_map/ppermute | solution.py:81
  18.9 2.8 %shard_map.88 = (f32[416,512]{1,0:T(8,128)S(1)}, f32[416,512]{1,0:T(8,128)}, s32[8,128]{1,0:T(8,128)}, bf16[64,256]{1,0:T(8,128)(2,1)}, f32[64,256]{1,0:T(8,128)}, /*index=5*/f32[64,256]{1,0:T(8,128)}) custom-call(s32[1]{0:T(128)} %bitcast.2.near_ref, s32[1]{0:T(128)} %bitcast.3.top_ref, s32[1]{0:T(128)} %bitcast.4.cls_ref, ...), custom_call_target="tpu_custom_call" | custom-call | bytes 9000000 | tf_op jit(solution)/shard_map/pallas_call | solution.py:498
  21.9 1.3 %shard_map.86 = (bf16[16,16,512]{2,1,0:T(8,128)(2,1)S(1)}, bf16[16,16,512]{2,1,0:T(8,128)(2,1)S(1)}, bf16[16,16,512]{2,1,0:T(8,128)(2,1)S(1)}) custom-call(s32[1]{0:T(128)} %bitcast.2.near_ref, s32[1]{0:T(128)} %bitcast.3.top_ref, bf16[16,2,4,16,512]{4,3,2,1,0:T(8,128)(2,1)} %bitcast.44), custom_call_target="tpu_custom_call" | custom-call | bytes 5400000 | tf_op jit(solution)/shard_map/pallas_call | solution.py:351
  23.2 1.7 %collective-permute-start = (bf16[16,16,512]{2,1,0:T(8,128)(2,1)S(1)}, bf16[16,16,512]{2,1,0:T(8,128)(2,1)S(1)}, u32[]{:S(2)}, u32[]{:S(2)}) collective-permute-start(bf16[16,16,512]{2,1,0:T(8,128)(2,1)S(1)} %get-tuple-element.29), channel_id=1, source_target_pairs={{0,4},{4,0},{8,12},{12,8},{16,20},{20,16},{24,28},{28,24},{1,5},{5... | collective-permute-start | bytes 786440 | tf_op jit(solution)/shard_map/ppermute | solution.py:81
  25.0 1.6 %collective-permute-start.1 = (bf16[16,16,512]{2,1,0:T(8,128)(2,1)S(1)}, bf16[16,16,512]{2,1,0:T(8,128)(2,1)S(1)}, u32[]{:S(2)}, u32[]{:S(2)}) collective-permute-start(bf16[16,16,512]{2,1,0:T(8,128)(2,1)S(1)} %get-tuple-element.30), channel_id=1, source_target_pairs={{0,8},{4,12},{8,0},{12,4},{16,24},{20,28},{24,16},{28,20},{1,9},{5... | collective-permute-start | bytes 786440 | tf_op jit(solution)/shard_map/ppermute | solution.py:81
  26.8 5.2 %collective-permute-done.refs_2_ = bf16[16,16,512]{2,1,0:T(8,128)(2,1)S(1)} collective-permute-done((bf16[16,16,512]{2,1,0:T(8,128)(2,1)S(1)}, bf16[16,16,512]{2,1,0:T(8,128)(2,1)S(1)}, u32[]{:S(2)}, u32[]{:S(2)}) %collective-permute-start) | collective-permute-done | bytes 262176 | tf_op jit(solution)/shard_map/ppermute | solution.py:81
  31.9 2.2 %collective-permute-done.1.refs_3_ = bf16[16,16,512]{2,1,0:T(8,128)(2,1)S(1)} collective-permute-done((bf16[16,16,512]{2,1,0:T(8,128)(2,1)S(1)}, bf16[16,16,512]{2,1,0:T(8,128)(2,1)S(1)}, u32[]{:S(2)}, u32[]{:S(2)}) %collective-permute-start.1) | collective-permute-done | bytes 262176 | tf_op jit(solution)/shard_map/ppermute | solution.py:81
  34.1 4.6 %collective-permute-done.2.refs_4_ = bf16[16,16,512]{2,1,0:T(8,128)(2,1)S(1)} collective-permute-done((bf16[16,16,512]{2,1,0:T(8,128)(2,1)S(1)}, bf16[16,16,512]{2,1,0:T(8,128)(2,1)S(1)}, u32[]{:S(2)}, u32[]{:S(2)}) %collective-permute-start.2) | collective-permute-done | bytes 262176 | tf_op jit(solution)/shard_map/ppermute | solution.py:81
  38.8 2.3 %shard_map.89 = (f32[384,512]{1,0:T(8,128)S(1)}, f32[384,512]{1,0:T(8,128)}) custom-call(s32[1]{0:T(128)} %bitcast.2.near_ref, s32[1]{0:T(128)} %bitcast.3.top_ref, s32[1]{0:T(128)} %bitcast.4.cls_ref, f32[1,128]{1,0:T(1,128)S(1)} %bitcast.37, bf16[16,2,4,16,512]{4,3,2,1,0:T(8,128)(2,1)} %bitcast.45, bf16[16,16,512]{2,1,0:T(8,128)(2,1)S(1)} %collective-permute-done.refs_2_, ...), custom_call_target="tpu_custom_call" | custom-call | bytes 9000000 | tf_op jit(solution)/shard_map/pallas_call | solution.py:498
  41.2 1.8 %collective-permute-start.11 = (bf16[12,32,512]{2,1,0:T(8,128)(2,1)S(1)}, bf16[12,32,512]{2,1,0:T(8,128)(2,1)S(1)}, u32[]{:S(2)}, u32[]{:S(2)}) collective-permute-start(bf16[12,32,512]{2,1,0:T(8,128)(2,1)S(1)} %copy-done), channel_id=1, source_target_pairs={{0,2},{1,3},{2,0},{3,1},{4,6},{5,7},{6,4},{7,5},{8,10},{9,11},{10,... | collective-permute-start | bytes 1179656 | tf_op jit(solution)/shard_map/ppermute | solution.py:81
  43.6 9.7 %collective-permute-done.11 = bf16[12,32,512]{2,1,0:T(8,128)(2,1)S(1)} collective-permute-done((bf16[12,32,512]{2,1,0:T(8,128)(2,1)S(1)}, bf16[12,32,512]{2,1,0:T(8,128)(2,1)S(1)}, u32[]{:S(2)}, u32[]{:S(2)}) %collective-permute-start.11) | collective-permute-done | bytes 393248 | tf_op jit(solution)/shard_map/ppermute | solution.py:81
  53.3 1.5 %shard_map.90 = (f32[1,192,512]{2,1,0:T(8,128)S(1)}, s16[1,208,512]{2,1,0:T(8,128)(2,1)S(1)}) custom-call(s32[1]{0:T(128)} %bitcast.1.bit_ref, f32[2,192,512]{2,1,0:T(8,128)S(1)} %bitcast.31, f32[2,192,512]{2,1,0:T(8,128)} %bitcast.11.get_ref), custom_call_target="tpu_custom_call" | custom-call | bytes 5400000 | tf_op jit(solution)/shard_map/pallas_call | solution.py:591
  54.8 1.8 %collective-permute-start.7 = (s16[1,208,512]{2,1,0:T(8,128)(2,1)S(1)}, s16[1,208,512]{2,1,0:T(8,128)(2,1)S(1)}, u32[]{:S(2)}, u32[]{:S(2)}) collective-permute-start(s16[1,208,512]{2,1,0:T(8,128)(2,1)S(1)} %get-tuple-element.43), channel_id=1, source_target_pairs={{0,2},{1,3},{2,0},{3,1},{4,6},{5,7},{6,4},{7,5},{8,10},{9,11},{10,... | collective-permute-start | bytes 638984 | tf_op jit(solution)/shard_map/ppermute | solution.py:81
  57.5 2.8 %collective-permute-start.10 = (s16[208,512]{1,0:T(8,128)(2,1)S(1)}, s16[208,512]{1,0:T(8,128)(2,1)S(1)}, u32[]{:S(2)}, u32[]{:S(2)}) collective-permute-start(s16[208,512]{1,0:T(8,128)(2,1)S(1)} %get-tuple-element.49), channel_id=1, source_target_pairs={{0,16},{4,20},{8,24},{12,28},{16,0},{20,4},{24,8},{28,12},{1,17},{... | collective-permute-start | bytes 638984 | tf_op jit(solution)/shard_map/ppermute | solution.py:81
  60.4 1.1 %table.1 = (bf16[512,512]{1,0:T(8,128)(2,1)S(1)}, bf16[16,32,512]{2,1,0:T(8,128)(2,1)S(1)}) custom-call(bf16[16,128,512]{2,1,0:T(8,128)(2,1)} %image_ref.1), custom_call_target="tpu_custom_call" | custom-call | bytes 7200000 | tf_op jit(solution)/shard_map/table/pallas_call | solution.py:56
  61.5 2.6 %shard_map.93 = (f32[8,128]{1,0:T(8,128)S(1)}, f32[8,128]{1,0:T(8,128)S(1)}) custom-call(bf16[16,32,512]{2,1,0:T(8,128)(2,1)S(1)} %get-tuple-element.50.low_ref, bf16[16,128]{1,0:T(8,128)(2,1)S(1)} %copy-done.1, f32[1,128]{1,0:T(1,128)S(1)} %bitcast.38, bf16[384,512]{1,0:T(8,128)(2,1)S(1)} %bitcast.23, bf16[384,512]{1,0:T(8,128)(2,1)S(1)} %bitcast.25, ...), custom_call_target="tpu_custom_call" | custom-call | bytes 14400000 | tf_op jit(solution)/shard_map/pallas_call | solution.py:248
  64.2 2.6 %shard_map.92 = (f32[8,128]{1,0:T(8,128)S(1)}, f32[8,128]{1,0:T(8,128)S(1)}) custom-call(bf16[16,32,512]{2,1,0:T(8,128)(2,1)S(1)} %get-tuple-element.50.low_ref, bf16[16,128]{1,0:T(8,128)(2,1)S(1)} %copy-done.1, f32[1,128]{1,0:T(1,128)S(1)} %bitcast.39, bf16[384,512]{1,0:T(8,128)(2,1)S(1)} %bitcast.24, bf16[384,512]{1,0:T(8,128)(2,1)S(1)} %bitcast.26, ...), custom_call_target="tpu_custom_call" | custom-call | bytes 14400000 | tf_op jit(solution)/shard_map/pallas_call | solution.py:248
  66.8 4.5 %shard_map.94.refs_2_ = f32[1,16]{1,0:T(1,128)S(1)} custom-call(bf16[16,32,512]{2,1,0:T(8,128)(2,1)S(1)} %get-tuple-element.50.low_ref, bf16[16,128]{1,0:T(8,128)(2,1)S(1)} %copy-done.1, f32[1,128]{1,0:T(1,128)S(1)} %bitcast.40, bf16[384,512]{1,0:T(8,128)(2,1)} %bitcast.46, bf16[384,512]{1,0:T(8,128)(2,1)S(1)} %bitcast.27, ...), custom_call_target="tpu_custom_call" | custom-call | bytes 14400000 | tf_op jit(solution)/shard_map/pallas_call | solution.py:248
  71.4 5.1 %shard_map.95 = f32[1,16]{1,0:T(1,128)} custom-call(bf16[16,32,512]{2,1,0:T(8,128)(2,1)S(1)} %get-tuple-element.50.low_ref, bf16[16,128]{1,0:T(8,128)(2,1)S(1)} %copy-done.1, f32[1,128]{1,0:T(1,128)S(1)} %bitcast.41, bf16[384,512]{1,0:T(8,128)(2,1)} %bitcast.47, bf16[384,512]{1,0:T(8,128)(2,1)S(1)} %bitcast.28, ...), custom_call_target="tpu_custom_call" | custom-call | bytes 14400000 | tf_op jit(solution)/shard_map/pallas_call | solution.py:248
  (33 shorter events, 3.1 us)
Async XLA Ops:
  0.6 18.3 %copy-start.5 = (f32[128]{0:T(128)S(1)}, f32[128]{0:T(128)}, u32[]{:S(2)}) copy-start(f32[128]{0:T(128)} %param.9) | copy-start | bytes 1540
  2.0 9.7 %collective-permute-start.3 = (bf16[17,16,512]{2,1,0:T(8,128)(2,1)S(1)}, bf16[17,16,512]{2,1,0:T(8,128)(2,1)S(1)}, u32[]{:S(2)}, u32[]{:S(2)}) collective-permute-start(bf16[17,16,512]{2,1,0:T(8,128)(2,1)S(1)} %get-tuple-element.33), channel_id=1, source_target_pairs={{0,4},{4,0},{8,12},{12,8},{16,20},{20,16},{24,28},{28,24},{1,5},{5... | collective-permute-start | bytes 835592 | tf_op jit(solution)/shard_map/ppermute | solution.py:81
  5.0 9.5 %collective-permute-start.4 = (bf16[17,16,512]{2,1,0:T(8,128)(2,1)S(1)}, bf16[17,16,512]{2,1,0:T(8,128)(2,1)S(1)}, u32[]{:S(2)}, u32[]{:S(2)}) collective-permute-start(bf16[17,16,512]{2,1,0:T(8,128)(2,1)S(1)} %get-tuple-element.34), channel_id=1, source_target_pairs={{0,8},{4,12},{8,0},{12,4},{16,24},{20,28},{24,16},{28,20},{1,9},{5... | collective-permute-start | bytes 835592 | tf_op jit(solution)/shard_map/ppermute | solution.py:81
  6.6 12.3 %collective-permute-start.5 = (bf16[17,16,512]{2,1,0:T(8,128)(2,1)S(1)}, bf16[17,16,512]{2,1,0:T(8,128)(2,1)S(1)}, u32[]{:S(2)}, u32[]{:S(2)}) collective-permute-start(bf16[17,16,512]{2,1,0:T(8,128)(2,1)S(1)} %get-tuple-element.35), channel_id=1, source_target_pairs={{0,12},{4,8},{8,4},{12,0},{16,28},{20,24},{24,20},{28,16},{1,13},{... | collective-permute-start | bytes 835592 | tf_op jit(solution)/shard_map/ppermute | solution.py:81
  21.8 17.0 %copy-start.2 = (f32[64,256]{1,0:T(8,128)S(1)}, f32[64,256]{1,0:T(8,128)}, u32[]{:S(2)}) copy-start(f32[64,256]{1,0:T(8,128)} %get-tuple-element.38.refs_7_) | copy-start | bytes 196612
  21.8 17.0 %copy-start.3 = (f32[64,256]{1,0:T(8,128)S(1)}, f32[64,256]{1,0:T(8,128)}, u32[]{:S(2)}) copy-start(f32[64,256]{1,0:T(8,128)} %get-tuple-element.39.refs_8_) | copy-start | bytes 196612
  21.8 17.0 %copy-start.4 = (bf16[64,256]{1,0:T(8,128)(2,1)S(1)}, bf16[64,256]{1,0:T(8,128)(2,1)}, u32[]{:S(2)}) copy-start(bf16[64,256]{1,0:T(8,128)(2,1)} %get-tuple-element.37.refs_6_) | copy-start | bytes 98308
  21.8 17.0 %copy-start.6 = (s32[8,128]{1,0:T(8,128)S(1)}, s32[8,128]{1,0:T(8,128)}, u32[]{:S(2)}) copy-start(s32[8,128]{1,0:T(8,128)} %get-tuple-element.36.refs_5_) | copy-start | bytes 12292
  21.8 19.4 %copy-start = (bf16[12,32,512]{2,1,0:T(8,128)(2,1)S(1)}, bf16[12,32,512]{2,1,0:T(8,128)(2,1)}, u32[]{:S(2)}) copy-start(bf16[12,32,512]{2,1,0:T(8,128)(2,1)} %param.10) | copy-start | bytes 1179652
  21.8 21.1 %collective-permute-start.8 = (f32[416,512]{1,0:T(8,128)}, f32[416,512]{1,0:T(8,128)S(1)}, u32[]{:S(2)}, u32[]{:S(2)}) collective-permute-start(f32[416,512]{1,0:T(8,128)} %get-tuple-element.45), channel_id=1, source_target_pairs={{0,1},{1,0},{2,3},{3,2},{4,5},{5,4},{6,7},{7,6},{8,9},{9,8},{10,11... | collective-permute-start | bytes 2555912 | tf_op jit(solution)/shard_map/ppermute | solution.py:81
  23.2 8.7 %collective-permute-start = (bf16[16,16,512]{2,1,0:T(8,128)(2,1)S(1)}, bf16[16,16,512]{2,1,0:T(8,128)(2,1)S(1)}, u32[]{:S(2)}, u32[]{:S(2)}) collective-permute-start(bf16[16,16,512]{2,1,0:T(8,128)(2,1)S(1)} %get-tuple-element.29), channel_id=1, source_target_pairs={{0,4},{4,0},{8,12},{12,8},{16,20},{20,16},{24,28},{28,24},{1,5},{5... | collective-permute-start | bytes 786440 | tf_op jit(solution)/shard_map/ppermute | solution.py:81
  25.0 9.2 %collective-permute-start.1 = (bf16[16,16,512]{2,1,0:T(8,128)(2,1)S(1)}, bf16[16,16,512]{2,1,0:T(8,128)(2,1)S(1)}, u32[]{:S(2)}, u32[]{:S(2)}) collective-permute-start(bf16[16,16,512]{2,1,0:T(8,128)(2,1)S(1)} %get-tuple-element.30), channel_id=1, source_target_pairs={{0,8},{4,12},{8,0},{12,4},{16,24},{20,28},{24,16},{28,20},{1,9},{5... | collective-permute-start | bytes 786440 | tf_op jit(solution)/shard_map/ppermute | solution.py:81
  26.5 12.2 %collective-permute-start.2 = (bf16[16,16,512]{2,1,0:T(8,128)(2,1)S(1)}, bf16[16,16,512]{2,1,0:T(8,128)(2,1)S(1)}, u32[]{:S(2)}, u32[]{:S(2)}) collective-permute-start(bf16[16,16,512]{2,1,0:T(8,128)(2,1)S(1)} %get-tuple-element.31), channel_id=1, source_target_pairs={{0,12},{4,8},{8,4},{12,0},{16,28},{20,24},{24,20},{28,16},{1,13},{... | collective-permute-start | bytes 786440 | tf_op jit(solution)/shard_map/ppermute | solution.py:81
  41.1 12.2 %collective-permute-start.6 = (f32[384,512]{1,0:T(8,128)}, f32[384,512]{1,0:T(8,128)}, u32[]{:S(2)}, u32[]{:S(2)}) collective-permute-start(f32[384,512]{1,0:T(8,128)} %get-tuple-element.41), channel_id=1, source_target_pairs={{0,1},{1,0},{2,3},{3,2},{4,5},{5,4},{6,7},{7,6},{8,9},{9,8},{10,11... | collective-permute-start | bytes 2359304 | tf_op jit(solution)/shard_map/ppermute | solution.py:81
  41.2 12.1 %collective-permute-start.11 = (bf16[12,32,512]{2,1,0:T(8,128)(2,1)S(1)}, bf16[12,32,512]{2,1,0:T(8,128)(2,1)S(1)}, u32[]{:S(2)}, u32[]{:S(2)}) collective-permute-start(bf16[12,32,512]{2,1,0:T(8,128)(2,1)S(1)} %copy-done), channel_id=1, source_target_pairs={{0,2},{1,3},{2,0},{3,1},{4,6},{5,7},{6,4},{7,5},{8,10},{9,11},{10,... | collective-permute-start | bytes 1179656 | tf_op jit(solution)/shard_map/ppermute | solution.py:81
  43.2 14.1 %collective-permute-start.9 = (s16[1,208,512]{2,1,0:T(8,128)(2,1)S(1)}, s16[1,208,512]{2,1,0:T(8,128)(2,1)S(1)}, u32[]{:S(2)}, u32[]{:S(2)}) collective-permute-start(s16[1,208,512]{2,1,0:T(8,128)(2,1)S(1)} %get-tuple-element.47), channel_id=1, source_target_pairs={{0,2},{1,3},{2,0},{3,1},{4,6},{5,7},{6,4},{7,5},{8,10},{9,11},{10,... | collective-permute-start | bytes 638984 | tf_op jit(solution)/shard_map/ppermute | solution.py:81
  43.6 17.9 %collective-permute-start.13 = (bf16[12,32,512]{2,1,0:T(8,128)(2,1)S(1)}, bf16[12,32,512]{2,1,0:T(8,128)(2,1)S(1)}, u32[]{:S(2)}, u32[]{:S(2)}) collective-permute-start(bf16[12,32,512]{2,1,0:T(8,128)(2,1)S(1)} %copy-done), channel_id=1, source_target_pairs={{0,1},{1,0},{2,3},{3,2},{4,5},{5,4},{6,7},{7,6},{8,9},{9,8},{10,11... | collective-permute-start | bytes 1179656 | tf_op jit(solution)/shard_map/ppermute | solution.py:81
  53.2 8.3 %copy-start.7 = (bf16[12,32,512]{2,1,0:T(8,128)(2,1)}, bf16[12,32,512]{2,1,0:T(8,128)(2,1)S(1)}, u32[]{:S(2)}) copy-start(bf16[12,32,512]{2,1,0:T(8,128)(2,1)S(1)} %collective-permute-done.11) | copy-start | bytes 1179652
  53.2 13.6 %collective-permute-start.12 = (bf16[12,32,512]{2,1,0:T(8,128)(2,1)S(1)}, bf16[12,32,512]{2,1,0:T(8,128)(2,1)S(1)}, u32[]{:S(2)}, u32[]{:S(2)}) collective-permute-start(bf16[12,32,512]{2,1,0:T(8,128)(2,1)S(1)} %collective-permute-done.11), channel_id=1, source_target_pairs={{0,1},{1,0},{2,3},{3,2},{4,5},{5,4},{6,7},{7,6},{8,9},{9,8},{10,11... | collective-permute-start | bytes 1179656 | tf_op jit(solution)/shard_map/ppermute | solution.py:81
  53.2 8.3 %copy-start.1 = (bf16[16,128]{1,0:T(8,128)(2,1)S(1)}, bf16[16,128]{1,0:T(8,128)(2,1)}, u32[]{:S(2)}) copy-start(bf16[16,128]{1,0:T(8,128)(2,1)} %ctf_ref.7) | copy-start | bytes 12292
  54.8 21.7 %collective-permute-start.7 = (s16[1,208,512]{2,1,0:T(8,128)(2,1)S(1)}, s16[1,208,512]{2,1,0:T(8,128)(2,1)S(1)}, u32[]{:S(2)}, u32[]{:S(2)}) collective-permute-start(s16[1,208,512]{2,1,0:T(8,128)(2,1)S(1)} %get-tuple-element.43), channel_id=1, source_target_pairs={{0,2},{1,3},{2,0},{3,1},{4,6},{5,7},{6,4},{7,5},{8,10},{9,11},{10,... | collective-permute-start | bytes 638984 | tf_op jit(solution)/shard_map/ppermute | solution.py:81
  57.5 18.9 %collective-permute-start.10 = (s16[208,512]{1,0:T(8,128)(2,1)S(1)}, s16[208,512]{1,0:T(8,128)(2,1)S(1)}, u32[]{:S(2)}, u32[]{:S(2)}) collective-permute-start(s16[208,512]{1,0:T(8,128)(2,1)S(1)} %get-tuple-element.49), channel_id=1, source_target_pairs={{0,16},{4,20},{8,24},{12,28},{16,0},{20,4},{24,8},{28,12},{1,17},{... | collective-permute-start | bytes 638984 | tf_op jit(solution)/shard_map/ppermute | solution.py:81
